TPU v7x, 32 devices: a whole 2x2x4 slice. The times are simulated.
32 devices in a mesh: groups: 2 (over x), seq: 8 (over z, y), head: 2 (over core).
Axes of the slice: x: 2, y: 2, z: 4, core: 2. Of those that a mesh axis runs over, the one named last changes fastest.
Arguments:
- queries: float32 [4096, 2048], P(('groups', 'seq'), 'head'), parts along dimension 0, may hold values from -6 to 6
- keys: float32 [4096, 2048], P(('groups', 'seq'), 'head'), parts along dimension 0, may hold values from -0.01171875 to 0.01171875
- values: float32 [4096, 2048], P(('groups', 'seq'), 'head'), parts along dimension 0, may hold values from -6 to 6
- level_weight: float32 [16, 6, 4096], P('head', None, ('groups', 'seq')), parts along dimension 2, may hold values from 0.1 to 1
- prefix_weight: float32 [16, 8, 4096], P('head', None, ('groups', 'seq')), parts along dimension 2, may hold values from 0.1 to 1
- prefix_state: float32 [16, 2048, 128], P('head', 'groups'), parts along dimension 1, may hold values from -0.5 to 0.5
Outputs:
- attended: float32 [4096, 2048], P(('groups', 'seq'), 'head'), parts along dimension 0
There are 2 independent parts, one for each index of `groups`. A program takes and returns all parts, laid end to end along the dimension named above; each array names one. Nothing has to cross between parts.
All inputs are finite; a program needn't handle non-finite values.
Results may differ from a plain program's by a relative error of at most 0.00005.
Values sent between devices are 32-bit elements; how exact they have to be, the bound alone decides.
No kernel may reach another device: no remote copies, remote signals or barrier semaphores. Data moves between devices by JAX's collectives and lax.ppermute only.
A program may use at most 128 MiB of HBM per device.

v0:
```python
import jax
import jax.numpy as jnp
from jax import lax
from jax.sharding import PartitionSpec as P

DH = 128
LEVELS = 6
BUCKETS = 8


def swapped(array, axis, stride):
    return lax.ppermute(array, axis, [(i, i ^ 1 << stride) for i in range(lax.axis_size(axis))])


def shards(queries, keys, values, level_weight, prefix_weight, prefix_state):
    highest_level = lax.Precision.HIGHEST
    tok_rows = queries.shape[0]
    head_count = queries.shape[1] // DH
    query_heads = queries.reshape(tok_rows, head_count, DH)
    key_head_count = keys.reshape(tok_rows, head_count, DH)
    value_heads = values.reshape(tok_rows, head_count, DH)
    query_key_scores = jnp.einsum(
        "thd,shd->hts", query_heads, key_head_count, precision=highest_level
    )
    row_index = lax.broadcasted_iota(jnp.int32, (tok_rows, tok_rows), 0)
    col_index = lax.broadcasted_iota(jnp.int32, (tok_rows, tok_rows), 1)
    causal = col_index <= row_index
    query_key_scores = jnp.where(causal[None], query_key_scores, 0.0) * level_weight[:, 0, :, None]
    local_out = jnp.einsum("hts,she->the", query_key_scores, value_heads, precision=highest_level)
    block_memory_state = jnp.einsum(
        "thd,the->hde", key_head_count, value_heads, precision=highest_level
    )
    position = lax.axis_index("seq")
    running = block_memory_state
    collected = []
    for level_bit in range(LEVELS - 1):
        if 1 << level_bit < lax.axis_size("seq"):
            partner = swapped(running, "seq", level_bit)
            upper_half = jnp.right_shift(position, level_bit) & 1 == 1
            collected.append(jnp.where(upper_half, partner, 0.0))
            running = running + partner
        else:
            collected.append(jnp.zeros_like(block_memory_state))
    per_level_states = jnp.stack(collected)
    scaled = jnp.einsum("thd,hlt->hltd", query_heads, level_weight[:, 1:, :])
    level_out = jnp.einsum("hltd,lhde->the", scaled, per_level_states, precision=highest_level)
    weighted = jnp.einsum("thd,hbt->htbd", query_heads, prefix_weight).reshape(
        head_count, tok_rows, BUCKETS * DH
    )
    prefix_out = jnp.einsum("htr,hre->the", weighted, prefix_state, precision=highest_level)
    combined = local_out + level_out + prefix_out
    return combined.reshape(tok_rows, head_count * DH)


def solution(mesh):
    return jax.shard_map(
        shards,
        mesh=mesh,
        in_specs=(
            P(("groups", "seq"), "head"),
            P(("groups", "seq"), "head"),
            P(("groups", "seq"), "head"),
            P("head", None, ("groups", "seq")),
            P("head", None, ("groups", "seq")),
            P("head", "groups", None),
        ),
        out_specs=P(("groups", "seq"), "head"),
        check_vma=False,
    )
```

profile of v0, /device:TPU:0, one launch (start us, length us, event | category | flops | bytes accessed | tf_op | source)
XLA Modules:
  0.0 82.6 jit_solution(12338821892422495612)
XLA Ops:
  0.0 0.0 copy-start
  0.0 1.7 %copy.22 = f32[256,1024]{0,1:T(8,128)S(1)} copy(f32[256,1024]{1,0:T(8,128)} %param.7) | data formatting | bytes 2097152 | tf_op jit(solution)/shard_map/reshape | solution.py:20
  1.7 0.0 copy-done
  1.7 2.0 %fusion.30 = f32[8,128,128]{2,1,0:T(8,128)} fusion(f32[256,8,128]{0,2,1:T(8,128)S(1)} %bitcast.62, f32[256,1024]{1,0:T(8,128)S(1)} %copy-done), kind=kOutput, calls=%fused_computation.22 | convolution fusion | flops 402653184 | bytes 2621440 | tf_op jit(solution)/shard_map/thd,the->hde/dot_general | solution.py:30
  3.7 3.0 %collective-permute-start = (f32[8,128,128]{2,1,0:T(8,128)}, f32[8,128,128]{2,1,0:T(8,128)}, u32[]{:S(2)}, u32[]{:S(2)}) collective-permute-start(f32[8,128,128]{2,1,0:T(8,128)} %fusion.30), channel_id=1, source_target_pairs={{0,2},{2,0},{4,6},{6,4},{8,10},{10,8},{12,14},{14,12},{1,3},{3,1},... | collective-permute-start | bytes 1572872 | tf_op jit(solution)/shard_map/ppermute | solution.py:12
  6.7 0.0 copy-done.6
  6.7 1.3 %copy.15 = f32[8,256,8]{2,1,0:T(8,128)} copy(f32[8,256,8]{1,2,0:T(8,128)S(1)} %bitcast.67) | data formatting | bytes 131072 | tf_op jit(solution)/shard_map/shard_map
  8.0 0.0 copy-done.3
  8.0 0.2 copy.25
  8.2 0.2 copy.14
  8.4 0.8 copy-done.2
  9.2 5.1 %broadcast_multiply_fusion = f32[8,256,8,128]{3,2,1,0:T(8,128)} fusion(f32[8,256,128]{2,1,0:T(8,128)S(1)} %copy.14, f32[8,256,8]{2,1,0:T(8,128)S(1)} %copy-done.2), kind=kLoop, calls=%fused_computation.3 | loop fusion | flops 2097152 | bytes 9502720 | tf_op jit(solution)/shard_map/thd,hbt->htbd/dot_general | solution.py:47
  14.3 4.6 %collective-permute-done = f32[8,128,128]{2,1,0:T(8,128)} collective-permute-done((f32[8,128,128]{2,1,0:T(8,128)}, f32[8,128,128]{2,1,0:T(8,128)}, u32[]{:S(2)}, u32[]{:S(2)}) %collective-permute-start) | collective-permute-done | bytes 524320 | tf_op jit(solution)/shard_map/ppermute | solution.py:12
  18.9 2.3 %select_bitcast_fusion.2 = (f32[1,8,128,128]{3,2,1,0:T(8,128)}, f32[8,128,128]{2,1,0:T(8,128)}) fusion(f32[8,128,128]{2,1,0:T(8,128)} %collective-permute-done, pred[]{:T(512)S(6)} %eq.9, f32[8,128,128]{2,1,0:T(8,128)} %fusion.30), kind=kLoop, calls=%fused_computation.34 | loop fusion | flops 262144 | bytes 2097153 | tf_op jit(solution)/shard_map/stack | solution.py:44
  21.2 1.8 %collective-permute-start.1 = (f32[8,128,128]{2,1,0:T(8,128)}, f32[8,128,128]{2,1,0:T(8,128)}, u32[]{:S(2)}, u32[]{:S(2)}) collective-permute-start(f32[8,128,128]{2,1,0:T(8,128)} %get-tuple-element.6), channel_id=1, source_target_pairs={{0,4},{2,6},{4,0},{6,2},{8,12},{10,14},{12,8},{14,10},{1,5},{3,7},... | collective-permute-start | bytes 1572872 | tf_op jit(solution)/shard_map/ppermute | solution.py:12
  23.0 0.0 copy-done.7
  23.0 9.3 %reshape.29 = f32[8,256,1024]{2,1,0:T(8,128)} reshape(f32[8,256,8,128]{3,2,1,0:T(8,128)} %broadcast_multiply_fusion) | data formatting | bytes 16777216 | tf_op jit(solution)/shard_map/reshape | solution.py:47
  32.3 0.1 pad.3.clone
  32.4 3.1 %fusion.32 = f32[8,256,256]{2,1,0:T(8,128)S(1)} fusion(f32[256,8,128]{0,2,1:T(8,128)S(1)} %bitcast.63, f32[256,1024]{1,0:T(8,128)} %param.6), kind=kOutput, calls=%fused_computation.24 | convolution fusion | flops 805306368 | bytes 4194304 | tf_op jit(solution)/shard_map/thd,shd->hts/dot_general | solution.py:22
  35.5 0.0 collective-permute-done.1
  35.5 2.1 %select_bitcast_fusion.1 = (f32[1,8,128,128]{3,2,1,0:T(8,128)S(1)}, f32[8,128,128]{2,1,0:T(8,128)}) fusion(f32[8,128,128]{2,1,0:T(8,128)} %collective-permute-done.1, pred[]{:T(512)S(6)} %eq.10, f32[8,128,128]{2,1,0:T(8,128)} %get-tuple-element.6), kind=kLoop, calls=%fused_computation.33 | loop fusion | flops 262144 | bytes 2097153 | tf_op jit(solution)/shard_map/stack | solution.py:44
  37.6 2.6 %collective-permute-start.2 = (f32[8,128,128]{2,1,0:T(8,128)}, f32[8,128,128]{2,1,0:T(8,128)}, u32[]{:S(2)}, u32[]{:S(2)}) collective-permute-start(f32[8,128,128]{2,1,0:T(8,128)} %get-tuple-element.8), channel_id=1, source_target_pairs={{0,8},{2,10},{4,12},{6,14},{8,0},{10,2},{12,4},{14,6},{1,9},{3,11}... | collective-permute-start | bytes 1572872 | tf_op jit(solution)/shard_map/ppermute | solution.py:12
  40.2 3.7 %fusion.14 = f32[256,8,128]{0,2,1:T(8,128)} fusion(f32[8,256,256]{2,1,0:T(8,128)S(1)} %fusion.32, f32[8,256]{1,0:T(8,128)S(1)} %slice_bitcast_fusion.1, pred[256,256]{1,0:T(8,128)(4,1)S(1)} %iota_compare_fusion, f32[256,1024]{1,0:T(8,128)S(1)} %copy-done), kind=kOutput, calls=%fused_computation.15 | convolution fusion | flops 806354944 | bytes 4268032 | tf_op jit(solution)/shard_map/hts,she->the/dot_general | solution.py:29
  43.9 0.0 copy-done.4
  43.9 1.0 %copy.10 = f32[1,8,128,128]{2,3,0,1:T(8,128)} copy(f32[1,8,128,128]{3,2,1,0:T(8,128)S(1)} %copy-done.4) | data formatting | bytes 1048576 | tf_op jit(solution)/shard_map/stack | solution.py:44
  44.9 1.0 %copy.11 = f32[1,8,128,128]{2,3,0,1:T(8,128)} copy(f32[1,8,128,128]{3,2,1,0:T(8,128)S(1)} %get-tuple-element.7) | data formatting | bytes 1048576 | tf_op jit(solution)/shard_map/stack | solution.py:44
  45.9 16.6 %collective-permute-done.2 = f32[8,128,128]{2,1,0:T(8,128)} collective-permute-done((f32[8,128,128]{2,1,0:T(8,128)}, f32[8,128,128]{2,1,0:T(8,128)}, u32[]{:S(2)}, u32[]{:S(2)}) %collective-permute-start.2) | collective-permute-done | bytes 524320 | tf_op jit(solution)/shard_map/ppermute | solution.py:12
  62.6 1.0 %copy.12 = f32[1,8,128,128]{2,3,0,1:T(8,128)} copy(f32[1,8,128,128]{3,2,1,0:T(8,128)S(1)} %select_bitcast_fusion) | data formatting | bytes 1048576 | tf_op jit(solution)/shard_map/stack | solution.py:44
  63.6 7.2 %fusion.23 = f32[256,8,128]{0,2,1:T(8,128)S(1)} fusion(f32[256,8,128]{0,2,1:T(8,128)} %fusion.14, f32[8,256,128]{2,1,0:T(8,128)S(1)} %copy.14, f32[8,256,5]{1,2,0:T(8,128)S(1)} %copy.13, f32[1,8,128,128]{2,3,0,1:T(8,128)} %copy.12, f32[1,8,128,128]{2,3,0,1:T(8,128)} %copy.11, f32[1,8,128,128]{2,3,0,1:T(8,128)S(1)} %copy-done.5, f32[5]{0:T(128)S(1)} %pad.3.clone), kind=kOutput, calls=%fused_computation.19 | convolution fusion | flops 2016804864 | bytes 4759572 | tf_op jit(solution)/shard_map/hltd,lhde->the/dot_general | solution.py:46
  70.8 0.0 copy-done.1
  70.8 10.5 %fusion.22 = f32[256,8,128]{0,2,1:T(8,128)S(1)} fusion(f32[256,8,128]{0,2,1:T(8,128)S(1)} %fusion.23, f32[8,256,1024]{2,1,0:T(8,128)} %reshape.29, f32[8,1024,128]{2,1,0:T(8,128)S(1)} %copy-done.1), kind=kOutput, calls=%fused_computation.18 | convolution fusion | flops 3221487616 | bytes 14680064 | tf_op jit(solution)/shard_map/htr,hre->the/dot_general | solution.py:50
  81.3 1.3 %copy.18 = f32[256,1024]{1,0:T(8,128)} copy(f32[256,1024]{0,1:T(8,128)S(1)} %bitcast.64) | data formatting | bytes 2097152 | tf_op jit(solution)/shard_map/reshape | solution.py:52
  (14 shorter events, 0.1 us)
Async XLA Ops:
  0.0 1.7 %copy-start = (f32[256,1024]{1,0:T(8,128)S(1)}, f32[256,1024]{1,0:T(8,128)}, u32[]{:S(2)}) copy-start(f32[256,1024]{1,0:T(8,128)} %param.8) | copy-start | bytes 3145732
  0.0 6.7 %copy-start.6 = (f32[8,8,256]{2,1,0:T(8,128)S(1)}, f32[8,8,256]{2,1,0:T(8,128)}, u32[]{:S(2)}) copy-start(f32[8,8,256]{2,1,0:T(8,128)} %param.10) | copy-start | bytes 196612
  0.0 8.0 %copy-start.3 = (f32[256,1024]{1,0:T(8,128)S(1)}, f32[256,1024]{1,0:T(8,128)}, u32[]{:S(2)}) copy-start(f32[256,1024]{1,0:T(8,128)} %param.6) | copy-start | bytes 3145732
  3.7 15.2 %collective-permute-start = (f32[8,128,128]{2,1,0:T(8,128)}, f32[8,128,128]{2,1,0:T(8,128)}, u32[]{:S(2)}, u32[]{:S(2)}) collective-permute-start(f32[8,128,128]{2,1,0:T(8,128)} %fusion.30), channel_id=1, source_target_pairs={{0,2},{2,0},{4,6},{6,4},{8,10},{10,8},{12,14},{14,12},{1,3},{3,1},... | collective-permute-start | bytes 1572872 | tf_op jit(solution)/shard_map/ppermute | solution.py:12
  8.0 1.2 %copy-start.2 = (f32[8,256,8]{2,1,0:T(8,128)S(1)}, f32[8,256,8]{2,1,0:T(8,128)}, u32[]{:S(2)}) copy-start(f32[8,256,8]{2,1,0:T(8,128)} %copy.15) | copy-start | bytes 196612
  9.2 13.8 %copy-start.7 = (f32[8,6,256]{2,0,1:T(8,128)S(1)}, f32[8,6,256]{2,0,1:T(8,128)}, u32[]{:S(2)}) copy-start(f32[8,6,256]{2,0,1:T(8,128)} %param.9) | copy-start | bytes 147460
  21.2 14.3 %collective-permute-start.1 = (f32[8,128,128]{2,1,0:T(8,128)}, f32[8,128,128]{2,1,0:T(8,128)}, u32[]{:S(2)}, u32[]{:S(2)}) collective-permute-start(f32[8,128,128]{2,1,0:T(8,128)} %get-tuple-element.6), channel_id=1, source_target_pairs={{0,4},{2,6},{4,0},{6,2},{8,12},{10,14},{12,8},{14,10},{1,5},{3,7},... | collective-permute-start | bytes 1572872 | tf_op jit(solution)/shard_map/ppermute | solution.py:12
  37.6 6.3 %copy-start.4 = (f32[1,8,128,128]{3,2,1,0:T(8,128)S(1)}, f32[1,8,128,128]{3,2,1,0:T(8,128)}, u32[]{:S(2)}) copy-start(f32[1,8,128,128]{3,2,1,0:T(8,128)} %get-tuple-element.5) | copy-start | bytes 1572868
  37.6 24.9 %collective-permute-start.2 = (f32[8,128,128]{2,1,0:T(8,128)}, f32[8,128,128]{2,1,0:T(8,128)}, u32[]{:S(2)}, u32[]{:S(2)}) collective-permute-start(f32[8,128,128]{2,1,0:T(8,128)} %get-tuple-element.8), channel_id=1, source_target_pairs={{0,8},{2,10},{4,12},{6,14},{8,0},{10,2},{12,4},{14,6},{1,9},{3,11}... | collective-permute-start | bytes 1572872 | tf_op jit(solution)/shard_map/ppermute | solution.py:12
  44.9 18.7 %copy-start.5 = (f32[1,8,128,128]{2,3,0,1:T(8,128)S(1)}, f32[1,8,128,128]{2,3,0,1:T(8,128)}, u32[]{:S(2)}) copy-start(f32[1,8,128,128]{2,3,0,1:T(8,128)} %copy.10) | copy-start | bytes 1572868
  63.6 7.2 %copy-start.1 = (f32[8,1024,128]{2,1,0:T(8,128)S(1)}, f32[8,1024,128]{2,1,0:T(8,128)}, u32[]{:S(2)}) copy-start(f32[8,1024,128]{2,1,0:T(8,128)} %param.11) | copy-start | bytes 12582916
where the time goes:
time: 83 us; the launch traced here: 82.6 us
  matrix products  26.4 us (32%)
  waiting for transfers between devices  21.2 us (26%)
  local copies, waits for them, and re-layouts  18 us (22%)
  other arithmetic  9.53 us (11%)
  starting transfers between devices  7.39 us (9%)
    ppermute x3, waiting for transfers between devices, swapped(): lax.ppermute(array, axis, [(i, i ^ 1 << stride) for i in range(lax.axis_s...  21.2 us
    dot_general x1, matrix products, shards(): jnp.einsum('htr,hre->the', weighted, prefix_state, precision=highest_level)  10.5 us
    reshape x1, local copies, waits for them, and re-layouts, shards(): jnp.einsum('thd,hbt->htbd', query_heads, prefix_weight)  9.27 us
    ppermute x3, starting transfers between devices, swapped(): lax.ppermute(array, axis, [(i, i ^ 1 << stride) for i in range(lax.axis_s...  7.39 us
    dot_general x1, matrix products, shards(): jnp.einsum('hltd,lhde->the', scaled, per_level_states, precision=highest_...  7.18 us
    dot_general x1, other arithmetic, shards(): jnp.einsum('thd,hbt->htbd', query_heads, prefix_weight)  5.08 us
    another operation x3, other arithmetic, shards(): per_level_states = jnp.stack(collected)  4.42 us
    dot_general x1, matrix products, shards(): jnp.einsum('hts,she->the', query_key_scores, value_heads, precision=highe...  3.69 us
  transfers between devices with their start and end apart: 3, of which 2 were waited for; matrix products, arithmetic and copies ran while one was open for 30% of the time, Pallas kernels for 0%

commit v1 on v0

v1 whole, which is shorter than its diff:
```python
import functools

import jax
import jax.numpy as jnp
from jax import lax
from jax.experimental import pallas as pl
from jax.experimental.pallas import tpu as pltpu
from jax.sharding import PartitionSpec as P

DH = 128
BF16 = jnp.bfloat16
F32 = jnp.float32
VMEM_LIMIT = 40 * 1024 * 1024


def split(x):
    high = x.astype(BF16)
    low = (x - high.astype(F32)).astype(BF16)
    return high, low


def beside(x):
    return jnp.concatenate(split(x), axis=1)


def fold_columns(x):
    half = x.shape[1] // 2
    return x[:, :half] + x[:, half:]


def outer_state(k, v):
    full = lax.dot_general(
        beside(k), beside(v), (((0,), (0,)), ((), ())), preferred_element_type=F32
    )
    full = fold_columns(full)
    return full[:DH] + full[DH:]


def through_state(scaled, state):
    wide = beside(state)
    return jnp.dot(
        beside(scaled), jnp.concatenate([wide, wide], axis=0), preferred_element_type=F32
    )


def states_kernel(flip, chunks, k_hbm, v_hbm, *refs):
    outs = refs[:chunks]
    k_buf, v_buf, sems = refs[chunks:]
    width = k_buf.shape[2]
    odd = lax.rem(lax.axis_index("seq"), 2)
    half = odd if flip else 1 - odd
    copies = []
    for c in range(chunks):
        columns = pl.ds(pl.multiple_of((half * chunks + c) * width, DH), width)
        pair = (
            pltpu.make_async_copy(k_hbm.at[:, columns], k_buf.at[c], sems.at[0, c]),
            pltpu.make_async_copy(v_hbm.at[:, columns], v_buf.at[c], sems.at[1, c]),
        )
        for copy in pair:
            copy.start()
        copies.append(pair)
    for c in range(chunks):
        for copy in copies[c]:
            copy.wait()
        for j in range(width // DH):
            at = slice(j * DH, (j + 1) * DH)
            outs[c][j] = outer_state(k_buf[c, :, at], v_buf[c, :, at])


def block_states(keys, values, flip, chunks):
    rows, columns = keys.shape
    width = columns // (2 * chunks)
    shape = jax.ShapeDtypeStruct((width // DH, DH, DH), F32)
    return pl.pallas_call(
        functools.partial(states_kernel, flip, chunks),
        out_shape=[shape] * chunks,
        in_specs=[pl.BlockSpec(memory_space=pl.ANY)] * 2,
        out_specs=[pl.BlockSpec(memory_space=pltpu.VMEM)] * chunks,
        scratch_shapes=[
            pltpu.VMEM((chunks, rows, width), F32),
            pltpu.VMEM((chunks, rows, width), F32),
            pltpu.SemaphoreType.DMA((2, chunks)),
        ],
        compiler_params=pltpu.CompilerParams(vmem_limit_bytes=VMEM_LIMIT),
        cost_estimate=pl.CostEstimate(
            flops=8 * rows * width * chunks * DH,
            bytes_accessed=8 * rows * width * chunks,
            transcendentals=0,
        ),
        name="states_flip" if flip else "states_own",
    )(keys, values)


def base_kernel(q_ref, k_ref, v_ref, level_ref, bucket_ref, prefix_ref, out_ref):
    q, k, v = q_ref[...], k_ref[...], v_ref[...]
    rows = q.shape[0]
    buckets = bucket_ref.shape[1]
    k_high, k_low = split(k)
    q_wide = beside(q)
    nt = (((1,), (1,)), ((), ()))
    scores = lax.dot_general(
        q_wide, jnp.concatenate([k_high, k_high], axis=1), nt, preferred_element_type=F32
    ) + lax.dot_general(
        q_wide, jnp.concatenate([k_low, k_low], axis=1), nt, preferred_element_type=F32
    )
    row = lax.broadcasted_iota(jnp.int32, (rows, rows), 0)
    column = lax.broadcasted_iota(jnp.int32, (rows, rows), 1)
    level = jnp.transpose(level_ref[0])
    bucket = jnp.transpose(bucket_ref[0])
    scores = jnp.where(column <= row, scores, 0.0) * level[:, 0:1]
    scores_high, scores_low = split(scores)
    v_wide = beside(v)
    total = jnp.dot(scores_high, v_wide, preferred_element_type=F32)
    total += jnp.dot(scores_low, v_wide, preferred_element_type=F32)
    for b in range(buckets):
        total += through_state(
            q * bucket[:, b : b + 1], prefix_ref[0, b * DH : (b + 1) * DH, :]
        )
    out_ref[...] = fold_columns(total)


def base_part(queries, keys, values, level_weight, prefix_weight, prefix_state):
    rows, columns = queries.shape
    heads = columns // DH
    by_head = lambda shape: pl.BlockSpec((1, *shape[1:]), lambda h: (h, 0, 0))
    column_block = pl.BlockSpec((rows, DH), lambda h: (0, h))
    return pl.pallas_call(
        base_kernel,
        out_shape=jax.ShapeDtypeStruct((rows, columns), F32),
        grid=(heads,),
        in_specs=[
            column_block,
            column_block,
            column_block,
            by_head(level_weight.shape),
            by_head(prefix_weight.shape),
            by_head(prefix_state.shape),
        ],
        out_specs=column_block,
        compiler_params=pltpu.CompilerParams(
            dimension_semantics=("arbitrary",), vmem_limit_bytes=VMEM_LIMIT
        ),
        cost_estimate=pl.CostEstimate(
            flops=2 * heads * rows * rows * 256 * 12,
            bytes_accessed=16 * rows * columns + 4 * prefix_state.size,
            transcendentals=0,
        ),
        name="base_part",
    )(queries, keys, values, level_weight, prefix_weight, prefix_state)


def levels_kernel(first, count, side_ref, q_ref, level_ref, *refs):
    state_refs = refs[:count]
    in_ref, out_ref = refs[count:]
    q = q_ref[...]
    level = jnp.transpose(level_ref[0])
    total = None
    for i in range(count):
        take = side_ref[1 + first + i].astype(F32)
        weight = level[:, 1 + first + i : 2 + first + i] * take
        term = through_state(q * weight, state_refs[i][0])
        total = term if total is None else total + term
    out_ref[...] = in_ref[...] + fold_columns(total)


def add_levels(side, queries, level_weight, total, states, first, place, name):
    rows, _ = queries.shape
    heads = states[0].shape[0]
    column_block = pl.BlockSpec((rows, DH), lambda h, s: (0, place(h, s)))
    return pl.pallas_call(
        functools.partial(levels_kernel, first, len(states)),
        out_shape=jax.ShapeDtypeStruct(total.shape, F32),
        grid_spec=pltpu.PrefetchScalarGridSpec(
            num_scalar_prefetch=1,
            grid=(heads,),
            in_specs=[
                column_block,
                pl.BlockSpec((1, *level_weight.shape[1:]), lambda h, s: (place(h, s), 0, 0)),
                *[pl.BlockSpec((1, DH, DH), lambda h, s: (h, 0, 0))] * len(states),
                column_block,
            ],
            out_specs=column_block,
        ),
        input_output_aliases={3 + len(states): 0},
        compiler_params=pltpu.CompilerParams(
            dimension_semantics=("arbitrary",), vmem_limit_bytes=VMEM_LIMIT
        ),
        cost_estimate=pl.CostEstimate(
            flops=2 * heads * rows * 256 * 256 * len(states),
            bytes_accessed=4 * heads * (3 * rows * DH + len(states) * DH * DH),
            transcendentals=0,
        ),
        name=name,
    )(side, queries, level_weight, *states, total)


def swapped(array, bit):
    size = lax.axis_size("seq")
    return lax.ppermute(array, "seq", [(i, i ^ 1 << bit) for i in range(size)])


def shards(queries, keys, values, level_weight, prefix_weight, prefix_state):
    heads = queries.shape[1] // DH
    levels = lax.axis_size("seq").bit_length() - 1
    chunks = 2
    per = heads // (2 * chunks)
    position = lax.axis_index("seq").astype(jnp.int32)
    side = jnp.stack([position & 1] + [(position >> b) & 1 for b in range(levels)])

    given = block_states(keys, values, True, chunks)
    received = [swapped(x, 0) for x in given]
    own = block_states(keys, values, False, chunks)
    total = base_part(queries, keys, values, level_weight, prefix_weight, prefix_state)

    own_states = [received]
    running = [a + b for a, b in zip(own, received)]
    for bit in range(1, levels):
        arrived = [swapped(x, bit) for x in running]
        own_states.append(arrived)
        running = [a + b for a, b in zip(running, arrived)]
    other_states = [[swapped(x, 0) for x in own]]
    for arrived in own_states[1:]:
        other_states.append([swapped(x, 0) for x in arrived])

    def own_place(c):
        return lambda h, s: (1 - s[0]) * (chunks * per) + c * per + h

    def other_place(c):
        return lambda h, s: s[0] * (chunks * per) + c * per + h

    for c in range(chunks):
        total = add_levels(
            side, queries, level_weight, total, [x[c] for x in own_states], 0, own_place(c), f"own{c}"
        )
    if levels > 1:
        for c in range(chunks):
            total = add_levels(
                side, queries, level_weight, total, [x[c] for x in other_states[:-1]], 0, other_place(c), f"other{c}"
            )
    for c in range(chunks):
        total = add_levels(
            side,
            queries,
            level_weight,
            total,
            [other_states[-1][c]],
            levels - 1,
            other_place(c),
            f"last{c}",
        )
    return total


def solution(mesh):
    return jax.shard_map(
        shards,
        mesh=mesh,
        in_specs=(
            P(("groups", "seq"), "head"),
            P(("groups", "seq"), "head"),
            P(("groups", "seq"), "head"),
            P("head", None, ("groups", "seq")),
            P("head", None, ("groups", "seq")),
            P("head", "groups", None),
        ),
        out_specs=P(("groups", "seq"), "head"),
        check_vma=False,
    )
```

time: 83 us -> 52.9 us (0.64)
  Pallas kernels: 0 us -> 26.8 us
  matrix products: 26.4 us -> 0 us
  waiting for transfers between devices: 21.2 us -> 3.61 us
  local copies, waits for them, and re-layouts: 18 us -> 3.28 us
  starting transfers between devices: 7.39 us -> 18.7 us
  other arithmetic: 9.53 us -> 0.14 us
    pallas_call x0 -> x9, Pallas kernels: none -> 26.8 us  [the longest x6 18.1 us: add_levels(): pl.pallas_call(functools.partial(levels_kernel, first, len(states)), out_...]
    dot_general x5 -> x0, matrix products: 26.4 us -> none  [the longest x1 10.5 us: shards(): jnp.einsum('htr,hre->the', weighted, prefix_state, precision=highest_level)]
    ppermute x3 -> x12, waiting for transfers between devices: 21.2 us -> 3.61 us  [swapped(): return lax.ppermute(array, 'seq', [(i, i ^ 1 << bit) for i in range(size)])]
    reshape x4 -> x0, local copies, waits for them, and re-layouts: 12.5 us -> none  [the longest x1 9.27 us: shards(): jnp.einsum('thd,hbt->htbd', query_heads, prefix_weight)]
    ppermute x3 -> x12, starting transfers between devices: 7.39 us -> 18.7 us  [swapped(): return lax.ppermute(array, 'seq', [(i, i ^ 1 << bit) for i in range(size)])]
    dot_general x1 -> x0, other arithmetic: 5.08 us -> none  [shards(): jnp.einsum('thd,hbt->htbd', query_heads, prefix_weight)]
    another operation x6 -> x0, local copies, waits for them, and re-layouts: 4.43 us -> none  [the longest x5 3.12 us: shards(): per_level_states = jnp.stack(collected)]
    another operation x3 -> x1, other arithmetic: 4.42 us -> 0.08 us  [shards(): jnp.stack([position & 1] + [position >> b & 1 for b in range(levels)])]
  transfers between devices with their start and end apart: 3 -> 12, of which waited for: 2 -> 1; matrix products, arithmetic and copies ran while one was open for 30% -> 2% of each run, Pallas kernels for 0% -> 44%
where the time goes in v1:
time: 52.9 us; the launch traced here: 52.6 us
  Pallas kernels  26.8 us (51%)
  starting transfers between devices  18.7 us (35%)
  waiting for transfers between devices  3.61 us (7%)
  local copies, waits for them, and re-layouts  3.28 us (6%)
    ppermute x12, starting transfers between devices, swapped(): return lax.ppermute(array, 'seq', [(i, i ^ 1 << bit) for i in range(size)])  18.7 us
    pallas_call x6, Pallas kernels, add_levels(): pl.pallas_call(functools.partial(levels_kernel, first, len(states)), out_...  18.1 us
    pallas_call x1, Pallas kernels, base_part(): pl.pallas_call(base_kernel, out_shape=jax.ShapeDtypeStruct((rows, columns...  7.29 us
    ppermute x12, waiting for transfers between devices, swapped(): return lax.ppermute(array, 'seq', [(i, i ^ 1 << bit) for i in range(size)])  3.61 us
    unnamed x11, local copies, waits for them, and re-layouts  3.28 us
    pallas_call x2, Pallas kernels, block_states(): pl.pallas_call(functools.partial(states_kernel, flip, chunks), out_shape=...  1.35 us
  transfers between devices with their start and end apart: 12, of which 1 were waited for; matrix products, arithmetic and copies ran while one was open for 2% of the time, Pallas kernels for 44%

profile of v1, /device:TPU:0, one launch (start us, length us, event | category | flops | bytes accessed | tf_op | source)
XLA Modules:
  0.0 52.6 jit_solution(3641696835475284991)
XLA Ops:
  0.0 1.2 %copy-done.1 = f32[256,1024]{1,0:T(8,128)S(1)} copy-done((f32[256,1024]{1,0:T(8,128)S(1)}, f32[256,1024]{1,0:T(8,128)}, u32[]{:S(2)}) %copy-start.1) | copy-done | bytes 1048600
  1.2 1.2 %copy-done.2 = f32[256,1024]{1,0:T(8,128)S(1)} copy-done((f32[256,1024]{1,0:T(8,128)S(1)}, f32[256,1024]{1,0:T(8,128)}, u32[]{:S(2)}) %copy-start.2) | copy-done | bytes 1048600
  2.5 0.7 %states_flip.1 = (f32[2,128,128]{2,1,0:T(8,128)S(1)}, f32[2,128,128]{2,1,0:T(8,128)S(1)}) custom-call(f32[256,1024]{1,0:T(8,128)S(1)} %copy-done.1, f32[256,1024]{1,0:T(8,128)S(1)} %copy-done.2), custom_call_target="tpu_custom_call" | custom-call | flops 134217728 | bytes 1048576 | tf_op jit(solution)/shard_map/states_flip/pallas_call | solution.py:74
  3.1 3.1 %collective-permute-start.4 = (f32[2,128,128]{2,1,0:T(8,128)S(1)}, f32[2,128,128]{2,1,0:T(8,128)S(1)}, u32[]{:S(2)}, u32[]{:S(2)}) collective-permute-start(f32[2,128,128]{2,1,0:T(8,128)S(1)} %get-tuple-element.12), channel_id=1, source_target_pairs={{0,2},{2,0},{4,6},{6,4},{8,10},{10,8},{12,14},{14,12},{1,3},{3,1},... | collective-permute-start | bytes 393224 | tf_op jit(solution)/shard_map/ppermute | solution.py:199
  6.2 0.1 collective-permute-start
  6.3 0.7 %states_own.1 = (f32[2,128,128]{2,1,0:T(8,128)S(1)}, f32[2,128,128]{2,1,0:T(8,128)S(1)}) custom-call(f32[256,1024]{1,0:T(8,128)S(1)} %copy-done.1, f32[256,1024]{1,0:T(8,128)S(1)} %copy-done.2), custom_call_target="tpu_custom_call" | custom-call | flops 134217728 | bytes 1048576 | tf_op jit(solution)/shard_map/states_own/pallas_call | solution.py:74
  7.0 3.6 %collective-permute-done.4.refs_0_ = f32[2,128,128]{2,1,0:T(8,128)S(1)} collective-permute-done((f32[2,128,128]{2,1,0:T(8,128)S(1)}, f32[2,128,128]{2,1,0:T(8,128)S(1)}, u32[]{:S(2)}, u32[]{:S(2)}) %collective-permute-start.4) | collective-permute-done | bytes 131104 | tf_op jit(solution)/shard_map/ppermute | solution.py:199
  10.6 2.1 %collective-permute-start.5 = (f32[2,128,128]{2,1,0:T(8,128)S(1)}, f32[2,128,128]{2,1,0:T(8,128)S(1)}, u32[]{:S(2)}, u32[]{:S(2)}) collective-permute-start(f32[2,128,128]{2,1,0:T(8,128)S(1)} %add.14), channel_id=1, source_target_pairs={{0,4},{2,6},{4,0},{6,2},{8,12},{10,14},{12,8},{14,10},{1,5},{3,7},... | collective-permute-start | bytes 393224 | tf_op jit(solution)/shard_map/ppermute | solution.py:199
  12.7 0.0 collective-permute-done.refs_0_
  12.7 1.7 %collective-permute-start.1 = (f32[2,128,128]{2,1,0:T(8,128)S(1)}, f32[2,128,128]{2,1,0:T(8,128)S(1)}, u32[]{:S(2)}, u32[]{:S(2)}) collective-permute-start(f32[2,128,128]{2,1,0:T(8,128)S(1)} %add.12), channel_id=1, source_target_pairs={{0,4},{2,6},{4,0},{6,2},{8,12},{10,14},{12,8},{14,10},{1,5},{3,7},... | collective-permute-start | bytes 393224 | tf_op jit(solution)/shard_map/ppermute | solution.py:199
  14.4 1.5 %collective-permute-start.10 = (f32[2,128,128]{2,1,0:T(8,128)S(1)}, f32[2,128,128]{2,1,0:T(8,128)S(1)}, u32[]{:S(2)}, u32[]{:S(2)}) collective-permute-start(f32[2,128,128]{2,1,0:T(8,128)S(1)} %get-tuple-element.11), channel_id=1, source_target_pairs={{0,2},{2,0},{4,6},{6,4},{8,10},{10,8},{12,14},{14,12},{1,3},{3,1},... | collective-permute-start | bytes 393224 | tf_op jit(solution)/shard_map/ppermute | solution.py:199
  15.9 0.5 collective-permute-start.8
  16.4 0.8 %copy.19.level_ref = f32[8,6,256]{2,1,0:T(8,128)S(1)} copy(f32[8,6,256]{2,0,1:T(8,128)} %param.9) | data formatting | bytes 98304 | tf_op args[3]
  17.2 0.0 collective-permute-done.5.refs_1_
  17.3 2.9 %collective-permute-start.6 = (f32[2,128,128]{2,1,0:T(8,128)S(1)}, f32[2,128,128]{2,1,0:T(8,128)S(1)}, u32[]{:S(2)}, u32[]{:S(2)}) collective-permute-start(f32[2,128,128]{2,1,0:T(8,128)S(1)} %add.15), channel_id=1, source_target_pairs={{0,8},{2,10},{4,12},{6,14},{8,0},{10,2},{12,4},{14,6},{1,9},{3,11}... | collective-permute-start | bytes 393224 | tf_op jit(solution)/shard_map/ppermute | solution.py:199
  20.2 0.0 collective-permute-done.1.refs_1_
  20.2 2.8 %collective-permute-start.2 = (f32[2,128,128]{2,1,0:T(8,128)S(1)}, f32[2,128,128]{2,1,0:T(8,128)S(1)}, u32[]{:S(2)}, u32[]{:S(2)}) collective-permute-start(f32[2,128,128]{2,1,0:T(8,128)S(1)} %add.13), channel_id=1, source_target_pairs={{0,8},{2,10},{4,12},{6,14},{8,0},{10,2},{12,4},{14,6},{1,9},{3,11}... | collective-permute-start | bytes 393224 | tf_op jit(solution)/shard_map/ppermute | solution.py:199
  23.0 7.3 %base_part.1.refs_3_ = f32[256,1024]{1,0:T(8,128)} custom-call(f32[256,1024]{1,0:T(8,128)S(1)} %copy-done, f32[256,1024]{1,0:T(8,128)S(1)} %copy-done.1, f32[256,1024]{1,0:T(8,128)S(1)} %copy-done.2, f32[8,6,256]{2,1,0:T(8,128)S(1)} %copy.19.level_ref, f32[8,8,256]{2,1,0:T(8,128)S(1)} %copy-done.4, f32[8,1024,128]{2,1,0:T(8,128)S(1)} %copy-done.3), custom_call_target="tpu_custom_call" | custom-call | flops 3221225472 | bytes 8388608 | tf_op jit(solution)/shard_map/base_part/pallas_call | solution.py:127
  30.3 1.5 %collective-permute-start.11 = (f32[2,128,128]{2,1,0:T(8,128)S(1)}, f32[2,128,128]{2,1,0:T(8,128)S(1)}, u32[]{:S(2)}, u32[]{:S(2)}) collective-permute-start(f32[2,128,128]{2,1,0:T(8,128)S(1)} %collective-permute-done.5.refs_1_), channel_id=1, source_target_pairs={{0,2},{2,0},{4,6},{6,4},{8,10},{10,8},{12,14},{14,12},{1,3},{3,1},... | collective-permute-start | bytes 393224 | tf_op jit(solution)/shard_map/ppermute | solution.py:199
  31.8 0.0 collective-permute-done.10.refs_0_
  31.8 0.5 collective-permute-start.9
  32.3 0.0 collective-permute-done.6.refs_2_
  32.3 1.5 %collective-permute-start.7 = (f32[2,128,128]{2,1,0:T(8,128)S(1)}, f32[2,128,128]{2,1,0:T(8,128)S(1)}, u32[]{:S(2)}, u32[]{:S(2)}) collective-permute-start(f32[2,128,128]{2,1,0:T(8,128)S(1)} %collective-permute-done.6.refs_2_), channel_id=1, source_target_pairs={{0,2},{2,0},{4,6},{6,4},{8,10},{10,8},{12,14},{14,12},{1,3},{3,1},... | collective-permute-start | bytes 393224 | tf_op jit(solution)/shard_map/ppermute | solution.py:199
  33.8 0.5 collective-permute-start.3
  34.3 0.1 pad_add_fusion.side_ref
  34.4 3.0 %own0.1.refs_3_ = f32[256,1024]{1,0:T(8,128)} custom-call(s32[4]{0:T(128)S(1)} %pad_add_fusion.side_ref, f32[256,1024]{1,0:T(8,128)S(1)} %copy-done, f32[8,6,256]{2,1,0:T(8,128)S(1)} %copy.19.level_ref, f32[2,128,128]{2,1,0:T(8,128)S(1)} %collective-permute-done.4.refs_0_, ...), custom_call_target="tpu_custom_call", output_to_operand_aliasing={{}: (6, {})} | custom-call | flops 201326592 | bytes 1179648 | tf_op jit(solution)/shard_map/own0/pallas_call | solution.py:170
  37.4 3.0 %own1.1.refs_2_ = f32[256,1024]{1,0:T(8,128)} custom-call(s32[4]{0:T(128)S(1)} %pad_add_fusion.side_ref, f32[256,1024]{1,0:T(8,128)S(1)} %copy-done, f32[8,6,256]{2,1,0:T(8,128)S(1)} %copy.19.level_ref, f32[2,128,128]{2,1,0:T(8,128)S(1)} %collective-permute-done.refs_0_, ...), custom_call_target="tpu_custom_call", output_to_operand_aliasing={{}: (6, {})} | custom-call | flops 201326592 | bytes 1179648 | tf_op jit(solution)/shard_map/own1/pallas_call | solution.py:170
  40.4 3.1 %other0.1.refs_2_ = f32[256,1024]{1,0:T(8,128)} custom-call(s32[4]{0:T(128)S(1)} %pad_add_fusion.side_ref, f32[256,1024]{1,0:T(8,128)S(1)} %copy-done, f32[8,6,256]{2,1,0:T(8,128)S(1)} %copy.19.level_ref, f32[2,128,128]{2,1,0:T(8,128)S(1)} %collective-permute-done.10.refs_0_, ...), custom_call_target="tpu_custom_call", output_to_operand_aliasing={{}: (5, {})} | custom-call | flops 134217728 | bytes 1048576 | tf_op jit(solution)/shard_map/other0/pallas_call | solution.py:170
  43.6 3.1 %other1.1.refs_1_ = f32[256,1024]{1,0:T(8,128)} custom-call(s32[4]{0:T(128)S(1)} %pad_add_fusion.side_ref, f32[256,1024]{1,0:T(8,128)S(1)} %copy-done, f32[8,6,256]{2,1,0:T(8,128)S(1)} %copy.19.level_ref, f32[2,128,128]{2,1,0:T(8,128)S(1)} %collective-permute-done.8.refs_0_, ...), custom_call_target="tpu_custom_call", output_to_operand_aliasing={{}: (5, {})} | custom-call | flops 134217728 | bytes 1048576 | tf_op jit(solution)/shard_map/other1/pallas_call | solution.py:170
  46.7 2.9 %last0.1.refs_1_ = f32[256,1024]{1,0:T(8,128)} custom-call(s32[4]{0:T(128)S(1)} %pad_add_fusion.side_ref, f32[256,1024]{1,0:T(8,128)S(1)} %copy-done, f32[8,6,256]{2,1,0:T(8,128)S(1)} %copy.19.level_ref, f32[2,128,128]{2,1,0:T(8,128)S(1)} %collective-permute-done.7.refs_0_, f32[256,1024]{1,0:T(8,128)} %other1.1.refs_1_), custom_call_target="tpu_custom_call", output_to_operand_aliasing={{}: (4, {})} | custom-call | flops 67108864 | bytes 917504 | tf_op jit(solution)/shard_map/last0/pallas_call | solution.py:170
  49.6 0.0 collective-permute-done.3.refs_0_
  49.6 2.9 %last1.1 = f32[256,1024]{1,0:T(8,128)} custom-call(s32[4]{0:T(128)S(1)} %pad_add_fusion.side_ref, f32[256,1024]{1,0:T(8,128)S(1)} %copy-done, f32[8,6,256]{2,1,0:T(8,128)S(1)} %copy.19.level_ref, f32[2,128,128]{2,1,0:T(8,128)S(1)} %collective-permute-done.3.refs_0_, f32[256,1024]{1,0:T(8,128)} %last0.1.refs_1_), custom_call_target="tpu_custom_call", output_to_operand_aliasing={{}: (4, {})} | custom-call | flops 67108864 | bytes 917504 | tf_op jit(solution)/shard_map/last1/pallas_call | solution.py:170
  (17 shorter events, 0.1 us)
Async XLA Ops:
  0.0 1.2 %copy-start.1 = (f32[256,1024]{1,0:T(8,128)S(1)}, f32[256,1024]{1,0:T(8,128)}, u32[]{:S(2)}) copy-start(f32[256,1024]{1,0:T(8,128)} %k_ref.1) | copy-start | bytes 3145732
  1.2 1.2 %copy-start.2 = (f32[256,1024]{1,0:T(8,128)S(1)}, f32[256,1024]{1,0:T(8,128)}, u32[]{:S(2)}) copy-start(f32[256,1024]{1,0:T(8,128)} %v_ref.1) | copy-start | bytes 3145732
  2.5 20.5 %copy-start = (f32[256,1024]{1,0:T(8,128)S(1)}, f32[256,1024]{1,0:T(8,128)}, u32[]{:S(2)}) copy-start(f32[256,1024]{1,0:T(8,128)} %q_ref.13) | copy-start | bytes 3145732
  2.5 20.5 %copy-start.3 = (f32[8,1024,128]{2,1,0:T(8,128)S(1)}, f32[8,1024,128]{2,1,0:T(8,128)}, u32[]{:S(2)}) copy-start(f32[8,1024,128]{2,1,0:T(8,128)} %prefix_ref.1) | copy-start | bytes 12582916
  2.5 20.5 %copy-start.4 = (f32[8,8,256]{2,1,0:T(8,128)S(1)}, f32[8,8,256]{2,1,0:T(8,128)}, u32[]{:S(2)}) copy-start(f32[8,8,256]{2,1,0:T(8,128)} %bucket_ref.1) | copy-start | bytes 196612
  3.1 7.4 %collective-permute-start.4 = (f32[2,128,128]{2,1,0:T(8,128)S(1)}, f32[2,128,128]{2,1,0:T(8,128)S(1)}, u32[]{:S(2)}, u32[]{:S(2)}) collective-permute-start(f32[2,128,128]{2,1,0:T(8,128)S(1)} %get-tuple-element.12), channel_id=1, source_target_pairs={{0,2},{2,0},{4,6},{6,4},{8,10},{10,8},{12,14},{14,12},{1,3},{3,1},... | collective-permute-start | bytes 393224 | tf_op jit(solution)/shard_map/ppermute | solution.py:199
  6.2 6.5 %collective-permute-start = (f32[2,128,128]{2,1,0:T(8,128)S(1)}, f32[2,128,128]{2,1,0:T(8,128)S(1)}, u32[]{:S(2)}, u32[]{:S(2)}) collective-permute-start(f32[2,128,128]{2,1,0:T(8,128)S(1)} %get-tuple-element.10), channel_id=1, source_target_pairs={{0,2},{2,0},{4,6},{6,4},{8,10},{10,8},{12,14},{14,12},{1,3},{3,1},... | collective-permute-start | bytes 393224 | tf_op jit(solution)/shard_map/ppermute | solution.py:199
  10.6 6.7 %collective-permute-start.5 = (f32[2,128,128]{2,1,0:T(8,128)S(1)}, f32[2,128,128]{2,1,0:T(8,128)S(1)}, u32[]{:S(2)}, u32[]{:S(2)}) collective-permute-start(f32[2,128,128]{2,1,0:T(8,128)S(1)} %add.14), channel_id=1, source_target_pairs={{0,4},{2,6},{4,0},{6,2},{8,12},{10,14},{12,8},{14,10},{1,5},{3,7},... | collective-permute-start | bytes 393224 | tf_op jit(solution)/shard_map/ppermute | solution.py:199
  12.7 7.4 %collective-permute-start.1 = (f32[2,128,128]{2,1,0:T(8,128)S(1)}, f32[2,128,128]{2,1,0:T(8,128)S(1)}, u32[]{:S(2)}, u32[]{:S(2)}) collective-permute-start(f32[2,128,128]{2,1,0:T(8,128)S(1)} %add.12), channel_id=1, source_target_pairs={{0,4},{2,6},{4,0},{6,2},{8,12},{10,14},{12,8},{14,10},{1,5},{3,7},... | collective-permute-start | bytes 393224 | tf_op jit(solution)/shard_map/ppermute | solution.py:199
  14.4 17.4 %collective-permute-start.10 = (f32[2,128,128]{2,1,0:T(8,128)S(1)}, f32[2,128,128]{2,1,0:T(8,128)S(1)}, u32[]{:S(2)}, u32[]{:S(2)}) collective-permute-start(f32[2,128,128]{2,1,0:T(8,128)S(1)} %get-tuple-element.11), channel_id=1, source_target_pairs={{0,2},{2,0},{4,6},{6,4},{8,10},{10,8},{12,14},{14,12},{1,3},{3,1},... | collective-permute-start | bytes 393224 | tf_op jit(solution)/shard_map/ppermute | solution.py:199
  15.9 27.6 %collective-permute-start.8 = (f32[2,128,128]{2,1,0:T(8,128)S(1)}, f32[2,128,128]{2,1,0:T(8,128)S(1)}, u32[]{:S(2)}, u32[]{:S(2)}) collective-permute-start(f32[2,128,128]{2,1,0:T(8,128)S(1)} %get-tuple-element.9), channel_id=1, source_target_pairs={{0,2},{2,0},{4,6},{6,4},{8,10},{10,8},{12,14},{14,12},{1,3},{3,1},... | collective-permute-start | bytes 393224 | tf_op jit(solution)/shard_map/ppermute | solution.py:199
  17.3 15.0 %collective-permute-start.6 = (f32[2,128,128]{2,1,0:T(8,128)S(1)}, f32[2,128,128]{2,1,0:T(8,128)S(1)}, u32[]{:S(2)}, u32[]{:S(2)}) collective-permute-start(f32[2,128,128]{2,1,0:T(8,128)S(1)} %add.15), channel_id=1, source_target_pairs={{0,8},{2,10},{4,12},{6,14},{8,0},{10,2},{12,4},{14,6},{1,9},{3,11}... | collective-permute-start | bytes 393224 | tf_op jit(solution)/shard_map/ppermute | solution.py:199
  20.2 13.7 %collective-permute-start.2 = (f32[2,128,128]{2,1,0:T(8,128)S(1)}, f32[2,128,128]{2,1,0:T(8,128)S(1)}, u32[]{:S(2)}, u32[]{:S(2)}) collective-permute-start(f32[2,128,128]{2,1,0:T(8,128)S(1)} %add.13), channel_id=1, source_target_pairs={{0,8},{2,10},{4,12},{6,14},{8,0},{10,2},{12,4},{14,6},{1,9},{3,11}... | collective-permute-start | bytes 393224 | tf_op jit(solution)/shard_map/ppermute | solution.py:199
  30.3 10.2 %collective-permute-start.11 = (f32[2,128,128]{2,1,0:T(8,128)S(1)}, f32[2,128,128]{2,1,0:T(8,128)S(1)}, u32[]{:S(2)}, u32[]{:S(2)}) collective-permute-start(f32[2,128,128]{2,1,0:T(8,128)S(1)} %collective-permute-done.5.refs_1_), channel_id=1, source_target_pairs={{0,2},{2,0},{4,6},{6,4},{8,10},{10,8},{12,14},{14,12},{1,3},{3,1},... | collective-permute-start | bytes 393224 | tf_op jit(solution)/shard_map/ppermute | solution.py:199
  31.8 11.8 %collective-permute-start.9 = (f32[2,128,128]{2,1,0:T(8,128)S(1)}, f32[2,128,128]{2,1,0:T(8,128)S(1)}, u32[]{:S(2)}, u32[]{:S(2)}) collective-permute-start(f32[2,128,128]{2,1,0:T(8,128)S(1)} %collective-permute-done.1.refs_1_), channel_id=1, source_target_pairs={{0,2},{2,0},{4,6},{6,4},{8,10},{10,8},{12,14},{14,12},{1,3},{3,1},... | collective-permute-start | bytes 393224 | tf_op jit(solution)/shard_map/ppermute | solution.py:199
  32.3 14.4 %collective-permute-start.7 = (f32[2,128,128]{2,1,0:T(8,128)S(1)}, f32[2,128,128]{2,1,0:T(8,128)S(1)}, u32[]{:S(2)}, u32[]{:S(2)}) collective-permute-start(f32[2,128,128]{2,1,0:T(8,128)S(1)} %collective-permute-done.6.refs_2_), channel_id=1, source_target_pairs={{0,2},{2,0},{4,6},{6,4},{8,10},{10,8},{12,14},{14,12},{1,3},{3,1},... | collective-permute-start | bytes 393224 | tf_op jit(solution)/shard_map/ppermute | solution.py:199
  33.8 15.8 %collective-permute-start.3 = (f32[2,128,128]{2,1,0:T(8,128)S(1)}, f32[2,128,128]{2,1,0:T(8,128)S(1)}, u32[]{:S(2)}, u32[]{:S(2)}) collective-permute-start(f32[2,128,128]{2,1,0:T(8,128)S(1)} %collective-permute-done.2.refs_2_), channel_id=1, source_target_pairs={{0,2},{2,0},{4,6},{6,4},{8,10},{10,8},{12,14},{14,12},{1,3},{3,1},... | collective-permute-start | bytes 393224 | tf_op jit(solution)/shard_map/ppermute | solution.py:199

commit v2 on v0

v2 whole, which is shorter than its diff:
```python
import functools

import jax
import jax.numpy as jnp
from jax import lax
from jax.experimental import pallas as pl
from jax.experimental.pallas import tpu as pltpu
from jax.sharding import PartitionSpec as P

DH = 128
BF16 = jnp.bfloat16
F32 = jnp.float32
PARTS = 2
GRANT = 67043328
IN_VMEM = pl.BlockSpec(memory_space=pltpu.VMEM)
IN_HBM = pl.BlockSpec(memory_space=pltpu.HBM)


def split(x):
    high = x.astype(BF16)
    low = (x - high.astype(F32)).astype(BF16)
    return high, low


def beside(x):
    return jnp.concatenate(split(x), axis=1)


def fold_columns(x):
    half = x.shape[1] // 2
    return x[:, :half] + x[:, half:]


def outer_state(k, v):
    full = lax.dot_general(
        beside(k), beside(v), (((0,), (0,)), ((), ())), preferred_element_type=F32
    )
    full = fold_columns(full)
    return full[:DH] + full[DH:]


def through_state(scaled, state):
    wide = beside(state)
    return jnp.dot(
        beside(scaled), jnp.concatenate([wide, wide], axis=0), preferred_element_type=F32
    )


def first_head(place, per):
    own = 1 - lax.rem(lax.axis_index("seq"), 2)
    half = own if place < PARTS else 1 - own
    return (half * PARTS + place % PARTS) * per


def head_columns(head, count=1):
    return pl.ds(pl.multiple_of(head * DH, DH), count * DH)


def given_kernel(k_hbm, v_hbm, *refs):
    outs = refs[:PARTS]
    k_buf, v_buf, sems = refs[PARTS:]
    per = outs[0].shape[0]
    copies = []
    for c in range(PARTS):
        columns = head_columns(first_head(PARTS + c, per), per)
        pair = (
            pltpu.make_async_copy(k_hbm.at[:, columns], k_buf.at[c], sems.at[0, c]),
            pltpu.make_async_copy(v_hbm.at[:, columns], v_buf.at[c], sems.at[1, c]),
        )
        for copy in pair:
            copy.start()
        copies.append(pair)
    for c in range(PARTS):
        for copy in copies[c]:
            copy.wait()
        for j in range(per):
            at = slice(j * DH, (j + 1) * DH)
            outs[c][j] = outer_state(k_buf[c, :, at], v_buf[c, :, at])


def given_states(keys, values):
    rows, columns = keys.shape
    width = columns // (2 * PARTS)
    return pl.pallas_call(
        given_kernel,
        out_shape=[jax.ShapeDtypeStruct((width // DH, DH, DH), F32)] * PARTS,
        in_specs=[IN_HBM] * 2,
        out_specs=[IN_VMEM] * PARTS,
        scratch_shapes=[
            pltpu.VMEM((PARTS, rows, width), F32),
            pltpu.VMEM((PARTS, rows, width), F32),
            pltpu.SemaphoreType.DMA((2, PARTS)),
        ],
        compiler_params=pltpu.CompilerParams(vmem_limit_bytes=GRANT - columns * DH * 5),
        cost_estimate=pl.CostEstimate(
            flops=4 * rows * columns * DH, bytes_accessed=4 * rows * columns, transcendentals=0
        ),
        name="states_given",
    )(keys, values)


def own_kernel(
    level_ref, bucket_ref, q_hbm, k_hbm, v_hbm, q_out, k_out, v_out, weight_ref, whole_ref, *refs
):
    part_refs, sems = refs[:-1], refs[-1]
    per = part_refs[0].shape[0]
    half = PARTS * per
    copies = []
    for i, (source, to) in enumerate(((k_hbm, k_out), (v_hbm, v_out), (q_hbm, q_out))):
        for h in range(2):
            copy = pltpu.make_async_copy(
                source.at[:, head_columns(first_head(h * PARTS, per), half)],
                to.at[:, h * half * DH : (h + 1) * half * DH],
                sems.at[i, h],
            )
            copy.start()
            copies.append(copy)
    position = lax.axis_index("seq")
    own_second = lax.rem(position, 2) == 0
    levels, heads, rows = level_ref.shape
    buckets = bucket_ref.shape[1]
    lines = []
    for i in range(levels):
        line = level_ref[i]
        if i:
            line = line * lax.rem(lax.shift_right_logical(position, i - 1), 2).astype(F32)
        lines.append(jnp.where(own_second, jnp.concatenate([line[half:], line[:half]], axis=0), line))
    first = jnp.where(own_second, half, 0)
    for h in range(heads):
        lines.append(bucket_ref[lax.rem(first + h, heads)])
    spare = weight_ref.shape[1] - heads * (levels + buckets)
    if spare:
        lines.append(jnp.zeros((spare, rows), F32))
    weight_ref[...] = jnp.transpose(jnp.concatenate(lines, axis=0))

    copies[0].wait()
    copies[2].wait()
    for c, part_ref in enumerate(part_refs):
        for j in range(per):
            at = slice((c * per + j) * DH, (c * per + j + 1) * DH)
            state = outer_state(k_out[:, at], v_out[:, at])
            part_ref[j] = state
            whole_ref[c * per + j] = state
    for i in (1, 3, 4, 5):
        copies[i].wait()


def own_block_states(queries, keys, values, level_weight, prefix_weight):
    rows, columns = keys.shape
    heads = columns // DH
    per = heads // (2 * PARTS)
    weights = heads * (level_weight.shape[1] + prefix_weight.shape[1])
    shapes = [queries.shape, keys.shape, values.shape, (rows, pl.cdiv(weights, DH) * DH)]
    shapes += [(PARTS * per, DH, DH)] + [(per, DH, DH)] * PARTS
    return pl.pallas_call(
        own_kernel,
        out_shape=[jax.ShapeDtypeStruct(s, F32) for s in shapes],
        in_specs=[IN_VMEM] * 2 + [IN_HBM] * 3,
        out_specs=[IN_VMEM] * len(shapes),
        scratch_shapes=[pltpu.SemaphoreType.DMA((3, 2))],
        compiler_params=pltpu.CompilerParams(vmem_limit_bytes=GRANT - 14 * rows * columns * 4),
        cost_estimate=pl.CostEstimate(
            flops=4 * rows * columns * DH, bytes_accessed=24 * rows * columns, transcendentals=0
        ),
        name="states_own",
    )(jnp.transpose(level_weight, (1, 0, 2)), prefix_weight, queries, keys, values)


def base_kernel(place, levels, buckets, q_ref, k_ref, v_ref, weight_ref, prefix_hbm, out_ref, buf, sems):
    rows = q_ref.shape[0]
    heads = prefix_hbm.shape[0]
    per = out_ref.shape[1] // DH
    start = first_head(place, per)
    copies = []
    for j in range(per):
        copies.append(pltpu.make_async_copy(prefix_hbm.at[start + j], buf.at[j], sems.at[j]))
        copies[j].start()
    row = lax.broadcasted_iota(jnp.int32, (rows, rows), 0)
    column = lax.broadcasted_iota(jnp.int32, (rows, rows), 1)
    nt = (((1,), (1,)), ((), ()))
    for j in range(per):
        head = place * per + j
        q, k, v = (ref[:, head * DH : (head + 1) * DH] for ref in (q_ref, k_ref, v_ref))
        k_high, k_low = split(k)
        q_wide = beside(q)
        scores = lax.dot_general(
            q_wide, jnp.concatenate([k_high, k_high], axis=1), nt, preferred_element_type=F32
        ) + lax.dot_general(
            q_wide, jnp.concatenate([k_low, k_low], axis=1), nt, preferred_element_type=F32
        )
        scores = jnp.where(column <= row, scores, 0.0) * weight_ref[:, head : head + 1]
        scores_high, scores_low = split(scores)
        v_wide = beside(v)
        total = jnp.dot(scores_high, v_wide, preferred_element_type=F32)
        total += jnp.dot(scores_low, v_wide, preferred_element_type=F32)
        copies[j].wait()
        for b in range(buckets):
            at = heads * levels + head * buckets + b
            total += through_state(
                q * weight_ref[:, at : at + 1], buf[j, b * DH : (b + 1) * DH, :]
            )
        out_ref[:, j * DH : (j + 1) * DH] = fold_columns(total)


def base_part(place, levels, buckets, loaded, prefix_state):
    rows, columns = loaded[0].shape
    width = columns // (2 * PARTS)
    per = width // DH
    return pl.pallas_call(
        functools.partial(base_kernel, place, levels, buckets),
        out_shape=jax.ShapeDtypeStruct((rows, width), F32),
        in_specs=[IN_VMEM] * len(loaded) + [IN_HBM],
        out_specs=IN_VMEM,
        scratch_shapes=[
            pltpu.VMEM((per, *prefix_state.shape[1:]), F32),
            pltpu.SemaphoreType.DMA((per,)),
        ],
        compiler_params=pltpu.CompilerParams(vmem_limit_bytes=GRANT - 16 * rows * columns * 4),
        cost_estimate=pl.CostEstimate(
            flops=2 * width * rows * rows * 24,
            bytes_accessed=16 * rows * width,
            transcendentals=0,
        ),
    )(*loaded, prefix_state)


def levels_kernel(places, first, spread, store, q_ref, weight_ref, *refs):
    count = 1 + max(ref for rows in spread for ref, _ in rows)
    state_refs, refs = refs[:count], refs[count:]
    base_refs, refs = refs[: len(places)], refs[len(places) :]
    per = base_refs[0].shape[1] // DH
    heads = q_ref.shape[1] // DH
    if store:
        out_hbm, buf, sems = refs[-3:]
    copies = []
    for c, place in enumerate(places):
        for j in range(per):
            at = slice(j * DH, (j + 1) * DH)
            head = place * per + j
            q = q_ref[:, head * DH : (head + 1) * DH]
            total = None
            for i, rows in enumerate(spread):
                column = (1 + first + i) * heads + head
                ref, entry = rows[c]
                term = through_state(q * weight_ref[:, column : column + 1], state_refs[ref][entry + j])
                total = term if total is None else total + term
            done = base_refs[c][:, at] + fold_columns(total)
            if store:
                buf[c, :, at] = done
            else:
                refs[c][:, at] = done
        if store:
            columns = head_columns(first_head(place, per), per)
            copy = pltpu.make_async_copy(buf.at[c], out_hbm.at[:, columns], sems.at[c])
            copy.start()
            copies.append(copy)
    for copy in copies:
        copy.wait()


def add_levels(queries, weights, bases, states, spread, places, first, store, out):
    rows, columns = queries.shape
    width = columns // (2 * PARTS)
    count = len(places)
    operands = [queries, weights, *states, *bases]
    in_specs = [IN_VMEM] * len(operands)
    aliases = {}
    if out is not None:
        aliases = {len(operands): 0}
        operands.append(out)
        in_specs.append(IN_HBM)
    shape = (rows, columns) if store else (rows, width)
    return pl.pallas_call(
        functools.partial(levels_kernel, places, first, spread, store),
        out_shape=[jax.ShapeDtypeStruct(shape, F32)] * (1 if store else count),
        in_specs=in_specs,
        out_specs=[IN_HBM if store else IN_VMEM] * (1 if store else count),
        scratch_shapes=[pltpu.VMEM((count, rows, width), F32), pltpu.SemaphoreType.DMA((count,))]
        if store
        else [],
        input_output_aliases=aliases,
        compiler_params=pltpu.CompilerParams(vmem_limit_bytes=GRANT // 4),
        cost_estimate=pl.CostEstimate(
            flops=4 * count * width * rows * rows * len(spread),
            bytes_accessed=12 * rows * width * count,
            transcendentals=0,
        ),
    )(*operands)


def swapped(array, bit, keep=lambda i: True):
    size = lax.axis_size("seq")
    pairs = [(i, i ^ 1 << bit) for i in range(size) if keep(i)]
    return lax.ppermute(array, "seq", pairs)


def attend(queries, keys, values, level_weight, prefix_weight, prefix_state):
    levels = lax.axis_size("seq").bit_length() - 1
    per = queries.shape[1] // DH // (2 * PARTS)
    places = range(PARTS)

    given = given_states(keys, values)
    received = [swapped(given[c], 0) for c in places]
    *loaded, own, part0, part1 = own_block_states(
        queries, keys, values, level_weight, prefix_weight
    )
    parts = (part0, part1)
    query_places, weights = loaded[0], loaded[-1]
    base = []
    for place in range(2 * PARTS):
        base.append(
            base_part(place, level_weight.shape[1], prefix_weight.shape[1], loaded, prefix_state)
        )

    own_states = [list(received)]
    running = [parts[c] + received[c] for c in places]
    for bit in range(1, levels):
        arrived = [swapped(running[c], bit) for c in places]
        own_states.append(arrived)
        running = [a + b for a, b in zip(running, arrived)]
    other_states = [[swapped(own, 0)]]
    for bit in range(1, levels - 1):
        both = jnp.concatenate(own_states[bit], axis=0)
        other_states.append([swapped(both, 0, lambda i: i >> bit & 1)])
    top = levels - 1
    last = [swapped(own_states[top][c], 0, lambda i: i >> top & 1) for c in places]

    spread = [[(i, c * per) for c in places] for i in range(levels - 1)]
    middle = add_levels(
        query_places, weights, base[PARTS:], [x[0] for x in other_states], spread, (2, 3), 0, False, None
    )
    flat = [x for level in own_states for x in level]
    spread = [[(i * PARTS + c, 0) for c in places] for i in range(levels)]
    (out,) = add_levels(query_places, weights, base[:PARTS], flat, spread, (0, 1), 0, True, None)
    for c in places:
        (out,) = add_levels(query_places, weights, [middle[c]], [last[c]], [[(0, 0)]], (PARTS + c,), top, True, out)
    return out


def solution(mesh):
    return jax.shard_map(
        attend,
        mesh=mesh,
        in_specs=(
            P(("groups", "seq"), "head"),
            P(("groups", "seq"), "head"),
            P(("groups", "seq"), "head"),
            P("head", None, ("groups", "seq")),
            P("head", None, ("groups", "seq")),
            P("head", "groups", None),
        ),
        out_specs=P(("groups", "seq"), "head"),
        check_vma=False,
    )
```

time: 83 us -> 39.7 us (0.48)
  the two profiles are of different devices: /device:TPU:0 before, /device:TPU:24 now
where the time goes in v2:
time: 39.7 us; the launch traced here: 39.3 us
  Pallas kernels  18.4 us (46%)
  starting transfers between devices  16 us (40%)
  waiting for transfers between devices  3 us (8%)
  local copies, waits for them, and re-layouts  1.64 us (4%)
    ppermute x10, starting transfers between devices, swapped(): return lax.ppermute(array, 'seq', pairs)  16 us
    pallas_call x4, Pallas kernels, base_part(): pl.pallas_call(functools.partial(base_kernel, place, levels, buckets), ou...  10.2 us
    pallas_call x4, Pallas kernels, add_levels(): pl.pallas_call(functools.partial(levels_kernel, places, first, spread, st...  4.06 us
    ppermute x10, waiting for transfers between devices, swapped(): return lax.ppermute(array, 'seq', pairs)  3 us
    pallas_call x1, Pallas kernels, given_states(): pl.pallas_call(given_kernel, out_shape=[jax.ShapeDtypeStruct((width // DH...  2.27 us
    pallas_call x1, Pallas kernels, own_block_states(): pl.pallas_call(own_kernel, out_shape=[jax.ShapeDtypeStruct(s, F32) for s...  1.9 us
    unnamed x4, local copies, waits for them, and re-layouts  1.64 us
  transfers between devices with their start and end apart: 10, of which 3 were waited for; matrix products, arithmetic and copies ran while one was open for 0% of the time, Pallas kernels for 39%

profile of v2, /device:TPU:24, one launch (start us, length us, event | category | flops | bytes accessed | tf_op | source)
XLA Modules:
  0.0 39.3 jit_solution(1231558488152819783)
XLA Ops:
  0.0 2.3 %states_given.1 = (f32[2,128,128]{2,1,0:T(8,128)}, f32[2,128,128]{2,1,0:T(8,128)}) custom-call(f32[256,1024]{1,0:T(8,128)} %k_hbm.3, f32[256,1024]{1,0:T(8,128)} %v_hbm.3), custom_call_target="tpu_custom_call" | custom-call | flops 134217728 | bytes 1048576 | tf_op jit(solution)/shard_map/states_given/pallas_call | solution.py:84
  2.3 1.6 %collective-permute-start = (f32[2,128,128]{2,1,0:T(8,128)}, f32[2,128,128]{2,1,0:T(8,128)S(1)}, u32[]{:S(2)}, u32[]{:S(2)}) collective-permute-start(f32[2,128,128]{2,1,0:T(8,128)} %get-tuple-element.19), channel_id=1, source_target_pairs={{0,2},{2,0},{4,6},{6,4},{8,10},{10,8},{12,14},{14,12},{1,3},{3,1},... | collective-permute-start | bytes 393224 | tf_op jit(solution)/shard_map/ppermute | solution.py:294
  3.9 0.5 %collective-permute-start.5 = (f32[2,128,128]{2,1,0:T(8,128)}, f32[2,128,128]{2,1,0:T(8,128)S(1)}, u32[]{:S(2)}, u32[]{:S(2)}) collective-permute-start(f32[2,128,128]{2,1,0:T(8,128)} %get-tuple-element.22), channel_id=1, source_target_pairs={{0,2},{2,0},{4,6},{6,4},{8,10},{10,8},{12,14},{14,12},{1,3},{3,1},... | collective-permute-start | bytes 393224 | tf_op jit(solution)/shard_map/ppermute | solution.py:294
  4.4 0.8 %copy-done = f32[8,8,256]{2,1,0:T(8,128)S(1)} copy-done((f32[8,8,256]{2,1,0:T(8,128)S(1)}, f32[8,8,256]{2,1,0:T(8,128)}, u32[]{:S(2)}) %copy-start) | copy-done | bytes 65560
  5.2 0.8 %copy-done.1 = f32[8,6,256]{2,0,1:T(8,128)S(1)} copy-done((f32[8,6,256]{2,0,1:T(8,128)S(1)}, f32[8,6,256]{2,0,1:T(8,128)}, u32[]{:S(2)}) %copy-start.1) | copy-done | bytes 49176
  6.0 1.9 %states_own.1 = (f32[256,1024]{1,0:T(8,128)S(1)}, f32[256,1024]{1,0:T(8,128)S(1)}, f32[256,1024]{1,0:T(8,128)S(1)}, f32[256,128]{1,0:T(8,128)S(1)}, f32[4,128,12...) custom-call(f32[6,8,256]{2,1,0:T(8,128)S(1)} %bitcast.1, f32[8,8,256]{2,1,0:T(8,128)S(1)} %copy-done, ...), custom_call_target="tpu_custom_call" | custom-call | flops 134217728 | bytes 6291456 | tf_op jit(solution)/shard_map/states_own/pallas_call | solution.py:155
  7.9 1.0 %collective-permute-done.refs_1_ = f32[2,128,128]{2,1,0:T(8,128)S(1)} collective-permute-done((f32[2,128,128]{2,1,0:T(8,128)}, f32[2,128,128]{2,1,0:T(8,128)S(1)}, u32[]{:S(2)}, u32[]{:S(2)}) %collective-permute-start) | collective-permute-done | bytes 131104 | tf_op jit(solution)/shard_map/ppermute | solution.py:294
  8.9 0.5 %collective-permute-start.1 = (f32[2,128,128]{2,1,0:T(8,128)S(1)}, f32[2,128,128]{2,1,0:T(8,128)S(1)}, u32[]{:S(2)}, u32[]{:S(2)}) collective-permute-start(f32[2,128,128]{2,1,0:T(8,128)S(1)} %add.12), channel_id=1, source_target_pairs={{0,4},{2,6},{4,0},{6,2},{8,12},{10,14},{12,8},{14,10},{1,5},{3,7},... | collective-permute-start | bytes 393224 | tf_op jit(solution)/shard_map/ppermute | solution.py:294
  9.5 1.1 %collective-permute-done.5.refs_0_ = f32[2,128,128]{2,1,0:T(8,128)S(1)} collective-permute-done((f32[2,128,128]{2,1,0:T(8,128)}, f32[2,128,128]{2,1,0:T(8,128)S(1)}, u32[]{:S(2)}, u32[]{:S(2)}) %collective-permute-start.5) | collective-permute-done | bytes 131104 | tf_op jit(solution)/shard_map/ppermute | solution.py:294
  10.6 0.5 %collective-permute-start.6 = (f32[2,128,128]{2,1,0:T(8,128)S(1)}, f32[2,128,128]{2,1,0:T(8,128)S(1)}, u32[]{:S(2)}, u32[]{:S(2)}) collective-permute-start(f32[2,128,128]{2,1,0:T(8,128)S(1)} %add.14), channel_id=1, source_target_pairs={{0,4},{2,6},{4,0},{6,2},{8,12},{10,14},{12,8},{14,10},{1,5},{3,7},... | collective-permute-start | bytes 393224 | tf_op jit(solution)/shard_map/ppermute | solution.py:294
  11.1 1.5 %collective-permute-start.4 = (f32[4,128,128]{2,1,0:T(8,128)S(1)}, f32[4,128,128]{2,1,0:T(8,128)S(1)}, u32[]{:S(2)}, u32[]{:S(2)}) collective-permute-start(f32[4,128,128]{2,1,0:T(8,128)S(1)} %get-tuple-element.20), channel_id=1, source_target_pairs={{0,2},{2,0},{4,6},{6,4},{8,10},{10,8},{12,14},{14,12},{1,3},{3,1},... | collective-permute-start | bytes 786440 | tf_op jit(solution)/shard_map/ppermute | solution.py:294
  12.7 2.5 %shard_map.64.refs_2_ = f32[256,256]{1,0:T(8,128)S(1)} custom-call(f32[256,1024]{1,0:T(8,128)S(1)} %get-tuple-element.16.q_ref, f32[256,1024]{1,0:T(8,128)S(1)} %get-tuple-element.23.k_ref, f32[256,1024]{1,0:T(8,128)S(1)} %get-tuple-element.24.v_ref, f32[256,128]{1,0:T(8,128)S(1)} %get-tuple-element.17.weight_ref, f32[8,1024,128]{2,1,0:T(8,128)} %prefix_hbm.7), custom_call_target="tpu_custom_call" | custom-call | flops 805306368 | bytes 1048576 | tf_op jit(solution)/shard_map/pallas_call | solution.py:209
  15.2 0.0 collective-permute-done.1.refs_3_
  15.2 0.4 %collective-permute-start.2 = (f32[2,128,128]{2,1,0:T(8,128)S(1)}, f32[2,128,128]{2,1,0:T(8,128)S(1)}, u32[]{:S(2)}, u32[]{:S(2)}) collective-permute-start(f32[2,128,128]{2,1,0:T(8,128)S(1)} %add.13), channel_id=1, source_target_pairs={{0,8},{2,10},{4,12},{6,14},{8,0},{10,2},{12,4},{14,6},{1,9},{3,11}... | collective-permute-start | bytes 393224 | tf_op jit(solution)/shard_map/ppermute | solution.py:294
  15.6 0.8 %collective-permute-done.6.refs_2_ = f32[2,128,128]{2,1,0:T(8,128)S(1)} collective-permute-done((f32[2,128,128]{2,1,0:T(8,128)S(1)}, f32[2,128,128]{2,1,0:T(8,128)S(1)}, u32[]{:S(2)}, u32[]{:S(2)}) %collective-permute-start.6) | collective-permute-done | bytes 131104 | tf_op jit(solution)/shard_map/ppermute | solution.py:294
  16.5 4.5 %collective-permute-start.7 = (f32[4,128,128]{2,1,0:T(8,128)S(1)}, f32[4,128,128]{2,1,0:T(8,128)S(1)}, u32[]{:S(2)}, u32[]{:S(2)}) collective-permute-start(f32[4,128,128]{2,1,0:T(8,128)S(1)} %pad_maximum_fusion), channel_id=1, source_target_pairs={{4,6},{6,4},{12,14},{14,12},{5,7},{7,5},{13,15},{15,13},{20,22},{2... | collective-permute-start | bytes 786440 | tf_op jit(solution)/shard_map/ppermute | solution.py:294
  21.0 0.6 %collective-permute-start.8 = (f32[2,128,128]{2,1,0:T(8,128)S(1)}, f32[2,128,128]{2,1,0:T(8,128)S(1)}, u32[]{:S(2)}, u32[]{:S(2)}) collective-permute-start(f32[2,128,128]{2,1,0:T(8,128)S(1)} %add.15), channel_id=1, source_target_pairs={{0,8},{2,10},{4,12},{6,14},{8,0},{10,2},{12,4},{14,6},{1,9},{3,11}... | collective-permute-start | bytes 393224 | tf_op jit(solution)/shard_map/ppermute | solution.py:294
  21.6 2.5 %shard_map.65.refs_3_ = f32[256,256]{1,0:T(8,128)S(1)} custom-call(f32[256,1024]{1,0:T(8,128)S(1)} %get-tuple-element.16.q_ref, f32[256,1024]{1,0:T(8,128)S(1)} %get-tuple-element.23.k_ref, f32[256,1024]{1,0:T(8,128)S(1)} %get-tuple-element.24.v_ref, f32[256,128]{1,0:T(8,128)S(1)} %get-tuple-element.17.weight_ref, f32[8,1024,128]{2,1,0:T(8,128)} %prefix_hbm.7), custom_call_target="tpu_custom_call" | custom-call | flops 805306368 | bytes 1048576 | tf_op jit(solution)/shard_map/pallas_call | solution.py:209
  24.2 2.5 %shard_map.67.refs_6_ = f32[256,256]{1,0:T(8,128)S(1)} custom-call(f32[256,1024]{1,0:T(8,128)S(1)} %get-tuple-element.16.q_ref, f32[256,1024]{1,0:T(8,128)S(1)} %get-tuple-element.23.k_ref, f32[256,1024]{1,0:T(8,128)S(1)} %get-tuple-element.24.v_ref, f32[256,128]{1,0:T(8,128)S(1)} %get-tuple-element.17.weight_ref, f32[8,1024,128]{2,1,0:T(8,128)} %prefix_hbm.7), custom_call_target="tpu_custom_call" | custom-call | flops 805306368 | bytes 1048576 | tf_op jit(solution)/shard_map/pallas_call | solution.py:209
  26.7 0.0 collective-permute-done.2.refs_5_
  26.8 2.7 %collective-permute-start.3 = (f32[2,128,128]{2,1,0:T(8,128)S(1)}, f32[2,128,128]{2,1,0:T(8,128)S(1)}, u32[]{:S(2)}, u32[]{:S(2)}) collective-permute-start(f32[2,128,128]{2,1,0:T(8,128)S(1)} %collective-permute-done.2.refs_5_), channel_id=1, source_target_pairs={{8,10},{10,8},{12,14},{14,12},{9,11},{11,9},{13,15},{15,13},{24,26... | collective-permute-start | bytes 393224 | tf_op jit(solution)/shard_map/ppermute | solution.py:294
  29.5 0.0 collective-permute-done.8.refs_4_
  29.5 3.1 %collective-permute-start.9 = (f32[2,128,128]{2,1,0:T(8,128)S(1)}, f32[2,128,128]{2,1,0:T(8,128)S(1)}, u32[]{:S(2)}, u32[]{:S(2)}) collective-permute-start(f32[2,128,128]{2,1,0:T(8,128)S(1)} %collective-permute-done.8.refs_4_), channel_id=1, source_target_pairs={{8,10},{10,8},{12,14},{14,12},{9,11},{11,9},{13,15},{15,13},{24,26... | collective-permute-start | bytes 393224 | tf_op jit(solution)/shard_map/ppermute | solution.py:294
  32.6 2.6 %shard_map.68.refs_7_ = f32[256,256]{1,0:T(8,128)S(1)} custom-call(f32[256,1024]{1,0:T(8,128)S(1)} %get-tuple-element.16.q_ref, f32[256,1024]{1,0:T(8,128)S(1)} %get-tuple-element.23.k_ref, f32[256,1024]{1,0:T(8,128)S(1)} %get-tuple-element.24.v_ref, f32[256,128]{1,0:T(8,128)S(1)} %get-tuple-element.17.weight_ref, f32[8,1024,128]{2,1,0:T(8,128)} %prefix_hbm.7), custom_call_target="tpu_custom_call" | custom-call | flops 805306368 | bytes 1048576 | tf_op jit(solution)/shard_map/pallas_call | solution.py:209
  35.2 1.5 %shard_map.69.refs_2_ = f32[256,1024]{1,0:T(8,128)} custom-call(f32[256,1024]{1,0:T(8,128)S(1)} %get-tuple-element.16.q_ref, f32[256,128]{1,0:T(8,128)S(1)} %get-tuple-element.17.weight_ref, f32[2,128,128]{2,1,0:T(8,128)S(1)} %collective-permute-done.5.refs_0_, f32[2,128,128]{2,1,0:T(8,128)S(1)} %collective-permute-done.refs_1_, ...), custom_call_target="tpu_custom_call" | custom-call | flops 402653184 | bytes 1572864 | tf_op jit(solution)/shard_map/pallas_call | solution.py:273
  36.6 0.0 collective-permute-done.4.refs_0_
  36.7 0.0 collective-permute-done.7.refs_1_
  36.7 0.6 %shard_map.66 = (f32[256,256]{1,0:T(8,128)S(1)}, f32[256,256]{1,0:T(8,128)S(1)}) custom-call(f32[256,1024]{1,0:T(8,128)S(1)} %get-tuple-element.16.q_ref, f32[256,128]{1,0:T(8,128)S(1)} %get-tuple-element.17.weight_ref, f32[4,128,128]{2,1,0:T(8,128)S(1)} %collective-permute-done.4.refs_0_, f32[4,128,128]{2,1,0:T(8,128)S(1)} %collective-permute-done.7.refs_1_, ...), custom_call_target="tpu_custom_call" | custom-call | flops 268435456 | bytes 1572864 | tf_op jit(solution)/shard_map/pallas_call | solution.py:273
  37.2 0.0 collective-permute-done.9.refs_0_
  37.2 1.0 %shard_map.70.refs_2_ = f32[256,1024]{1,0:T(8,128)} custom-call(f32[256,1024]{1,0:T(8,128)S(1)} %get-tuple-element.16.q_ref, f32[256,128]{1,0:T(8,128)S(1)} %get-tuple-element.17.weight_ref, f32[2,128,128]{2,1,0:T(8,128)S(1)} %collective-permute-done.9.refs_0_, f32[256,256]{1,0:T(8,128)S(1)} %get-tuple-element.26.refs_1_, ...), custom_call_target="tpu_custom_call", output_to_operand_aliasing={{}: (4, {})} | custom-call | flops 67108864 | bytes 786432 | tf_op jit(solution)/shard_map/pallas_call | solution.py:273
  38.3 0.0 collective-permute-done.3.refs_0_
  38.3 1.0 %shard_map.71 = f32[256,1024]{1,0:T(8,128)} custom-call(f32[256,1024]{1,0:T(8,128)S(1)} %get-tuple-element.16.q_ref, f32[256,128]{1,0:T(8,128)S(1)} %get-tuple-element.17.weight_ref, f32[2,128,128]{2,1,0:T(8,128)S(1)} %collective-permute-done.3.refs_0_, f32[256,256]{1,0:T(8,128)S(1)} %get-tuple-element.25.refs_1_, ...), custom_call_target="tpu_custom_call", output_to_operand_aliasing={{}: (4, {})} | custom-call | flops 67108864 | bytes 786432 | tf_op jit(solution)/shard_map/pallas_call | solution.py:273
  (7 shorter events, 0.1 us)
Async XLA Ops:
  2.3 6.6 %collective-permute-start = (f32[2,128,128]{2,1,0:T(8,128)}, f32[2,128,128]{2,1,0:T(8,128)S(1)}, u32[]{:S(2)}, u32[]{:S(2)}) collective-permute-start(f32[2,128,128]{2,1,0:T(8,128)} %get-tuple-element.19), channel_id=1, source_target_pairs={{0,2},{2,0},{4,6},{6,4},{8,10},{10,8},{12,14},{14,12},{1,3},{3,1},... | collective-permute-start | bytes 393224 | tf_op jit(solution)/shard_map/ppermute | solution.py:294
  3.9 6.7 %collective-permute-start.5 = (f32[2,128,128]{2,1,0:T(8,128)}, f32[2,128,128]{2,1,0:T(8,128)S(1)}, u32[]{:S(2)}, u32[]{:S(2)}) collective-permute-start(f32[2,128,128]{2,1,0:T(8,128)} %get-tuple-element.22), channel_id=1, source_target_pairs={{0,2},{2,0},{4,6},{6,4},{8,10},{10,8},{12,14},{14,12},{1,3},{3,1},... | collective-permute-start | bytes 393224 | tf_op jit(solution)/shard_map/ppermute | solution.py:294
  4.4 0.8 %copy-start = (f32[8,8,256]{2,1,0:T(8,128)S(1)}, f32[8,8,256]{2,1,0:T(8,128)}, u32[]{:S(2)}) copy-start(f32[8,8,256]{2,1,0:T(8,128)} %bucket_ref.1) | copy-start | bytes 196612
  5.2 0.8 %copy-start.1 = (f32[8,6,256]{2,0,1:T(8,128)S(1)}, f32[8,6,256]{2,0,1:T(8,128)}, u32[]{:S(2)}) copy-start(f32[8,6,256]{2,0,1:T(8,128)} %param.9) | copy-start | bytes 147460
  8.9 6.3 %collective-permute-start.1 = (f32[2,128,128]{2,1,0:T(8,128)S(1)}, f32[2,128,128]{2,1,0:T(8,128)S(1)}, u32[]{:S(2)}, u32[]{:S(2)}) collective-permute-start(f32[2,128,128]{2,1,0:T(8,128)S(1)} %add.12), channel_id=1, source_target_pairs={{0,4},{2,6},{4,0},{6,2},{8,12},{10,14},{12,8},{14,10},{1,5},{3,7},... | collective-permute-start | bytes 393224 | tf_op jit(solution)/shard_map/ppermute | solution.py:294
  10.6 5.9 %collective-permute-start.6 = (f32[2,128,128]{2,1,0:T(8,128)S(1)}, f32[2,128,128]{2,1,0:T(8,128)S(1)}, u32[]{:S(2)}, u32[]{:S(2)}) collective-permute-start(f32[2,128,128]{2,1,0:T(8,128)S(1)} %add.14), channel_id=1, source_target_pairs={{0,4},{2,6},{4,0},{6,2},{8,12},{10,14},{12,8},{14,10},{1,5},{3,7},... | collective-permute-start | bytes 393224 | tf_op jit(solution)/shard_map/ppermute | solution.py:294
  11.1 25.5 %collective-permute-start.4 = (f32[4,128,128]{2,1,0:T(8,128)S(1)}, f32[4,128,128]{2,1,0:T(8,128)S(1)}, u32[]{:S(2)}, u32[]{:S(2)}) collective-permute-start(f32[4,128,128]{2,1,0:T(8,128)S(1)} %get-tuple-element.20), channel_id=1, source_target_pairs={{0,2},{2,0},{4,6},{6,4},{8,10},{10,8},{12,14},{14,12},{1,3},{3,1},... | collective-permute-start | bytes 786440 | tf_op jit(solution)/shard_map/ppermute | solution.py:294
  15.2 11.5 %collective-permute-start.2 = (f32[2,128,128]{2,1,0:T(8,128)S(1)}, f32[2,128,128]{2,1,0:T(8,128)S(1)}, u32[]{:S(2)}, u32[]{:S(2)}) collective-permute-start(f32[2,128,128]{2,1,0:T(8,128)S(1)} %add.13), channel_id=1, source_target_pairs={{0,8},{2,10},{4,12},{6,14},{8,0},{10,2},{12,4},{14,6},{1,9},{3,11}... | collective-permute-start | bytes 393224 | tf_op jit(solution)/shard_map/ppermute | solution.py:294
  16.5 20.2 %collective-permute-start.7 = (f32[4,128,128]{2,1,0:T(8,128)S(1)}, f32[4,128,128]{2,1,0:T(8,128)S(1)}, u32[]{:S(2)}, u32[]{:S(2)}) collective-permute-start(f32[4,128,128]{2,1,0:T(8,128)S(1)} %pad_maximum_fusion), channel_id=1, source_target_pairs={{4,6},{6,4},{12,14},{14,12},{5,7},{7,5},{13,15},{15,13},{20,22},{2... | collective-permute-start | bytes 786440 | tf_op jit(solution)/shard_map/ppermute | solution.py:294
  21.0 8.5 %collective-permute-start.8 = (f32[2,128,128]{2,1,0:T(8,128)S(1)}, f32[2,128,128]{2,1,0:T(8,128)S(1)}, u32[]{:S(2)}, u32[]{:S(2)}) collective-permute-start(f32[2,128,128]{2,1,0:T(8,128)S(1)} %add.15), channel_id=1, source_target_pairs={{0,8},{2,10},{4,12},{6,14},{8,0},{10,2},{12,4},{14,6},{1,9},{3,11}... | collective-permute-start | bytes 393224 | tf_op jit(solution)/shard_map/ppermute | solution.py:294
  26.8 11.5 %collective-permute-start.3 = (f32[2,128,128]{2,1,0:T(8,128)S(1)}, f32[2,128,128]{2,1,0:T(8,128)S(1)}, u32[]{:S(2)}, u32[]{:S(2)}) collective-permute-start(f32[2,128,128]{2,1,0:T(8,128)S(1)} %collective-permute-done.2.refs_5_), channel_id=1, source_target_pairs={{8,10},{10,8},{12,14},{14,12},{9,11},{11,9},{13,15},{15,13},{24,26... | collective-permute-start | bytes 393224 | tf_op jit(solution)/shard_map/ppermute | solution.py:294
  29.5 7.7 %collective-permute-start.9 = (f32[2,128,128]{2,1,0:T(8,128)S(1)}, f32[2,128,128]{2,1,0:T(8,128)S(1)}, u32[]{:S(2)}, u32[]{:S(2)}) collective-permute-start(f32[2,128,128]{2,1,0:T(8,128)S(1)} %collective-permute-done.8.refs_4_), channel_id=1, source_target_pairs={{8,10},{10,8},{12,14},{14,12},{9,11},{11,9},{13,15},{15,13},{24,26... | collective-permute-start | bytes 393224 | tf_op jit(solution)/shard_map/ppermute | solution.py:294

commit v3 on v2

--- a/solution.py
+++ b/solution.py
@@ -91,7 +91,7 @@
             pltpu.VMEM((PARTS, rows, width), F32),
             pltpu.SemaphoreType.DMA((2, PARTS)),
         ],
-        compiler_params=pltpu.CompilerParams(vmem_limit_bytes=GRANT - columns * DH * 5),
+        compiler_params=pltpu.CompilerParams(vmem_limit_bytes=GRANT - 107 * rows * columns * 4 // 10),
         cost_estimate=pl.CostEstimate(
             flops=4 * rows * columns * DH, bytes_accessed=4 * rows * columns, transcendentals=0
         ),
@@ -100,7 +100,8 @@
 
 
 def own_kernel(
-    level_ref, bucket_ref, q_hbm, k_hbm, v_hbm, q_out, k_out, v_out, weight_ref, whole_ref, *refs
+    levels, buckets, line_ref, q_hbm, k_hbm, v_hbm, prefix_hbm,
+    q_out, k_out, v_out, prefix_out, weight_ref, whole_ref, *refs,
 ):
     part_refs, sems = refs[:-1], refs[-1]
     per = part_refs[0].shape[0]
@@ -115,19 +116,22 @@
             )
             copy.start()
             copies.append(copy)
+    copies.append(pltpu.make_async_copy(prefix_hbm.at[first_head(0, per)], prefix_out, sems.at[3, 0]))
+    copies[-1].start()
     position = lax.axis_index("seq")
     own_second = lax.rem(position, 2) == 0
-    levels, heads, rows = level_ref.shape
-    buckets = bucket_ref.shape[1]
+    rows = line_ref.shape[1]
+    heads = q_hbm.shape[1] // DH
     lines = []
     for i in range(levels):
-        line = level_ref[i]
+        line = line_ref[i * heads : (i + 1) * heads]
         if i:
             line = line * lax.rem(lax.shift_right_logical(position, i - 1), 2).astype(F32)
         lines.append(jnp.where(own_second, jnp.concatenate([line[half:], line[:half]], axis=0), line))
-    first = jnp.where(own_second, half, 0)
-    for h in range(heads):
-        lines.append(bucket_ref[lax.rem(first + h, heads)])
+    first = line_ref[heads * levels : heads * levels + half * buckets]
+    second = line_ref[heads * levels + half * buckets :]
+    lines.append(jnp.where(own_second, second, first))
+    lines.append(jnp.where(own_second, first, second))
     spare = weight_ref.shape[1] - heads * (levels + buckets)
     if spare:
         lines.append(jnp.zeros((spare, rows), F32))
@@ -141,94 +145,102 @@
             state = outer_state(k_out[:, at], v_out[:, at])
             part_ref[j] = state
             whole_ref[c * per + j] = state
-    for i in (1, 3, 4, 5):
+    for i in (1, 3, 4, 5, 6):
         copies[i].wait()
 
 
-def own_block_states(queries, keys, values, level_weight, prefix_weight):
+def own_block_states(queries, keys, values, level_weight, prefix_weight, prefix_state):
     rows, columns = keys.shape
     heads = columns // DH
     per = heads // (2 * PARTS)
     weights = heads * (level_weight.shape[1] + prefix_weight.shape[1])
-    shapes = [queries.shape, keys.shape, values.shape, (rows, pl.cdiv(weights, DH) * DH)]
+    lines = jnp.concatenate(
+        [
+            jnp.transpose(level_weight, (1, 0, 2)).reshape(-1, rows),
+            prefix_weight.reshape(-1, rows),
+        ],
+        axis=0,
+    )
+    shapes = [queries.shape, keys.shape, values.shape, prefix_state.shape[1:]]
+    shapes += [(rows, pl.cdiv(weights, DH) * DH)]
     shapes += [(PARTS * per, DH, DH)] + [(per, DH, DH)] * PARTS
     return pl.pallas_call(
-        own_kernel,
+        functools.partial(own_kernel, level_weight.shape[1], prefix_weight.shape[1]),
         out_shape=[jax.ShapeDtypeStruct(s, F32) for s in shapes],
-        in_specs=[IN_VMEM] * 2 + [IN_HBM] * 3,
+        in_specs=[IN_VMEM] + [IN_HBM] * 4,
         out_specs=[IN_VMEM] * len(shapes),
-        scratch_shapes=[pltpu.SemaphoreType.DMA((3, 2))],
-        compiler_params=pltpu.CompilerParams(vmem_limit_bytes=GRANT - 14 * rows * columns * 4),
+        scratch_shapes=[pltpu.SemaphoreType.DMA((4, 2))],
+        compiler_params=pltpu.CompilerParams(vmem_limit_bytes=GRANT - 146 * rows * columns * 4 // 10),
         cost_estimate=pl.CostEstimate(
             flops=4 * rows * columns * DH, bytes_accessed=24 * rows * columns, transcendentals=0
         ),
         name="states_own",
-    )(jnp.transpose(level_weight, (1, 0, 2)), prefix_weight, queries, keys, values)
-
-
-def base_kernel(place, levels, buckets, q_ref, k_ref, v_ref, weight_ref, prefix_hbm, out_ref, buf, sems):
+    )(lines, queries, keys, values, prefix_state)
+
+
+def base_kernel(head, per, levels, buckets, q_ref, k_ref, v_ref, weight_ref, prefix_ref, *refs):
     rows = q_ref.shape[0]
-    heads = prefix_hbm.shape[0]
-    per = out_ref.shape[1] // DH
-    start = first_head(place, per)
-    copies = []
-    for j in range(per):
-        copies.append(pltpu.make_async_copy(prefix_hbm.at[start + j], buf.at[j], sems.at[j]))
-        copies[j].start()
+    heads = q_ref.shape[1] // DH
+    copy = None
+    if len(refs) > 1:
+        prefix_hbm, out_ref, next_ref, sem = refs
+        after = head + 1
+        place = first_head(after // per, per) + after % per
+        copy = pltpu.make_async_copy(prefix_hbm.at[place], next_ref, sem)
+        copy.start()
+    else:
+        (out_ref,) = refs
+    at = slice(head * DH, (head + 1) * DH)
+    q, k, v = q_ref[:, at], k_ref[:, at], v_ref[:, at]
     row = lax.broadcasted_iota(jnp.int32, (rows, rows), 0)
     column = lax.broadcasted_iota(jnp.int32, (rows, rows), 1)
     nt = (((1,), (1,)), ((), ()))
-    for j in range(per):
-        head = place * per + j
-        q, k, v = (ref[:, head * DH : (head + 1) * DH] for ref in (q_ref, k_ref, v_ref))
-        k_high, k_low = split(k)
-        q_wide = beside(q)
-        scores = lax.dot_general(
-            q_wide, jnp.concatenate([k_high, k_high], axis=1), nt, preferred_element_type=F32
-        ) + lax.dot_general(
-            q_wide, jnp.concatenate([k_low, k_low], axis=1), nt, preferred_element_type=F32
+    k_high, k_low = split(k)
+    q_wide = beside(q)
+    scores = lax.dot_general(
+        q_wide, jnp.concatenate([k_high, k_high], axis=1), nt, preferred_element_type=F32
+    ) + lax.dot_general(
+        q_wide, jnp.concatenate([k_low, k_low], axis=1), nt, preferred_element_type=F32
+    )
+    scores = jnp.where(column <= row, scores, 0.0) * weight_ref[:, head : head + 1]
+    scores_high, scores_low = split(scores)
+    v_wide = beside(v)
+    total = jnp.dot(scores_high, v_wide, preferred_element_type=F32)
+    total += jnp.dot(scores_low, v_wide, preferred_element_type=F32)
+    for b in range(buckets):
+        line = heads * levels + head * buckets + b
+        total += through_state(
+            q * weight_ref[:, line : line + 1], prefix_ref[b * DH : (b + 1) * DH, :]
         )
-        scores = jnp.where(column <= row, scores, 0.0) * weight_ref[:, head : head + 1]
-        scores_high, scores_low = split(scores)
-        v_wide = beside(v)
-        total = jnp.dot(scores_high, v_wide, preferred_element_type=F32)
-        total += jnp.dot(scores_low, v_wide, preferred_element_type=F32)
-        copies[j].wait()
-        for b in range(buckets):
-            at = heads * levels + head * buckets + b
-            total += through_state(
-                q * weight_ref[:, at : at + 1], buf[j, b * DH : (b + 1) * DH, :]
-            )
-        out_ref[:, j * DH : (j + 1) * DH] = fold_columns(total)
-
-
-def base_part(place, levels, buckets, loaded, prefix_state):
+    out_ref[...] = fold_columns(total)
+    if copy is not None:
+        copy.wait()
+
+
+def base_part(head, per, levels, buckets, loaded, prefix, prefix_state):
     rows, columns = loaded[0].shape
-    width = columns // (2 * PARTS)
-    per = width // DH
+    more = head + 1 < columns // DH
+    shapes = [(rows, DH)] + [prefix.shape] * more
     return pl.pallas_call(
-        functools.partial(base_kernel, place, levels, buckets),
-        out_shape=jax.ShapeDtypeStruct((rows, width), F32),
-        in_specs=[IN_VMEM] * len(loaded) + [IN_HBM],
-        out_specs=IN_VMEM,
-        scratch_shapes=[
-            pltpu.VMEM((per, *prefix_state.shape[1:]), F32),
-            pltpu.SemaphoreType.DMA((per,)),
-        ],
+        functools.partial(base_kernel, head, per, levels, buckets),
+        out_shape=[jax.ShapeDtypeStruct(s, F32) for s in shapes],
+        in_specs=[IN_VMEM] * (len(loaded) + 1) + [IN_HBM] * more,
+        out_specs=[IN_VMEM] * len(shapes),
+        scratch_shapes=[pltpu.SemaphoreType.DMA] * more,
         compiler_params=pltpu.CompilerParams(vmem_limit_bytes=GRANT - 16 * rows * columns * 4),
         cost_estimate=pl.CostEstimate(
-            flops=2 * width * rows * rows * 24,
-            bytes_accessed=16 * rows * width,
+            flops=2 * DH * rows * rows * 24,
+            bytes_accessed=20 * rows * DH,
             transcendentals=0,
         ),
-    )(*loaded, prefix_state)
-
-
-def levels_kernel(places, first, spread, store, q_ref, weight_ref, *refs):
+    )(*loaded, prefix, *[prefix_state] * more)
+
+
+def levels_kernel(places, first, spread, store, bases, q_ref, weight_ref, *refs):
     count = 1 + max(ref for rows in spread for ref, _ in rows)
     state_refs, refs = refs[:count], refs[count:]
-    base_refs, refs = refs[: len(places)], refs[len(places) :]
-    per = base_refs[0].shape[1] // DH
+    per = sum(ref.shape[1] for ref in refs[:bases]) // DH // len(places)
+    base_refs, refs = refs[:bases], refs[bases:]
     heads = q_ref.shape[1] // DH
     if store:
         out_hbm, buf, sems = refs[-3:]
@@ -244,7 +256,11 @@
                 ref, entry = rows[c]
                 term = through_state(q * weight_ref[:, column : column + 1], state_refs[ref][entry + j])
                 total = term if total is None else total + term
-            done = base_refs[c][:, at] + fold_columns(total)
+            if bases == len(places):
+                before = base_refs[c][:, at]
+            else:
+                before = base_refs[c * per + j][...]
+            done = before + fold_columns(total)
             if store:
                 buf[c, :, at] = done
             else:
@@ -271,7 +287,7 @@
         in_specs.append(IN_HBM)
     shape = (rows, columns) if store else (rows, width)
     return pl.pallas_call(
-        functools.partial(levels_kernel, places, first, spread, store),
+        functools.partial(levels_kernel, places, first, spread, store, len(bases)),
         out_shape=[jax.ShapeDtypeStruct(shape, F32)] * (1 if store else count),
         in_specs=in_specs,
         out_specs=[IN_HBM if store else IN_VMEM] * (1 if store else count),
@@ -301,16 +317,20 @@
 
     given = given_states(keys, values)
     received = [swapped(given[c], 0) for c in places]
-    *loaded, own, part0, part1 = own_block_states(
-        queries, keys, values, level_weight, prefix_weight
+    *loaded, prefix, weights, own, part0, part1 = own_block_states(
+        queries, keys, values, level_weight, prefix_weight, prefix_state
     )
     parts = (part0, part1)
-    query_places, weights = loaded[0], loaded[-1]
+    loaded.append(weights)
+    query_places = loaded[0]
     base = []
-    for place in range(2 * PARTS):
-        base.append(
-            base_part(place, level_weight.shape[1], prefix_weight.shape[1], loaded, prefix_state)
+    for head in range(2 * PARTS * per):
+        done, *following = base_part(
+            head, per, level_weight.shape[1], prefix_weight.shape[1], loaded, prefix, prefix_state
         )
+        base.append(done)
+        if following:
+            (prefix,) = following
 
     own_states = [list(received)]
     running = [parts[c] + received[c] for c in places]
@@ -321,17 +341,18 @@
     other_states = [[swapped(own, 0)]]
     for bit in range(1, levels - 1):
         both = jnp.concatenate(own_states[bit], axis=0)
-        other_states.append([swapped(both, 0, lambda i: i >> bit & 1)])
+        other_states.append([swapped(both, 0)])
     top = levels - 1
-    last = [swapped(own_states[top][c], 0, lambda i: i >> top & 1) for c in places]
+    needs = lambda i: i >> top & 1
+    last = [swapped(own_states[top][c], 0, needs if c == PARTS - 1 else lambda i: True) for c in places]
 
     spread = [[(i, c * per) for c in places] for i in range(levels - 1)]
     middle = add_levels(
-        query_places, weights, base[PARTS:], [x[0] for x in other_states], spread, (2, 3), 0, False, None
+        query_places, weights, base[PARTS * per :], [x[0] for x in other_states], spread, (2, 3), 0, False, None
     )
     flat = [x for level in own_states for x in level]
     spread = [[(i * PARTS + c, 0) for c in places] for i in range(levels)]
-    (out,) = add_levels(query_places, weights, base[:PARTS], flat, spread, (0, 1), 0, True, None)
+    (out,) = add_levels(query_places, weights, base[: PARTS * per], flat, spread, (0, 1), 0, True, None)
     for c in places:
         (out,) = add_levels(query_places, weights, [middle[c]], [last[c]], [[(0, 0)]], (PARTS + c,), top, True, out)
     return out

time: 39.7 us -> 38.3 us (0.965)
  the two profiles are of different devices: /device:TPU:24 before, /device:TPU:0 now
where the time goes in v3:
time: 38.3 us; the launch traced here: 37.8 us
  Pallas kernels  19.5 us (51%)
  starting transfers between devices  13.8 us (36%)
  waiting for transfers between devices  3.34 us (9%)
  other arithmetic  0.94 us (2%)
    ppermute x10, starting transfers between devices, swapped(): return lax.ppermute(array, 'seq', pairs)  13.8 us
    pallas_call x8, Pallas kernels, base_part(): pl.pallas_call(functools.partial(base_kernel, head, per, levels, buckets)...  11.8 us
    pallas_call x4, Pallas kernels, add_levels(): pl.pallas_call(functools.partial(levels_kernel, places, first, spread, st...  4.09 us
    ppermute x10, waiting for transfers between devices, swapped(): return lax.ppermute(array, 'seq', pairs)  3.34 us
    pallas_call x1, Pallas kernels, own_block_states(): pl.pallas_call(functools.partial(own_kernel, level_weight.shape[1], prefi...  2.08 us
    pallas_call x1, Pallas kernels, given_states(): pl.pallas_call(given_kernel, out_shape=[jax.ShapeDtypeStruct((width // DH...  1.62 us
    concatenate x1, other arithmetic, own_block_states(): jnp.concatenate([jnp.transpose(level_weight, (1, 0, 2)).reshape(-1, rows)...  0.85 us
  transfers between devices with their start and end apart: 10, of which 3 were waited for; matrix products, arithmetic and copies ran while one was open for 2% of the time, Pallas kernels for 45%

profile of v3, /device:TPU:0, one launch (start us, length us, event | category | flops | bytes accessed | tf_op | source)
XLA Modules:
  0.0 37.8 jit_solution(18427552585033334709)
XLA Ops:
  0.0 1.6 %states_given.1 = (f32[2,128,128]{2,1,0:T(8,128)S(1)}, f32[2,128,128]{2,1,0:T(8,128)S(1)}) custom-call(f32[256,1024]{1,0:T(8,128)} %k_hbm.3, f32[256,1024]{1,0:T(8,128)} %v_hbm.3), custom_call_target="tpu_custom_call" | custom-call | flops 134217728 | bytes 1048576 | tf_op jit(solution)/shard_map/states_given/pallas_call | solution.py:84
  1.6 3.1 %collective-permute-start.5 = (f32[2,128,128]{2,1,0:T(8,128)S(1)}, f32[2,128,128]{2,1,0:T(8,128)S(1)}, u32[]{:S(2)}, u32[]{:S(2)}) collective-permute-start(f32[2,128,128]{2,1,0:T(8,128)S(1)} %get-tuple-element.37), channel_id=1, source_target_pairs={{0,2},{2,0},{4,6},{6,4},{8,10},{10,8},{12,14},{14,12},{1,3},{3,1},... | collective-permute-start | bytes 393224 | tf_op jit(solution)/shard_map/ppermute | solution.py:310
  4.7 0.1 collective-permute-start
  4.8 0.8 %pad_maximum_fusion.1.line_ref = f32[112,256]{1,0:T(8,128)S(1)} fusion(f32[64,256]{1,0:T(8,128)} %bitcast.4, f32[48,256]{1,0:T(8,128)} %bitcast.5), kind=kLoop, calls=%fused_computation.1 | loop fusion | flops 28672 | bytes 229376 | tf_op jit(solution)/shard_map/concatenate | solution.py:157
  5.6 2.1 %states_own.1 = (f32[256,1024]{1,0:T(8,128)S(1)}, f32[256,1024]{1,0:T(8,128)S(1)}, f32[256,1024]{1,0:T(8,128)S(1)}, f32[1024,128]{1,0:T(8,128)S(1)}, f32[256,128...) custom-call(f32[112,256]{1,0:T(8,128)S(1)} %pad_maximum_fusion.1.line_ref, ...), custom_call_target="tpu_custom_call" | custom-call | flops 134217728 | bytes 6291456 | tf_op jit(solution)/shard_map/states_own/pallas_call | solution.py:167
  7.7 1.3 %collective-permute-done.5.refs_0_ = f32[2,128,128]{2,1,0:T(8,128)S(1)} collective-permute-done((f32[2,128,128]{2,1,0:T(8,128)S(1)}, f32[2,128,128]{2,1,0:T(8,128)S(1)}, u32[]{:S(2)}, u32[]{:S(2)}) %collective-permute-start.5) | collective-permute-done | bytes 131104 | tf_op jit(solution)/shard_map/ppermute | solution.py:310
  9.1 2.1 %collective-permute-start.6 = (f32[2,128,128]{2,1,0:T(8,128)S(1)}, f32[2,128,128]{2,1,0:T(8,128)S(1)}, u32[]{:S(2)}, u32[]{:S(2)}) collective-permute-start(f32[2,128,128]{2,1,0:T(8,128)S(1)} %add.14), channel_id=1, source_target_pairs={{0,4},{2,6},{4,0},{6,2},{8,12},{10,14},{12,8},{14,10},{1,5},{3,7},... | collective-permute-start | bytes 393224 | tf_op jit(solution)/shard_map/ppermute | solution.py:310
  11.2 0.0 collective-permute-done.refs_1_
  11.2 1.7 %collective-permute-start.1 = (f32[2,128,128]{2,1,0:T(8,128)S(1)}, f32[2,128,128]{2,1,0:T(8,128)S(1)}, u32[]{:S(2)}, u32[]{:S(2)}) collective-permute-start(f32[2,128,128]{2,1,0:T(8,128)S(1)} %add.12), channel_id=1, source_target_pairs={{0,4},{2,6},{4,0},{6,2},{8,12},{10,14},{12,8},{14,10},{1,5},{3,7},... | collective-permute-start | bytes 393224 | tf_op jit(solution)/shard_map/ppermute | solution.py:310
  12.9 1.5 %collective-permute-start.4 = (f32[4,128,128]{2,1,0:T(8,128)S(1)}, f32[4,128,128]{2,1,0:T(8,128)S(1)}, u32[]{:S(2)}, u32[]{:S(2)}) collective-permute-start(f32[4,128,128]{2,1,0:T(8,128)S(1)} %get-tuple-element.35), channel_id=1, source_target_pairs={{0,2},{2,0},{4,6},{6,4},{8,10},{10,8},{12,14},{14,12},{1,3},{3,1},... | collective-permute-start | bytes 786440 | tf_op jit(solution)/shard_map/ppermute | solution.py:310
  14.4 1.6 %shard_map.64 = (f32[256,128]{1,0:T(8,128)S(1)}, f32[1024,128]{1,0:T(8,128)S(1)}) custom-call(f32[256,1024]{1,0:T(8,128)S(1)} %get-tuple-element.31.q_ref, f32[256,1024]{1,0:T(8,128)S(1)} %get-tuple-element.38.k_ref, f32[256,1024]{1,0:T(8,128)S(1)} %get-tuple-element.39.v_ref, f32[256,128]{1,0:T(8,128)S(1)} %get-tuple-element.32.weight_ref, ...), custom_call_target="tpu_custom_call" | custom-call | flops 402653184 | bytes 655360 | tf_op jit(solution)/shard_map/pallas_call | solution.py:224
  16.0 1.6 %shard_map.65 = (f32[256,128]{1,0:T(8,128)S(1)}, f32[1024,128]{1,0:T(8,128)S(1)}) custom-call(f32[256,1024]{1,0:T(8,128)S(1)} %get-tuple-element.31.q_ref, f32[256,1024]{1,0:T(8,128)S(1)} %get-tuple-element.38.k_ref, f32[256,1024]{1,0:T(8,128)S(1)} %get-tuple-element.39.v_ref, f32[256,128]{1,0:T(8,128)S(1)} %get-tuple-element.32.weight_ref, ...), custom_call_target="tpu_custom_call" | custom-call | flops 402653184 | bytes 655360 | tf_op jit(solution)/shard_map/pallas_call | solution.py:224
  17.6 0.0 collective-permute-done.6.refs_2_
  17.6 2.7 %collective-permute-start.8 = (f32[2,128,128]{2,1,0:T(8,128)S(1)}, f32[2,128,128]{2,1,0:T(8,128)S(1)}, u32[]{:S(2)}, u32[]{:S(2)}) collective-permute-start(f32[2,128,128]{2,1,0:T(8,128)S(1)} %add.15), channel_id=1, source_target_pairs={{0,8},{2,10},{4,12},{6,14},{8,0},{10,2},{12,4},{14,6},{1,9},{3,11}... | collective-permute-start | bytes 393224 | tf_op jit(solution)/shard_map/ppermute | solution.py:310
  20.3 0.4 %collective-permute-start.2 = (f32[2,128,128]{2,1,0:T(8,128)S(1)}, f32[2,128,128]{2,1,0:T(8,128)S(1)}, u32[]{:S(2)}, u32[]{:S(2)}) collective-permute-start(f32[2,128,128]{2,1,0:T(8,128)S(1)} %add.13), channel_id=1, source_target_pairs={{0,8},{2,10},{4,12},{6,14},{8,0},{10,2},{12,4},{14,6},{1,9},{3,11}... | collective-permute-start | bytes 393224 | tf_op jit(solution)/shard_map/ppermute | solution.py:310
  20.7 1.2 %collective-permute-start.7 = (f32[4,128,128]{2,1,0:T(8,128)S(1)}, f32[4,128,128]{2,1,0:T(8,128)S(1)}, u32[]{:S(2)}, u32[]{:S(2)}) collective-permute-start(f32[4,128,128]{2,1,0:T(8,128)S(1)} %pad_maximum_fusion), channel_id=1, source_target_pairs={{0,2},{2,0},{4,6},{6,4},{8,10},{10,8},{12,14},{14,12},{1,3},{3,1},... | collective-permute-start | bytes 786440 | tf_op jit(solution)/shard_map/ppermute | solution.py:310
  21.9 1.6 %shard_map.66 = (f32[256,128]{1,0:T(8,128)S(1)}, f32[1024,128]{1,0:T(8,128)S(1)}) custom-call(f32[256,1024]{1,0:T(8,128)S(1)} %get-tuple-element.31.q_ref, f32[256,1024]{1,0:T(8,128)S(1)} %get-tuple-element.38.k_ref, f32[256,1024]{1,0:T(8,128)S(1)} %get-tuple-element.39.v_ref, f32[256,128]{1,0:T(8,128)S(1)} %get-tuple-element.32.weight_ref, ...), custom_call_target="tpu_custom_call" | custom-call | flops 402653184 | bytes 655360 | tf_op jit(solution)/shard_map/pallas_call | solution.py:224
  23.5 1.6 %shard_map.67 = (f32[256,128]{1,0:T(8,128)S(1)}, f32[1024,128]{1,0:T(8,128)S(1)}) custom-call(f32[256,1024]{1,0:T(8,128)S(1)} %get-tuple-element.31.q_ref, f32[256,1024]{1,0:T(8,128)S(1)} %get-tuple-element.38.k_ref, f32[256,1024]{1,0:T(8,128)S(1)} %get-tuple-element.39.v_ref, f32[256,128]{1,0:T(8,128)S(1)} %get-tuple-element.32.weight_ref, ...), custom_call_target="tpu_custom_call" | custom-call | flops 402653184 | bytes 655360 | tf_op jit(solution)/shard_map/pallas_call | solution.py:224
  25.1 1.6 %shard_map.68 = (f32[256,128]{1,0:T(8,128)S(1)}, f32[1024,128]{1,0:T(8,128)S(1)}) custom-call(f32[256,1024]{1,0:T(8,128)S(1)} %get-tuple-element.31.q_ref, f32[256,1024]{1,0:T(8,128)S(1)} %get-tuple-element.38.k_ref, f32[256,1024]{1,0:T(8,128)S(1)} %get-tuple-element.39.v_ref, f32[256,128]{1,0:T(8,128)S(1)} %get-tuple-element.32.weight_ref, ...), custom_call_target="tpu_custom_call" | custom-call | flops 402653184 | bytes 655360 | tf_op jit(solution)/shard_map/pallas_call | solution.py:224
  26.7 1.6 %shard_map.69 = (f32[256,128]{1,0:T(8,128)S(1)}, f32[1024,128]{1,0:T(8,128)S(1)}) custom-call(f32[256,1024]{1,0:T(8,128)S(1)} %get-tuple-element.31.q_ref, f32[256,1024]{1,0:T(8,128)S(1)} %get-tuple-element.38.k_ref, f32[256,1024]{1,0:T(8,128)S(1)} %get-tuple-element.39.v_ref, f32[256,128]{1,0:T(8,128)S(1)} %get-tuple-element.32.weight_ref, ...), custom_call_target="tpu_custom_call" | custom-call | flops 402653184 | bytes 655360 | tf_op jit(solution)/shard_map/pallas_call | solution.py:224
  28.3 0.7 %collective-permute-done.8.refs_4_ = f32[2,128,128]{2,1,0:T(8,128)S(1)} collective-permute-done((f32[2,128,128]{2,1,0:T(8,128)S(1)}, f32[2,128,128]{2,1,0:T(8,128)S(1)}, u32[]{:S(2)}, u32[]{:S(2)}) %collective-permute-start.8) | collective-permute-done | bytes 131104 | tf_op jit(solution)/shard_map/ppermute | solution.py:310
  29.0 0.4 %collective-permute-start.9 = (f32[2,128,128]{2,1,0:T(8,128)S(1)}, f32[2,128,128]{2,1,0:T(8,128)S(1)}, u32[]{:S(2)}, u32[]{:S(2)}) collective-permute-start(f32[2,128,128]{2,1,0:T(8,128)S(1)} %collective-permute-done.8.refs_4_), channel_id=1, source_target_pairs={{0,2},{2,0},{4,6},{6,4},{8,10},{10,8},{12,14},{14,12},{1,3},{3,1},... | collective-permute-start | bytes 393224 | tf_op jit(solution)/shard_map/ppermute | solution.py:310
  29.4 1.3 %collective-permute-done.2.refs_5_ = f32[2,128,128]{2,1,0:T(8,128)S(1)} collective-permute-done((f32[2,128,128]{2,1,0:T(8,128)S(1)}, f32[2,128,128]{2,1,0:T(8,128)S(1)}, u32[]{:S(2)}, u32[]{:S(2)}) %collective-permute-start.2) | collective-permute-done | bytes 131104 | tf_op jit(solution)/shard_map/ppermute | solution.py:310
  30.7 0.7 %collective-permute-start.3 = (f32[2,128,128]{2,1,0:T(8,128)S(1)}, f32[2,128,128]{2,1,0:T(8,128)S(1)}, u32[]{:S(2)}, u32[]{:S(2)}) collective-permute-start(f32[2,128,128]{2,1,0:T(8,128)S(1)} %collective-permute-done.2.refs_5_), channel_id=1, source_target_pairs={{8,10},{10,8},{12,14},{14,12},{9,11},{11,9},{13,15},{15,13},{24,26... | collective-permute-start | bytes 393224 | tf_op jit(solution)/shard_map/ppermute | solution.py:310
  31.4 1.6 %shard_map.70 = (f32[256,128]{1,0:T(8,128)S(1)}, f32[1024,128]{1,0:T(8,128)S(1)}) custom-call(f32[256,1024]{1,0:T(8,128)S(1)} %get-tuple-element.31.q_ref, f32[256,1024]{1,0:T(8,128)S(1)} %get-tuple-element.38.k_ref, f32[256,1024]{1,0:T(8,128)S(1)} %get-tuple-element.39.v_ref, f32[256,128]{1,0:T(8,128)S(1)} %get-tuple-element.32.weight_ref, ...), custom_call_target="tpu_custom_call" | custom-call | flops 402653184 | bytes 655360 | tf_op jit(solution)/shard_map/pallas_call | solution.py:224
  33.0 0.7 %shard_map.71.refs_5_ = f32[256,128]{1,0:T(8,128)S(1)} custom-call(f32[256,1024]{1,0:T(8,128)S(1)} %get-tuple-element.31.q_ref, f32[256,1024]{1,0:T(8,128)S(1)} %get-tuple-element.38.k_ref, f32[256,1024]{1,0:T(8,128)S(1)} %get-tuple-element.39.v_ref, f32[256,128]{1,0:T(8,128)S(1)} %get-tuple-element.32.weight_ref, f32[1024,128]{1,0:T(8,128)S(1)} %get-tuple-element.50.prefix_ref), custom_call_target="tpu_custom_call" | custom-call | flops 402653184 | bytes 655360 | tf_op jit(solution)/shard_map/pallas_call | solution.py:224
  33.6 1.5 %shard_map.73.refs_2_ = f32[256,1024]{1,0:T(8,128)} custom-call(f32[256,1024]{1,0:T(8,128)S(1)} %get-tuple-element.31.q_ref, f32[256,128]{1,0:T(8,128)S(1)} %get-tuple-element.32.weight_ref, f32[2,128,128]{2,1,0:T(8,128)S(1)} %collective-permute-done.5.refs_0_, f32[2,128,128]{2,1,0:T(8,128)S(1)} %collective-permute-done.refs_1_, ...), custom_call_target="tpu_custom_call" | custom-call | flops 402653184 | bytes 1572864 | tf_op jit(solution)/shard_map/pallas_call | solution.py:289
  35.1 0.0 collective-permute-done.4.refs_0_
  35.2 0.0 collective-permute-done.7.refs_1_
  35.2 0.6 %shard_map.72 = (f32[256,256]{1,0:T(8,128)S(1)}, f32[256,256]{1,0:T(8,128)S(1)}) custom-call(f32[256,1024]{1,0:T(8,128)S(1)} %get-tuple-element.31.q_ref, f32[256,128]{1,0:T(8,128)S(1)} %get-tuple-element.32.weight_ref, f32[4,128,128]{2,1,0:T(8,128)S(1)} %collective-permute-done.4.refs_0_, f32[4,128,128]{2,1,0:T(8,128)S(1)} %collective-permute-done.7.refs_1_, ...), custom_call_target="tpu_custom_call" | custom-call | flops 268435456 | bytes 1572864 | tf_op jit(solution)/shard_map/pallas_call | solution.py:289
  35.7 1.0 %shard_map.74.refs_2_ = f32[256,1024]{1,0:T(8,128)} custom-call(f32[256,1024]{1,0:T(8,128)S(1)} %get-tuple-element.31.q_ref, f32[256,128]{1,0:T(8,128)S(1)} %get-tuple-element.32.weight_ref, f32[2,128,128]{2,1,0:T(8,128)S(1)} %collective-permute-done.9.refs_0_, f32[256,256]{1,0:T(8,128)S(1)} %get-tuple-element.52.refs_1_, ...), custom_call_target="tpu_custom_call", output_to_operand_aliasing={{}: (4, {})} | custom-call | flops 67108864 | bytes 786432 | tf_op jit(solution)/shard_map/pallas_call | solution.py:289
  36.8 1.0 %shard_map.75 = f32[256,1024]{1,0:T(8,128)} custom-call(f32[256,1024]{1,0:T(8,128)S(1)} %get-tuple-element.31.q_ref, f32[256,128]{1,0:T(8,128)S(1)} %get-tuple-element.32.weight_ref, f32[2,128,128]{2,1,0:T(8,128)S(1)} %collective-permute-done.3.refs_0_, f32[256,256]{1,0:T(8,128)S(1)} %get-tuple-element.51.refs_1_, ...), custom_call_target="tpu_custom_call", output_to_operand_aliasing={{}: (4, {})} | custom-call | flops 67108864 | bytes 786432 | tf_op jit(solution)/shard_map/pallas_call | solution.py:289
  (8 shorter events, 0.1 us)
Async XLA Ops:
  1.6 7.4 %collective-permute-start.5 = (f32[2,128,128]{2,1,0:T(8,128)S(1)}, f32[2,128,128]{2,1,0:T(8,128)S(1)}, u32[]{:S(2)}, u32[]{:S(2)}) collective-permute-start(f32[2,128,128]{2,1,0:T(8,128)S(1)} %get-tuple-element.37), channel_id=1, source_target_pairs={{0,2},{2,0},{4,6},{6,4},{8,10},{10,8},{12,14},{14,12},{1,3},{3,1},... | collective-permute-start | bytes 393224 | tf_op jit(solution)/shard_map/ppermute | solution.py:310
  4.7 6.5 %collective-permute-start = (f32[2,128,128]{2,1,0:T(8,128)S(1)}, f32[2,128,128]{2,1,0:T(8,128)S(1)}, u32[]{:S(2)}, u32[]{:S(2)}) collective-permute-start(f32[2,128,128]{2,1,0:T(8,128)S(1)} %get-tuple-element.34), channel_id=1, source_target_pairs={{0,2},{2,0},{4,6},{6,4},{8,10},{10,8},{12,14},{14,12},{1,3},{3,1},... | collective-permute-start | bytes 393224 | tf_op jit(solution)/shard_map/ppermute | solution.py:310
  9.1 8.5 %collective-permute-start.6 = (f32[2,128,128]{2,1,0:T(8,128)S(1)}, f32[2,128,128]{2,1,0:T(8,128)S(1)}, u32[]{:S(2)}, u32[]{:S(2)}) collective-permute-start(f32[2,128,128]{2,1,0:T(8,128)S(1)} %add.14), channel_id=1, source_target_pairs={{0,4},{2,6},{4,0},{6,2},{8,12},{10,14},{12,8},{14,10},{1,5},{3,7},... | collective-permute-start | bytes 393224 | tf_op jit(solution)/shard_map/ppermute | solution.py:310
  11.2 9.1 %collective-permute-start.1 = (f32[2,128,128]{2,1,0:T(8,128)S(1)}, f32[2,128,128]{2,1,0:T(8,128)S(1)}, u32[]{:S(2)}, u32[]{:S(2)}) collective-permute-start(f32[2,128,128]{2,1,0:T(8,128)S(1)} %add.12), channel_id=1, source_target_pairs={{0,4},{2,6},{4,0},{6,2},{8,12},{10,14},{12,8},{14,10},{1,5},{3,7},... | collective-permute-start | bytes 393224 | tf_op jit(solution)/shard_map/ppermute | solution.py:310
  12.9 22.3 %collective-permute-start.4 = (f32[4,128,128]{2,1,0:T(8,128)S(1)}, f32[4,128,128]{2,1,0:T(8,128)S(1)}, u32[]{:S(2)}, u32[]{:S(2)}) collective-permute-start(f32[4,128,128]{2,1,0:T(8,128)S(1)} %get-tuple-element.35), channel_id=1, source_target_pairs={{0,2},{2,0},{4,6},{6,4},{8,10},{10,8},{12,14},{14,12},{1,3},{3,1},... | collective-permute-start | bytes 786440 | tf_op jit(solution)/shard_map/ppermute | solution.py:310
  17.6 11.4 %collective-permute-start.8 = (f32[2,128,128]{2,1,0:T(8,128)S(1)}, f32[2,128,128]{2,1,0:T(8,128)S(1)}, u32[]{:S(2)}, u32[]{:S(2)}) collective-permute-start(f32[2,128,128]{2,1,0:T(8,128)S(1)} %add.15), channel_id=1, source_target_pairs={{0,8},{2,10},{4,12},{6,14},{8,0},{10,2},{12,4},{14,6},{1,9},{3,11}... | collective-permute-start | bytes 393224 | tf_op jit(solution)/shard_map/ppermute | solution.py:310
  20.3 10.4 %collective-permute-start.2 = (f32[2,128,128]{2,1,0:T(8,128)S(1)}, f32[2,128,128]{2,1,0:T(8,128)S(1)}, u32[]{:S(2)}, u32[]{:S(2)}) collective-permute-start(f32[2,128,128]{2,1,0:T(8,128)S(1)} %add.13), channel_id=1, source_target_pairs={{0,8},{2,10},{4,12},{6,14},{8,0},{10,2},{12,4},{14,6},{1,9},{3,11}... | collective-permute-start | bytes 393224 | tf_op jit(solution)/shard_map/ppermute | solution.py:310
  20.7 14.4 %collective-permute-start.7 = (f32[4,128,128]{2,1,0:T(8,128)S(1)}, f32[4,128,128]{2,1,0:T(8,128)S(1)}, u32[]{:S(2)}, u32[]{:S(2)}) collective-permute-start(f32[4,128,128]{2,1,0:T(8,128)S(1)} %pad_maximum_fusion), channel_id=1, source_target_pairs={{0,2},{2,0},{4,6},{6,4},{8,10},{10,8},{12,14},{14,12},{1,3},{3,1},... | collective-permute-start | bytes 786440 | tf_op jit(solution)/shard_map/ppermute | solution.py:310
  29.0 6.7 %collective-permute-start.9 = (f32[2,128,128]{2,1,0:T(8,128)S(1)}, f32[2,128,128]{2,1,0:T(8,128)S(1)}, u32[]{:S(2)}, u32[]{:S(2)}) collective-permute-start(f32[2,128,128]{2,1,0:T(8,128)S(1)} %collective-permute-done.8.refs_4_), channel_id=1, source_target_pairs={{0,2},{2,0},{4,6},{6,4},{8,10},{10,8},{12,14},{14,12},{1,3},{3,1},... | collective-permute-start | bytes 393224 | tf_op jit(solution)/shard_map/ppermute | solution.py:310
  30.7 6.1 %collective-permute-start.3 = (f32[2,128,128]{2,1,0:T(8,128)S(1)}, f32[2,128,128]{2,1,0:T(8,128)S(1)}, u32[]{:S(2)}, u32[]{:S(2)}) collective-permute-start(f32[2,128,128]{2,1,0:T(8,128)S(1)} %collective-permute-done.2.refs_5_), channel_id=1, source_target_pairs={{8,10},{10,8},{12,14},{14,12},{9,11},{11,9},{13,15},{15,13},{24,26... | collective-permute-start | bytes 393224 | tf_op jit(solution)/shard_map/ppermute | solution.py:310

commit v4 on v3

--- a/solution.py
+++ b/solution.py
@@ -56,44 +56,38 @@
     return pl.ds(pl.multiple_of(head * DH, DH), count * DH)
 
 
-def given_kernel(k_hbm, v_hbm, *refs):
-    outs = refs[:PARTS]
-    k_buf, v_buf, sems = refs[PARTS:]
-    per = outs[0].shape[0]
-    copies = []
-    for c in range(PARTS):
-        columns = head_columns(first_head(PARTS + c, per), per)
-        pair = (
-            pltpu.make_async_copy(k_hbm.at[:, columns], k_buf.at[c], sems.at[0, c]),
-            pltpu.make_async_copy(v_hbm.at[:, columns], v_buf.at[c], sems.at[1, c]),
-        )
-        for copy in pair:
-            copy.start()
-        copies.append(pair)
-    for c in range(PARTS):
-        for copy in copies[c]:
-            copy.wait()
-        for j in range(per):
-            at = slice(j * DH, (j + 1) * DH)
-            outs[c][j] = outer_state(k_buf[c, :, at], v_buf[c, :, at])
+def given_kernel(place, k_hbm, v_hbm, out_ref, k_buf, v_buf, sems):
+    per = out_ref.shape[0]
+    columns = head_columns(first_head(place, per), per)
+    copies = (
+        pltpu.make_async_copy(k_hbm.at[:, columns], k_buf, sems.at[0]),
+        pltpu.make_async_copy(v_hbm.at[:, columns], v_buf, sems.at[1]),
+    )
+    for copy in copies:
+        copy.start()
+    for copy in copies:
+        copy.wait()
+    for j in range(per):
+        at = slice(j * DH, (j + 1) * DH)
+        out_ref[j] = outer_state(k_buf[:, at], v_buf[:, at])
 
 
 def given_states(keys, values):
     rows, columns = keys.shape
     width = columns // (2 * PARTS)
     return pl.pallas_call(
-        given_kernel,
-        out_shape=[jax.ShapeDtypeStruct((width // DH, DH, DH), F32)] * PARTS,
+        functools.partial(given_kernel, PARTS),
+        out_shape=jax.ShapeDtypeStruct((width // DH, DH, DH), F32),
         in_specs=[IN_HBM] * 2,
-        out_specs=[IN_VMEM] * PARTS,
+        out_specs=IN_VMEM,
         scratch_shapes=[
-            pltpu.VMEM((PARTS, rows, width), F32),
-            pltpu.VMEM((PARTS, rows, width), F32),
-            pltpu.SemaphoreType.DMA((2, PARTS)),
+            pltpu.VMEM((rows, width), F32),
+            pltpu.VMEM((rows, width), F32),
+            pltpu.SemaphoreType.DMA((2,)),
         ],
-        compiler_params=pltpu.CompilerParams(vmem_limit_bytes=GRANT - 107 * rows * columns * 4 // 10),
+        compiler_params=pltpu.CompilerParams(vmem_limit_bytes=GRANT - 105 * rows * columns * 4 // 10),
         cost_estimate=pl.CostEstimate(
-            flops=4 * rows * columns * DH, bytes_accessed=4 * rows * columns, transcendentals=0
+            flops=2 * rows * columns * DH, bytes_accessed=2 * rows * columns, transcendentals=0
         ),
         name="states_given",
     )(keys, values)
@@ -103,8 +97,8 @@
     levels, buckets, line_ref, q_hbm, k_hbm, v_hbm, prefix_hbm,
     q_out, k_out, v_out, prefix_out, weight_ref, whole_ref, *refs,
 ):
-    part_refs, sems = refs[:-1], refs[-1]
-    per = part_refs[0].shape[0]
+    (*part_refs, given_ref), sems = refs[:-1], refs[-1]
+    per = given_ref.shape[0]
     half = PARTS * per
     copies = []
     for i, (source, to) in enumerate(((k_hbm, k_out), (v_hbm, v_out), (q_hbm, q_out))):
@@ -116,7 +110,9 @@
             )
             copy.start()
             copies.append(copy)
-    copies.append(pltpu.make_async_copy(prefix_hbm.at[first_head(0, per)], prefix_out, sems.at[3, 0]))
+    copies.append(
+        pltpu.make_async_copy(prefix_hbm.at[pl.ds(first_head(0, per), per)], prefix_out, sems.at[3, 0])
+    )
     copies[-1].start()
     position = lax.axis_index("seq")
     own_second = lax.rem(position, 2) == 0
@@ -137,6 +133,12 @@
         lines.append(jnp.zeros((spare, rows), F32))
     weight_ref[...] = jnp.transpose(jnp.concatenate(lines, axis=0))
 
+    copies[1].wait()
+    copies[3].wait()
+    for j in range(per):
+        head = half + (PARTS - 1) * per + j
+        at = slice(head * DH, (head + 1) * DH)
+        given_ref[j] = outer_state(k_out[:, at], v_out[:, at])
     copies[0].wait()
     copies[2].wait()
     for c, part_ref in enumerate(part_refs):
@@ -145,7 +147,7 @@
             state = outer_state(k_out[:, at], v_out[:, at])
             part_ref[j] = state
             whole_ref[c * per + j] = state
-    for i in (1, 3, 4, 5, 6):
+    for i in (4, 5, 6):
         copies[i].wait()
 
 
@@ -161,16 +163,16 @@
         ],
         axis=0,
     )
-    shapes = [queries.shape, keys.shape, values.shape, prefix_state.shape[1:]]
+    shapes = [queries.shape, keys.shape, values.shape, (per, *prefix_state.shape[1:])]
     shapes += [(rows, pl.cdiv(weights, DH) * DH)]
-    shapes += [(PARTS * per, DH, DH)] + [(per, DH, DH)] * PARTS
+    shapes += [(PARTS * per, DH, DH)] + [(per, DH, DH)] * (PARTS + 1)
     return pl.pallas_call(
         functools.partial(own_kernel, level_weight.shape[1], prefix_weight.shape[1]),
         out_shape=[jax.ShapeDtypeStruct(s, F32) for s in shapes],
         in_specs=[IN_VMEM] + [IN_HBM] * 4,
         out_specs=[IN_VMEM] * len(shapes),
         scratch_shapes=[pltpu.SemaphoreType.DMA((4, 2))],
-        compiler_params=pltpu.CompilerParams(vmem_limit_bytes=GRANT - 146 * rows * columns * 4 // 10),
+        compiler_params=pltpu.CompilerParams(vmem_limit_bytes=GRANT - 153 * rows * columns * 4 // 10),
         cost_estimate=pl.CostEstimate(
             flops=4 * rows * columns * DH, bytes_accessed=24 * rows * columns, transcendentals=0
         ),
@@ -178,69 +180,72 @@
     )(lines, queries, keys, values, prefix_state)
 
 
-def base_kernel(head, per, levels, buckets, q_ref, k_ref, v_ref, weight_ref, prefix_ref, *refs):
+def base_kernel(place, levels, buckets, q_ref, k_ref, v_ref, weight_ref, prefix_ref, *refs):
     rows = q_ref.shape[0]
     heads = q_ref.shape[1] // DH
+    per = prefix_ref.shape[0]
     copy = None
     if len(refs) > 1:
         prefix_hbm, out_ref, next_ref, sem = refs
-        after = head + 1
-        place = first_head(after // per, per) + after % per
-        copy = pltpu.make_async_copy(prefix_hbm.at[place], next_ref, sem)
+        following = pl.ds(first_head(place + 1, per), per)
+        copy = pltpu.make_async_copy(prefix_hbm.at[following], next_ref, sem)
         copy.start()
     else:
         (out_ref,) = refs
-    at = slice(head * DH, (head + 1) * DH)
-    q, k, v = q_ref[:, at], k_ref[:, at], v_ref[:, at]
     row = lax.broadcasted_iota(jnp.int32, (rows, rows), 0)
     column = lax.broadcasted_iota(jnp.int32, (rows, rows), 1)
     nt = (((1,), (1,)), ((), ()))
-    k_high, k_low = split(k)
-    q_wide = beside(q)
-    scores = lax.dot_general(
-        q_wide, jnp.concatenate([k_high, k_high], axis=1), nt, preferred_element_type=F32
-    ) + lax.dot_general(
-        q_wide, jnp.concatenate([k_low, k_low], axis=1), nt, preferred_element_type=F32
-    )
-    scores = jnp.where(column <= row, scores, 0.0) * weight_ref[:, head : head + 1]
-    scores_high, scores_low = split(scores)
-    v_wide = beside(v)
-    total = jnp.dot(scores_high, v_wide, preferred_element_type=F32)
-    total += jnp.dot(scores_low, v_wide, preferred_element_type=F32)
-    for b in range(buckets):
-        line = heads * levels + head * buckets + b
-        total += through_state(
-            q * weight_ref[:, line : line + 1], prefix_ref[b * DH : (b + 1) * DH, :]
+    for j in range(per):
+        head = place * per + j
+        at = slice(head * DH, (head + 1) * DH)
+        q, k, v = q_ref[:, at], k_ref[:, at], v_ref[:, at]
+        k_high, k_low = split(k)
+        q_wide = beside(q)
+        scores = lax.dot_general(
+            q_wide, jnp.concatenate([k_high, k_high], axis=1), nt, preferred_element_type=F32
+        ) + lax.dot_general(
+            q_wide, jnp.concatenate([k_low, k_low], axis=1), nt, preferred_element_type=F32
         )
-    out_ref[...] = fold_columns(total)
+        scores = jnp.where(column <= row, scores, 0.0) * weight_ref[:, head : head + 1]
+        scores_high, scores_low = split(scores)
+        v_wide = beside(v)
+        total = jnp.dot(scores_high, v_wide, preferred_element_type=F32)
+        total += jnp.dot(scores_low, v_wide, preferred_element_type=F32)
+        for b in range(buckets):
+            line = heads * levels + head * buckets + b
+            total += through_state(
+                q * weight_ref[:, line : line + 1], prefix_ref[j, b * DH : (b + 1) * DH, :]
+            )
+        out_ref[:, j * DH : (j + 1) * DH] = fold_columns(total)
     if copy is not None:
         copy.wait()
 
 
-def base_part(head, per, levels, buckets, loaded, prefix, prefix_state):
+def base_part(place, levels, buckets, loaded, prefix, prefix_state):
     rows, columns = loaded[0].shape
-    more = head + 1 < columns // DH
-    shapes = [(rows, DH)] + [prefix.shape] * more
+    per = prefix.shape[0]
+    more = place + 1 < 2 * PARTS
+    shapes = [(rows, per * DH)] + [prefix.shape] * more
     return pl.pallas_call(
-        functools.partial(base_kernel, head, per, levels, buckets),
+        functools.partial(base_kernel, place, levels, buckets),
         out_shape=[jax.ShapeDtypeStruct(s, F32) for s in shapes],
         in_specs=[IN_VMEM] * (len(loaded) + 1) + [IN_HBM] * more,
         out_specs=[IN_VMEM] * len(shapes),
         scratch_shapes=[pltpu.SemaphoreType.DMA] * more,
-        compiler_params=pltpu.CompilerParams(vmem_limit_bytes=GRANT - 16 * rows * columns * 4),
+        compiler_params=pltpu.CompilerParams(vmem_limit_bytes=GRANT - 17 * rows * columns * 4),
         cost_estimate=pl.CostEstimate(
-            flops=2 * DH * rows * rows * 24,
-            bytes_accessed=20 * rows * DH,
+            flops=2 * per * DH * rows * rows * 24,
+            bytes_accessed=20 * rows * per * DH,
             transcendentals=0,
         ),
     )(*loaded, prefix, *[prefix_state] * more)
 
 
-def levels_kernel(places, first, spread, store, bases, q_ref, weight_ref, *refs):
+def levels_kernel(places, first, spread, store, q_ref, weight_ref, *refs):
     count = 1 + max(ref for rows in spread for ref, _ in rows)
     state_refs, refs = refs[:count], refs[count:]
-    per = sum(ref.shape[1] for ref in refs[:bases]) // DH // len(places)
-    base_refs, refs = refs[:bases], refs[bases:]
+    base_refs, refs = refs[: len(places)], refs[len(places) :]
+    per = base_refs[0].shape[1] // DH
     heads = q_ref.shape[1] // DH
     if store:
         out_hbm, buf, sems = refs[-3:]
@@ -256,11 +261,7 @@
                 ref, entry = rows[c]
                 term = through_state(q * weight_ref[:, column : column + 1], state_refs[ref][entry + j])
                 total = term if total is None else total + term
-            if bases == len(places):
-                before = base_refs[c][:, at]
-            else:
-                before = base_refs[c * per + j][...]
-            done = before + fold_columns(total)
+            done = base_refs[c][:, at] + fold_columns(total)
             if store:
                 buf[c, :, at] = done
             else:
@@ -287,7 +288,7 @@
         in_specs.append(IN_HBM)
     shape = (rows, columns) if store else (rows, width)
     return pl.pallas_call(
-        functools.partial(levels_kernel, places, first, spread, store, len(bases)),
+        functools.partial(levels_kernel, places, first, spread, store),
         out_shape=[jax.ShapeDtypeStruct(shape, F32)] * (1 if store else count),
         in_specs=in_specs,
         out_specs=[IN_HBM if store else IN_VMEM] * (1 if store else count),
@@ -315,19 +316,18 @@
     per = queries.shape[1] // DH // (2 * PARTS)
     places = range(PARTS)
 
-    given = given_states(keys, values)
+    given = [given_states(keys, values)]
+    *loaded, prefix, weights, own, part0, part1, rest = own_block_states(
+        queries, keys, values, level_weight, prefix_weight, prefix_state
+    )
+    given.append(rest)
     received = [swapped(given[c], 0) for c in places]
-    *loaded, prefix, weights, own, part0, part1 = own_block_states(
-        queries, keys, values, level_weight, prefix_weight, prefix_state
-    )
     parts = (part0, part1)
     loaded.append(weights)
     query_places = loaded[0]
     base = []
-    for head in range(2 * PARTS * per):
-        done, *following = base_part(
-            head, per, level_weight.shape[1], prefix_weight.shape[1], loaded, prefix, prefix_state
-        )
+    for place in range(2 * PARTS):
+        done, *following = base_part(place, level_weight.shape[1], prefix_weight.shape[1], loaded, prefix, prefix_state)
         base.append(done)
         if following:
             (prefix,) = following
@@ -348,11 +348,11 @@
 
     spread = [[(i, c * per) for c in places] for i in range(levels - 1)]
     middle = add_levels(
-        query_places, weights, base[PARTS * per :], [x[0] for x in other_states], spread, (2, 3), 0, False, None
+        query_places, weights, base[PARTS:], [x[0] for x in other_states], spread, (2, 3), 0, False, None
     )
     flat = [x for level in own_states for x in level]
     spread = [[(i * PARTS + c, 0) for c in places] for i in range(levels)]
-    (out,) = add_levels(query_places, weights, base[: PARTS * per], flat, spread, (0, 1), 0, True, None)
+    (out,) = add_levels(query_places, weights, base[:PARTS], flat, spread, (0, 1), 0, True, None)
     for c in places:
         (out,) = add_levels(query_places, weights, [middle[c]], [last[c]], [[(0, 0)]], (PARTS + c,), top, True, out)
     return out

time: 38.3 us -> 36 us (0.940)
  Pallas kernels: 19.5 us -> 15.4 us
  waiting for transfers between devices: 3.34 us -> 5.45 us
    pallas_call x9 -> x5, Pallas kernels: 13.4 us -> 9.08 us  [the longest x4 7.76 us: base_part(): pl.pallas_call(functools.partial(base_kernel, place, levels, buckets), ou...]
    ppermute x10, waiting for transfers between devices: 3.34 us -> 5.45 us  [swapped(): return lax.ppermute(array, 'seq', pairs)]
  transfers between devices with their start and end apart: 10 -> 10, of which waited for: 3 -> 4; matrix products, arithmetic and copies ran while one was open for 2% -> 3% of each run, Pallas kernels for 45% -> 37%
where the time goes in v4:
time: 36 us; the launch traced here: 35.5 us
  Pallas kernels  15.4 us (43%)
  starting transfers between devices  13.6 us (38%)
  waiting for transfers between devices  5.45 us (15%)
  other arithmetic  0.93 us (3%)
    ppermute x10, starting transfers between devices, swapped(): return lax.ppermute(array, 'seq', pairs)  13.6 us
    pallas_call x4, Pallas kernels, base_part(): pl.pallas_call(functools.partial(base_kernel, place, levels, buckets), ou...  7.76 us
    ppermute x10, waiting for transfers between devices, swapped(): return lax.ppermute(array, 'seq', pairs)  5.45 us
    pallas_call x4, Pallas kernels, add_levels(): pl.pallas_call(functools.partial(levels_kernel, places, first, spread, st...  4.06 us
    pallas_call x1, Pallas kernels, own_block_states(): pl.pallas_call(functools.partial(own_kernel, level_weight.shape[1], prefi...  2.27 us
    pallas_call x1, Pallas kernels, given_states(): pl.pallas_call(functools.partial(given_kernel, PARTS), out_shape=jax.Shap...  1.32 us
    concatenate x1, other arithmetic, own_block_states(): jnp.concatenate([jnp.transpose(level_weight, (1, 0, 2)).reshape(-1, rows)...  0.85 us
  transfers between devices with their start and end apart: 10, of which 4 were waited for; matrix products, arithmetic and copies ran while one was open for 3% of the time, Pallas kernels for 37%

profile of v4, /device:TPU:0, one launch (start us, length us, event | category | flops | bytes accessed | tf_op | source)
XLA Modules:
  0.0 35.5 jit_solution(11748541769597507394)
XLA Ops:
  0.0 1.3 %states_given.1 = f32[2,128,128]{2,1,0:T(8,128)S(1)} custom-call(f32[256,1024]{1,0:T(8,128)} %k_hbm.3, f32[256,1024]{1,0:T(8,128)} %v_hbm.3), custom_call_target="tpu_custom_call" | custom-call | flops 67108864 | bytes 524288 | tf_op jit(solution)/shard_map/states_given/pallas_call | solution.py:78
  1.3 3.1 %collective-permute-start.5 = (f32[2,128,128]{2,1,0:T(8,128)S(1)}, f32[2,128,128]{2,1,0:T(8,128)S(1)}, u32[]{:S(2)}, u32[]{:S(2)}) collective-permute-start(f32[2,128,128]{2,1,0:T(8,128)S(1)} %states_given.1), channel_id=1, source_target_pairs={{0,2},{2,0},{4,6},{6,4},{8,10},{10,8},{12,14},{14,12},{1,3},{3,1},... | collective-permute-start | bytes 393224 | tf_op jit(solution)/shard_map/ppermute | solution.py:311
  4.4 0.8 %pad_maximum_fusion.1.line_ref = f32[112,256]{1,0:T(8,128)S(1)} fusion(f32[64,256]{1,0:T(8,128)} %bitcast.4, f32[48,256]{1,0:T(8,128)} %bitcast.5), kind=kLoop, calls=%fused_computation.1 | loop fusion | flops 28672 | bytes 229376 | tf_op jit(solution)/shard_map/concatenate | solution.py:159
  5.2 2.3 %states_own.1 = (f32[256,1024]{1,0:T(8,128)S(1)}, f32[256,1024]{1,0:T(8,128)S(1)}, f32[256,1024]{1,0:T(8,128)S(1)}, f32[2,1024,128]{2,1,0:T(8,128)S(1)}, f32[256...) custom-call(f32[112,256]{1,0:T(8,128)S(1)} %pad_maximum_fusion.1.lin, ...), custom_call_target="tpu_custom_call" | custom-call | flops 134217728 | bytes 6291456 | tf_op jit(solution)/shard_map/states_own/pallas_call | solution.py:169
  7.5 0.1 collective-permute-start
  7.6 0.3 collective-permute-done.5.refs_0_
  7.9 1.9 %collective-permute-start.6 = (f32[2,128,128]{2,1,0:T(8,128)S(1)}, f32[2,128,128]{2,1,0:T(8,128)S(1)}, u32[]{:S(2)}, u32[]{:S(2)}) collective-permute-start(f32[2,128,128]{2,1,0:T(8,128)S(1)} %add.14), channel_id=1, source_target_pairs={{0,4},{2,6},{4,0},{6,2},{8,12},{10,14},{12,8},{14,10},{1,5},{3,7},... | collective-permute-start | bytes 393224 | tf_op jit(solution)/shard_map/ppermute | solution.py:311
  9.8 2.8 %collective-permute-done.refs_1_ = f32[2,128,128]{2,1,0:T(8,128)S(1)} collective-permute-done((f32[2,128,128]{2,1,0:T(8,128)S(1)}, f32[2,128,128]{2,1,0:T(8,128)S(1)}, u32[]{:S(2)}, u32[]{:S(2)}) %collective-permute-start) | collective-permute-done | bytes 131104 | tf_op jit(solution)/shard_map/ppermute | solution.py:311
  12.6 1.6 %collective-permute-start.1 = (f32[2,128,128]{2,1,0:T(8,128)S(1)}, f32[2,128,128]{2,1,0:T(8,128)S(1)}, u32[]{:S(2)}, u32[]{:S(2)}) collective-permute-start(f32[2,128,128]{2,1,0:T(8,128)S(1)} %add.12), channel_id=1, source_target_pairs={{0,4},{2,6},{4,0},{6,2},{8,12},{10,14},{12,8},{14,10},{1,5},{3,7},... | collective-permute-start | bytes 393224 | tf_op jit(solution)/shard_map/ppermute | solution.py:311
  14.2 0.5 %collective-permute-start.4 = (f32[4,128,128]{2,1,0:T(8,128)S(1)}, f32[4,128,128]{2,1,0:T(8,128)S(1)}, u32[]{:S(2)}, u32[]{:S(2)}) collective-permute-start(f32[4,128,128]{2,1,0:T(8,128)S(1)} %get-tuple-element.26), channel_id=1, source_target_pairs={{0,2},{2,0},{4,6},{6,4},{8,10},{10,8},{12,14},{14,12},{1,3},{3,1},... | collective-permute-start | bytes 786440 | tf_op jit(solution)/shard_map/ppermute | solution.py:311
  14.7 2.2 %shard_map.64 = (f32[256,256]{1,0:T(8,128)S(1)}, f32[2,1024,128]{2,1,0:T(8,128)S(1)}) custom-call(f32[256,1024]{1,0:T(8,128)S(1)} %get-tuple-element.22.q_ref, f32[256,1024]{1,0:T(8,128)S(1)} %get-tuple-element.28.k_ref, f32[256,1024]{1,0:T(8,128)S(1)} %get-tuple-element.29.v_ref, f32[256,128]{1,0:T(8,128)S(1)} %get-tuple-element.23.weight_ref, ...), custom_call_target="tpu_custom_call" | custom-call | flops 805306368 | bytes 1310720 | tf_op jit(solution)/shard_map/pallas_call | solution.py:229
  16.9 0.0 collective-permute-done.6.refs_2_
  17.0 2.7 %collective-permute-start.8 = (f32[2,128,128]{2,1,0:T(8,128)S(1)}, f32[2,128,128]{2,1,0:T(8,128)S(1)}, u32[]{:S(2)}, u32[]{:S(2)}) collective-permute-start(f32[2,128,128]{2,1,0:T(8,128)S(1)} %add.15), channel_id=1, source_target_pairs={{0,8},{2,10},{4,12},{6,14},{8,0},{10,2},{12,4},{14,6},{1,9},{3,11}... | collective-permute-start | bytes 393224 | tf_op jit(solution)/shard_map/ppermute | solution.py:311
  19.6 0.0 collective-permute-done.1.refs_3_
  19.7 1.6 %collective-permute-start.2 = (f32[2,128,128]{2,1,0:T(8,128)S(1)}, f32[2,128,128]{2,1,0:T(8,128)S(1)}, u32[]{:S(2)}, u32[]{:S(2)}) collective-permute-start(f32[2,128,128]{2,1,0:T(8,128)S(1)} %add.13), channel_id=1, source_target_pairs={{0,8},{2,10},{4,12},{6,14},{8,0},{10,2},{12,4},{14,6},{1,9},{3,11}... | collective-permute-start | bytes 393224 | tf_op jit(solution)/shard_map/ppermute | solution.py:311
  21.3 0.4 %collective-permute-start.7 = (f32[4,128,128]{2,1,0:T(8,128)S(1)}, f32[4,128,128]{2,1,0:T(8,128)S(1)}, u32[]{:S(2)}, u32[]{:S(2)}) collective-permute-start(f32[4,128,128]{2,1,0:T(8,128)S(1)} %pad_maximum_fusion), channel_id=1, source_target_pairs={{0,2},{2,0},{4,6},{6,4},{8,10},{10,8},{12,14},{14,12},{1,3},{3,1},... | collective-permute-start | bytes 786440 | tf_op jit(solution)/shard_map/ppermute | solution.py:311
  21.7 2.2 %shard_map.65 = (f32[256,256]{1,0:T(8,128)S(1)}, f32[2,1024,128]{2,1,0:T(8,128)S(1)}) custom-call(f32[256,1024]{1,0:T(8,128)S(1)} %get-tuple-element.22.q_ref, f32[256,1024]{1,0:T(8,128)S(1)} %get-tuple-element.28.k_ref, f32[256,1024]{1,0:T(8,128)S(1)} %get-tuple-element.29.v_ref, f32[256,128]{1,0:T(8,128)S(1)} %get-tuple-element.23.weight_ref, ...), custom_call_target="tpu_custom_call" | custom-call | flops 805306368 | bytes 1310720 | tf_op jit(solution)/shard_map/pallas_call | solution.py:229
  23.9 2.2 %shard_map.66 = (f32[256,256]{1,0:T(8,128)S(1)}, f32[2,1024,128]{2,1,0:T(8,128)S(1)}) custom-call(f32[256,1024]{1,0:T(8,128)S(1)} %get-tuple-element.22.q_ref, f32[256,1024]{1,0:T(8,128)S(1)} %get-tuple-element.28.k_ref, f32[256,1024]{1,0:T(8,128)S(1)} %get-tuple-element.29.v_ref, f32[256,128]{1,0:T(8,128)S(1)} %get-tuple-element.23.weight_ref, ...), custom_call_target="tpu_custom_call" | custom-call | flops 805306368 | bytes 1310720 | tf_op jit(solution)/shard_map/pallas_call | solution.py:229
  26.1 2.0 %collective-permute-done.8.refs_4_ = f32[2,128,128]{2,1,0:T(8,128)S(1)} collective-permute-done((f32[2,128,128]{2,1,0:T(8,128)S(1)}, f32[2,128,128]{2,1,0:T(8,128)S(1)}, u32[]{:S(2)}, u32[]{:S(2)}) %collective-permute-start.8) | collective-permute-done | bytes 131104 | tf_op jit(solution)/shard_map/ppermute | solution.py:311
  28.2 1.1 %collective-permute-start.9 = (f32[2,128,128]{2,1,0:T(8,128)S(1)}, f32[2,128,128]{2,1,0:T(8,128)S(1)}, u32[]{:S(2)}, u32[]{:S(2)}) collective-permute-start(f32[2,128,128]{2,1,0:T(8,128)S(1)} %collective-permute-done.8.refs_4_), channel_id=1, source_target_pairs={{0,2},{2,0},{4,6},{6,4},{8,10},{10,8},{12,14},{14,12},{1,3},{3,1},... | collective-permute-start | bytes 393224 | tf_op jit(solution)/shard_map/ppermute | solution.py:311
  29.3 0.3 collective-permute-done.2.refs_5_
  29.6 0.7 %collective-permute-start.3 = (f32[2,128,128]{2,1,0:T(8,128)S(1)}, f32[2,128,128]{2,1,0:T(8,128)S(1)}, u32[]{:S(2)}, u32[]{:S(2)}) collective-permute-start(f32[2,128,128]{2,1,0:T(8,128)S(1)} %collective-permute-done.2.refs_5_), channel_id=1, source_target_pairs={{8,10},{10,8},{12,14},{14,12},{9,11},{11,9},{13,15},{15,13},{24,26... | collective-permute-start | bytes 393224 | tf_op jit(solution)/shard_map/ppermute | solution.py:311
  30.3 1.1 %shard_map.67.refs_3_ = f32[256,256]{1,0:T(8,128)S(1)} custom-call(f32[256,1024]{1,0:T(8,128)S(1)} %get-tuple-element.22.q_ref, f32[256,1024]{1,0:T(8,128)S(1)} %get-tuple-element.28.k_ref, f32[256,1024]{1,0:T(8,128)S(1)} %get-tuple-element.29.v_ref, f32[256,128]{1,0:T(8,128)S(1)} %get-tuple-element.23.weight_ref, ...), custom_call_target="tpu_custom_call" | custom-call | flops 805306368 | bytes 1310720 | tf_op jit(solution)/shard_map/pallas_call | solution.py:229
  31.4 1.5 %shard_map.69.refs_2_ = f32[256,1024]{1,0:T(8,128)} custom-call(f32[256,1024]{1,0:T(8,128)S(1)} %get-tuple-element.22.q_ref, f32[256,128]{1,0:T(8,128)S(1)} %get-tuple-element.23.weight_ref, f32[2,128,128]{2,1,0:T(8,128)S(1)} %collective-permute-done.5.refs_0_, f32[2,128,128]{2,1,0:T(8,128)S(1)} %collective-permute-done.refs_1_, ...), custom_call_target="tpu_custom_call" | custom-call | flops 402653184 | bytes 1572864 | tf_op jit(solution)/shard_map/pallas_call | solution.py:290
  32.9 0.0 collective-permute-done.4.refs_0_
  32.9 0.0 collective-permute-done.7.refs_1_
  32.9 0.6 %shard_map.68 = (f32[256,256]{1,0:T(8,128)S(1)}, f32[256,256]{1,0:T(8,128)S(1)}) custom-call(f32[256,1024]{1,0:T(8,128)S(1)} %get-tuple-element.22.q_ref, f32[256,128]{1,0:T(8,128)S(1)} %get-tuple-element.23.weight_ref, f32[4,128,128]{2,1,0:T(8,128)S(1)} %collective-permute-done.4.refs_0_, f32[4,128,128]{2,1,0:T(8,128)S(1)} %collective-permute-done.7.refs_1_, ...), custom_call_target="tpu_custom_call" | custom-call | flops 268435456 | bytes 1572864 | tf_op jit(solution)/shard_map/pallas_call | solution.py:290
  33.5 0.0 collective-permute-done.9.refs_0_
  33.5 1.0 %shard_map.70.refs_2_ = f32[256,1024]{1,0:T(8,128)} custom-call(f32[256,1024]{1,0:T(8,128)S(1)} %get-tuple-element.22.q_ref, f32[256,128]{1,0:T(8,128)S(1)} %get-tuple-element.23.weight_ref, f32[2,128,128]{2,1,0:T(8,128)S(1)} %collective-permute-done.9.refs_0_, f32[256,256]{1,0:T(8,128)S(1)} %get-tuple-element.36.refs_1_, ...), custom_call_target="tpu_custom_call", output_to_operand_aliasing={{}: (4, {})} | custom-call | flops 67108864 | bytes 786432 | tf_op jit(solution)/shard_map/pallas_call | solution.py:290
  34.5 0.0 collective-permute-done.3.refs_0_
  34.5 1.0 %shard_map.71 = f32[256,1024]{1,0:T(8,128)} custom-call(f32[256,1024]{1,0:T(8,128)S(1)} %get-tuple-element.22.q_ref, f32[256,128]{1,0:T(8,128)S(1)} %get-tuple-element.23.weight_ref, f32[2,128,128]{2,1,0:T(8,128)S(1)} %collective-permute-done.3.refs_0_, f32[256,256]{1,0:T(8,128)S(1)} %get-tuple-element.35.refs_1_, ...), custom_call_target="tpu_custom_call", output_to_operand_aliasing={{}: (4, {})} | custom-call | flops 67108864 | bytes 786432 | tf_op jit(solution)/shard_map/pallas_call | solution.py:290
  (5 shorter events, 0.1 us)
Async XLA Ops:
  1.3 6.6 %collective-permute-start.5 = (f32[2,128,128]{2,1,0:T(8,128)S(1)}, f32[2,128,128]{2,1,0:T(8,128)S(1)}, u32[]{:S(2)}, u32[]{:S(2)}) collective-permute-start(f32[2,128,128]{2,1,0:T(8,128)S(1)} %states_given.1), channel_id=1, source_target_pairs={{0,2},{2,0},{4,6},{6,4},{8,10},{10,8},{12,14},{14,12},{1,3},{3,1},... | collective-permute-start | bytes 393224 | tf_op jit(solution)/shard_map/ppermute | solution.py:311
  7.5 5.0 %collective-permute-start = (f32[2,128,128]{2,1,0:T(8,128)S(1)}, f32[2,128,128]{2,1,0:T(8,128)S(1)}, u32[]{:S(2)}, u32[]{:S(2)}) collective-permute-start(f32[2,128,128]{2,1,0:T(8,128)S(1)} %get-tuple-element.25), channel_id=1, source_target_pairs={{0,2},{2,0},{4,6},{6,4},{8,10},{10,8},{12,14},{14,12},{1,3},{3,1},... | collective-permute-start | bytes 393224 | tf_op jit(solution)/shard_map/ppermute | solution.py:311
  7.9 9.0 %collective-permute-start.6 = (f32[2,128,128]{2,1,0:T(8,128)S(1)}, f32[2,128,128]{2,1,0:T(8,128)S(1)}, u32[]{:S(2)}, u32[]{:S(2)}) collective-permute-start(f32[2,128,128]{2,1,0:T(8,128)S(1)} %add.14), channel_id=1, source_target_pairs={{0,4},{2,6},{4,0},{6,2},{8,12},{10,14},{12,8},{14,10},{1,5},{3,7},... | collective-permute-start | bytes 393224 | tf_op jit(solution)/shard_map/ppermute | solution.py:311
  12.6 7.1 %collective-permute-start.1 = (f32[2,128,128]{2,1,0:T(8,128)S(1)}, f32[2,128,128]{2,1,0:T(8,128)S(1)}, u32[]{:S(2)}, u32[]{:S(2)}) collective-permute-start(f32[2,128,128]{2,1,0:T(8,128)S(1)} %add.12), channel_id=1, source_target_pairs={{0,4},{2,6},{4,0},{6,2},{8,12},{10,14},{12,8},{14,10},{1,5},{3,7},... | collective-permute-start | bytes 393224 | tf_op jit(solution)/shard_map/ppermute | solution.py:311
  14.2 18.7 %collective-permute-start.4 = (f32[4,128,128]{2,1,0:T(8,128)S(1)}, f32[4,128,128]{2,1,0:T(8,128)S(1)}, u32[]{:S(2)}, u32[]{:S(2)}) collective-permute-start(f32[4,128,128]{2,1,0:T(8,128)S(1)} %get-tuple-element.26), channel_id=1, source_target_pairs={{0,2},{2,0},{4,6},{6,4},{8,10},{10,8},{12,14},{14,12},{1,3},{3,1},... | collective-permute-start | bytes 786440 | tf_op jit(solution)/shard_map/ppermute | solution.py:311
  17.0 11.2 %collective-permute-start.8 = (f32[2,128,128]{2,1,0:T(8,128)S(1)}, f32[2,128,128]{2,1,0:T(8,128)S(1)}, u32[]{:S(2)}, u32[]{:S(2)}) collective-permute-start(f32[2,128,128]{2,1,0:T(8,128)S(1)} %add.15), channel_id=1, source_target_pairs={{0,8},{2,10},{4,12},{6,14},{8,0},{10,2},{12,4},{14,6},{1,9},{3,11}... | collective-permute-start | bytes 393224 | tf_op jit(solution)/shard_map/ppermute | solution.py:311
  19.7 10.0 %collective-permute-start.2 = (f32[2,128,128]{2,1,0:T(8,128)S(1)}, f32[2,128,128]{2,1,0:T(8,128)S(1)}, u32[]{:S(2)}, u32[]{:S(2)}) collective-permute-start(f32[2,128,128]{2,1,0:T(8,128)S(1)} %add.13), channel_id=1, source_target_pairs={{0,8},{2,10},{4,12},{6,14},{8,0},{10,2},{12,4},{14,6},{1,9},{3,11}... | collective-permute-start | bytes 393224 | tf_op jit(solution)/shard_map/ppermute | solution.py:311
  21.3 11.6 %collective-permute-start.7 = (f32[4,128,128]{2,1,0:T(8,128)S(1)}, f32[4,128,128]{2,1,0:T(8,128)S(1)}, u32[]{:S(2)}, u32[]{:S(2)}) collective-permute-start(f32[4,128,128]{2,1,0:T(8,128)S(1)} %pad_maximum_fusion), channel_id=1, source_target_pairs={{0,2},{2,0},{4,6},{6,4},{8,10},{10,8},{12,14},{14,12},{1,3},{3,1},... | collective-permute-start | bytes 786440 | tf_op jit(solution)/shard_map/ppermute | solution.py:311
  28.2 5.3 %collective-permute-start.9 = (f32[2,128,128]{2,1,0:T(8,128)S(1)}, f32[2,128,128]{2,1,0:T(8,128)S(1)}, u32[]{:S(2)}, u32[]{:S(2)}) collective-permute-start(f32[2,128,128]{2,1,0:T(8,128)S(1)} %collective-permute-done.8.refs_4_), channel_id=1, source_target_pairs={{0,2},{2,0},{4,6},{6,4},{8,10},{10,8},{12,14},{14,12},{1,3},{3,1},... | collective-permute-start | bytes 393224 | tf_op jit(solution)/shard_map/ppermute | solution.py:311
  29.6 4.9 %collective-permute-start.3 = (f32[2,128,128]{2,1,0:T(8,128)S(1)}, f32[2,128,128]{2,1,0:T(8,128)S(1)}, u32[]{:S(2)}, u32[]{:S(2)}) collective-permute-start(f32[2,128,128]{2,1,0:T(8,128)S(1)} %collective-permute-done.2.refs_5_), channel_id=1, source_target_pairs={{8,10},{10,8},{12,14},{14,12},{9,11},{11,9},{13,15},{15,13},{24,26... | collective-permute-start | bytes 393224 | tf_op jit(solution)/shard_map/ppermute | solution.py:311

commit v5 on v4

--- a/solution.py
+++ b/solution.py
@@ -241,9 +241,8 @@
     )(*loaded, prefix, *[prefix_state] * more)
 
 
-def levels_kernel(places, first, spread, store, q_ref, weight_ref, *refs):
-    count = 1 + max(ref for rows in spread for ref, _ in rows)
-    state_refs, refs = refs[:count], refs[count:]
+def levels_kernel(places, terms, states, store, q_ref, weight_ref, *refs):
+    state_refs, refs = refs[:states], refs[states:]
     base_refs, refs = refs[: len(places)], refs[len(places) :]
     per = base_refs[0].shape[1] // DH
     heads = q_ref.shape[1] // DH
@@ -256,12 +255,13 @@
             head = place * per + j
             q = q_ref[:, head * DH : (head + 1) * DH]
             total = None
-            for i, rows in enumerate(spread):
-                column = (1 + first + i) * heads + head
-                ref, entry = rows[c]
+            for level, ref, entry in terms[c]:
+                column = level * heads + head
                 term = through_state(q * weight_ref[:, column : column + 1], state_refs[ref][entry + j])
                 total = term if total is None else total + term
-            done = base_refs[c][:, at] + fold_columns(total)
+            done = base_refs[c][:, at]
+            if total is not None:
+                done += fold_columns(total)
             if store:
                 buf[c, :, at] = done
             else:
@@ -275,7 +275,7 @@
         copy.wait()
 
 
-def add_levels(queries, weights, bases, states, spread, places, first, store, out):
+def add_levels(queries, weights, bases, states, terms, places, store, out):
     rows, columns = queries.shape
     width = columns // (2 * PARTS)
     count = len(places)
@@ -288,7 +288,7 @@
         in_specs.append(IN_HBM)
     shape = (rows, columns) if store else (rows, width)
     return pl.pallas_call(
-        functools.partial(levels_kernel, places, first, spread, store),
+        functools.partial(levels_kernel, places, terms, len(states), store),
         out_shape=[jax.ShapeDtypeStruct(shape, F32)] * (1 if store else count),
         in_specs=in_specs,
         out_specs=[IN_HBM if store else IN_VMEM] * (1 if store else count),
@@ -298,16 +298,16 @@
         input_output_aliases=aliases,
         compiler_params=pltpu.CompilerParams(vmem_limit_bytes=GRANT // 4),
         cost_estimate=pl.CostEstimate(
-            flops=4 * count * width * rows * rows * len(spread),
+            flops=4 * width * rows * rows * sum(len(t) for t in terms),
             bytes_accessed=12 * rows * width * count,
             transcendentals=0,
         ),
     )(*operands)
 
 
-def swapped(array, bit, keep=lambda i: True):
+def swapped(array, bit, keep=lambda i: True, alt=None):
     size = lax.axis_size("seq")
-    pairs = [(i, i ^ 1 << bit) for i in range(size) if keep(i)]
+    pairs = [(i, i ^ (1 << bit if alt is None or i >> alt & 1 else 2)) for i in range(size) if keep(i)]
     return lax.ppermute(array, "seq", pairs)
 
 
@@ -344,17 +344,19 @@
         other_states.append([swapped(both, 0)])
     top = levels - 1
     needs = lambda i: i >> top & 1
-    last = [swapped(own_states[top][c], 0, needs if c == PARTS - 1 else lambda i: True) for c in places]
-
-    spread = [[(i, c * per) for c in places] for i in range(levels - 1)]
-    middle = add_levels(
-        query_places, weights, base[PARTS:], [x[0] for x in other_states], spread, (2, 3), 0, False, None
-    )
+    last = [swapped(own_states[top][c], 0, needs if c == PARTS - 1 else lambda i: True, top) for c in places]
+
     flat = [x for level in own_states for x in level]
-    spread = [[(i * PARTS + c, 0) for c in places] for i in range(levels)]
-    (out,) = add_levels(query_places, weights, base[:PARTS], flat, spread, (0, 1), 0, True, None)
-    for c in places:
-        (out,) = add_levels(query_places, weights, [middle[c]], [last[c]], [[(0, 0)]], (PARTS + c,), top, True, out)
+    terms = [[(1 + i, i * PARTS + c, 0) for i in range(levels)] for c in places]
+    (out,) = add_levels(query_places, weights, base[:PARTS], flat, terms, tuple(places), True, None)
+    flat = [x[0] for x in other_states] + last[:-1]
+    terms = [[(1 + i, i, c * per) for i in range(levels - 1)] for c in places]
+    for c in places[:-1]:
+        terms[c].append((levels, levels - 1 + c, 0))
+    other = tuple(PARTS + c for c in places)
+    middle = add_levels(query_places, weights, base[PARTS:], flat, terms, other, False, None)
+    terms = [[] for _ in places[:-1]] + [[(levels, 0, 0)]]
+    (out,) = add_levels(query_places, weights, middle, last[-1:], terms, other, True, out)
     return out
 
 

time: 36 us -> 37.3 us (1.036)
  the two profiles are of different devices: /device:TPU:0 before, /device:TPU:26 now
where the time goes in v5:
time: 37.3 us; the launch traced here: 37 us
  Pallas kernels  14.5 us (39%)
  waiting for transfers between devices  11.6 us (31%)
  starting transfers between devices  9.85 us (26%)
  other arithmetic  0.93 us (2%)
    ppermute x10, waiting for transfers between devices, swapped(): return lax.ppermute(array, 'seq', pairs)  11.6 us
    ppermute x10, starting transfers between devices, swapped(): return lax.ppermute(array, 'seq', pairs)  9.85 us
    pallas_call x4, Pallas kernels, base_part(): pl.pallas_call(functools.partial(base_kernel, place, levels, buckets), ou...  7.76 us
    pallas_call x3, Pallas kernels, add_levels(): pl.pallas_call(functools.partial(levels_kernel, places, terms, len(states...  3.11 us
    pallas_call x1, Pallas kernels, own_block_states(): pl.pallas_call(functools.partial(own_kernel, level_weight.shape[1], prefi...  2.27 us
    pallas_call x1, Pallas kernels, given_states(): pl.pallas_call(functools.partial(given_kernel, PARTS), out_shape=jax.Shap...  1.32 us
    concatenate x1, other arithmetic, own_block_states(): jnp.concatenate([jnp.transpose(level_weight, (1, 0, 2)).reshape(-1, rows)...  0.85 us
  transfers between devices with their start and end apart: 10, of which 4 were waited for; matrix products, arithmetic and copies ran while one was open for 3% of the time, Pallas kernels for 33%

profile of v5, /device:TPU:26, one launch (start us, length us, event | category | flops | bytes accessed | tf_op | source)
XLA Modules:
  0.0 37.0 jit_solution(1102368368800366169)
XLA Ops:
  0.0 1.3 %states_given.1 = f32[2,128,128]{2,1,0:T(8,128)S(1)} custom-call(f32[256,1024]{1,0:T(8,128)} %k_hbm.3, f32[256,1024]{1,0:T(8,128)} %v_hbm.3), custom_call_target="tpu_custom_call" | custom-call | flops 67108864 | bytes 524288 | tf_op jit(solution)/shard_map/states_given/pallas_call | solution.py:78
  1.3 1.6 %collective-permute-start.5 = (f32[2,128,128]{2,1,0:T(8,128)S(1)}, f32[2,128,128]{2,1,0:T(8,128)S(1)}, u32[]{:S(2)}, u32[]{:S(2)}) collective-permute-start(f32[2,128,128]{2,1,0:T(8,128)S(1)} %states_given.1), channel_id=1, source_target_pairs={{0,2},{2,0},{4,6},{6,4},{8,10},{10,8},{12,14},{14,12},{1,3},{3,1},... | collective-permute-start | bytes 393224 | tf_op jit(solution)/shard_map/ppermute | solution.py:311
  2.9 0.8 %pad_maximum_fusion.1.line_ref = f32[112,256]{1,0:T(8,128)S(1)} fusion(f32[64,256]{1,0:T(8,128)} %bitcast.4, f32[48,256]{1,0:T(8,128)} %bitcast.5), kind=kLoop, calls=%fused_computation.1 | loop fusion | flops 28672 | bytes 229376 | tf_op jit(solution)/shard_map/concatenate | solution.py:159
  3.8 2.3 %states_own.1 = (f32[256,1024]{1,0:T(8,128)S(1)}, f32[256,1024]{1,0:T(8,128)S(1)}, f32[256,1024]{1,0:T(8,128)S(1)}, f32[2,1024,128]{2,1,0:T(8,128)S(1)}, f32[256...) custom-call(f32[112,256]{1,0:T(8,128)S(1)} %pad_maximum_fusion.1.lin, ...), custom_call_target="tpu_custom_call" | custom-call | flops 134217728 | bytes 6291456 | tf_op jit(solution)/shard_map/states_own/pallas_call | solution.py:169
  6.0 0.6 %collective-permute-start = (f32[2,128,128]{2,1,0:T(8,128)S(1)}, f32[2,128,128]{2,1,0:T(8,128)S(1)}, u32[]{:S(2)}, u32[]{:S(2)}) collective-permute-start(f32[2,128,128]{2,1,0:T(8,128)S(1)} %get-tuple-element.25), channel_id=1, source_target_pairs={{0,2},{2,0},{4,6},{6,4},{8,10},{10,8},{12,14},{14,12},{1,3},{3,1},... | collective-permute-start | bytes 393224 | tf_op jit(solution)/shard_map/ppermute | solution.py:311
  6.6 0.0 collective-permute-done.5.refs_0_
  6.7 0.5 %collective-permute-start.6 = (f32[2,128,128]{2,1,0:T(8,128)S(1)}, f32[2,128,128]{2,1,0:T(8,128)S(1)}, u32[]{:S(2)}, u32[]{:S(2)}) collective-permute-start(f32[2,128,128]{2,1,0:T(8,128)S(1)} %add.14), channel_id=1, source_target_pairs={{0,4},{2,6},{4,0},{6,2},{8,12},{10,14},{12,8},{14,10},{1,5},{3,7},... | collective-permute-start | bytes 393224 | tf_op jit(solution)/shard_map/ppermute | solution.py:311
  7.2 3.9 %collective-permute-done.refs_1_ = f32[2,128,128]{2,1,0:T(8,128)S(1)} collective-permute-done((f32[2,128,128]{2,1,0:T(8,128)S(1)}, f32[2,128,128]{2,1,0:T(8,128)S(1)}, u32[]{:S(2)}, u32[]{:S(2)}) %collective-permute-start) | collective-permute-done | bytes 131104 | tf_op jit(solution)/shard_map/ppermute | solution.py:311
  11.1 0.5 %collective-permute-start.1 = (f32[2,128,128]{2,1,0:T(8,128)S(1)}, f32[2,128,128]{2,1,0:T(8,128)S(1)}, u32[]{:S(2)}, u32[]{:S(2)}) collective-permute-start(f32[2,128,128]{2,1,0:T(8,128)S(1)} %add.12), channel_id=1, source_target_pairs={{0,4},{2,6},{4,0},{6,2},{8,12},{10,14},{12,8},{14,10},{1,5},{3,7},... | collective-permute-start | bytes 393224 | tf_op jit(solution)/shard_map/ppermute | solution.py:311
  11.6 0.5 %collective-permute-start.4 = (f32[4,128,128]{2,1,0:T(8,128)S(1)}, f32[4,128,128]{2,1,0:T(8,128)S(1)}, u32[]{:S(2)}, u32[]{:S(2)}) collective-permute-start(f32[4,128,128]{2,1,0:T(8,128)S(1)} %get-tuple-element.26), channel_id=1, source_target_pairs={{0,2},{2,0},{4,6},{6,4},{8,10},{10,8},{12,14},{14,12},{1,3},{3,1},... | collective-permute-start | bytes 786440 | tf_op jit(solution)/shard_map/ppermute | solution.py:311
  12.1 2.2 %shard_map.64 = (f32[256,256]{1,0:T(8,128)S(1)}, f32[2,1024,128]{2,1,0:T(8,128)S(1)}) custom-call(f32[256,1024]{1,0:T(8,128)S(1)} %get-tuple-element.22.q_ref, f32[256,1024]{1,0:T(8,128)S(1)} %get-tuple-element.28.k_ref, f32[256,1024]{1,0:T(8,128)S(1)} %get-tuple-element.29.v_ref, f32[256,128]{1,0:T(8,128)S(1)} %get-tuple-element.23.weight_ref, ...), custom_call_target="tpu_custom_call" | custom-call | flops 805306368 | bytes 1310720 | tf_op jit(solution)/shard_map/pallas_call | solution.py:229
  14.3 0.0 collective-permute-done.6.refs_2_
  14.4 0.4 %collective-permute-start.8 = (f32[2,128,128]{2,1,0:T(8,128)S(1)}, f32[2,128,128]{2,1,0:T(8,128)S(1)}, u32[]{:S(2)}, u32[]{:S(2)}) collective-permute-start(f32[2,128,128]{2,1,0:T(8,128)S(1)} %add.15), channel_id=1, source_target_pairs={{0,8},{2,10},{4,12},{6,14},{8,0},{10,2},{12,4},{14,6},{1,9},{3,11}... | collective-permute-start | bytes 393224 | tf_op jit(solution)/shard_map/ppermute | solution.py:311
  14.8 2.4 %collective-permute-done.1.refs_3_ = f32[2,128,128]{2,1,0:T(8,128)S(1)} collective-permute-done((f32[2,128,128]{2,1,0:T(8,128)S(1)}, f32[2,128,128]{2,1,0:T(8,128)S(1)}, u32[]{:S(2)}, u32[]{:S(2)}) %collective-permute-start.1) | collective-permute-done | bytes 131104 | tf_op jit(solution)/shard_map/ppermute | solution.py:311
  17.2 0.2 collective-permute-start.2
  17.5 1.6 %collective-permute-start.7 = (f32[4,128,128]{2,1,0:T(8,128)S(1)}, f32[4,128,128]{2,1,0:T(8,128)S(1)}, u32[]{:S(2)}, u32[]{:S(2)}) collective-permute-start(f32[4,128,128]{2,1,0:T(8,128)S(1)} %pad_maximum_fusion), channel_id=1, source_target_pairs={{0,2},{2,0},{4,6},{6,4},{8,10},{10,8},{12,14},{14,12},{1,3},{3,1},... | collective-permute-start | bytes 786440 | tf_op jit(solution)/shard_map/ppermute | solution.py:311
  19.1 2.2 %shard_map.65 = (f32[256,256]{1,0:T(8,128)S(1)}, f32[2,1024,128]{2,1,0:T(8,128)S(1)}) custom-call(f32[256,1024]{1,0:T(8,128)S(1)} %get-tuple-element.22.q_ref, f32[256,1024]{1,0:T(8,128)S(1)} %get-tuple-element.28.k_ref, f32[256,1024]{1,0:T(8,128)S(1)} %get-tuple-element.29.v_ref, f32[256,128]{1,0:T(8,128)S(1)} %get-tuple-element.23.weight_ref, ...), custom_call_target="tpu_custom_call" | custom-call | flops 805306368 | bytes 1310720 | tf_op jit(solution)/shard_map/pallas_call | solution.py:229
  21.3 4.0 %collective-permute-done.8.refs_4_ = f32[2,128,128]{2,1,0:T(8,128)S(1)} collective-permute-done((f32[2,128,128]{2,1,0:T(8,128)S(1)}, f32[2,128,128]{2,1,0:T(8,128)S(1)}, u32[]{:S(2)}, u32[]{:S(2)}) %collective-permute-start.8) | collective-permute-done | bytes 131104 | tf_op jit(solution)/shard_map/ppermute | solution.py:311
  25.3 1.5 %collective-permute-start.9 = (f32[2,128,128]{2,1,0:T(8,128)S(1)}, f32[2,128,128]{2,1,0:T(8,128)S(1)}, u32[]{:S(2)}, u32[]{:S(2)}) collective-permute-start(f32[2,128,128]{2,1,0:T(8,128)S(1)} %collective-permute-done.8.refs_4_), channel_id=1, source_target_pairs={{0,4},{2,6},{4,0},{6,2},{8,10},{10,8},{12,14},{14,12},{1,5},{3,7},... | collective-permute-start | bytes 393224 | tf_op jit(solution)/shard_map/ppermute | solution.py:311
  26.8 2.2 %shard_map.66 = (f32[256,256]{1,0:T(8,128)S(1)}, f32[2,1024,128]{2,1,0:T(8,128)S(1)}) custom-call(f32[256,1024]{1,0:T(8,128)S(1)} %get-tuple-element.22.q_ref, f32[256,1024]{1,0:T(8,128)S(1)} %get-tuple-element.28.k_ref, f32[256,1024]{1,0:T(8,128)S(1)} %get-tuple-element.29.v_ref, f32[256,128]{1,0:T(8,128)S(1)} %get-tuple-element.23.weight_ref, ...), custom_call_target="tpu_custom_call" | custom-call | flops 805306368 | bytes 1310720 | tf_op jit(solution)/shard_map/pallas_call | solution.py:229
  29.1 0.0 collective-permute-done.2.refs_5_
  29.1 2.4 %collective-permute-start.3 = (f32[2,128,128]{2,1,0:T(8,128)S(1)}, f32[2,128,128]{2,1,0:T(8,128)S(1)}, u32[]{:S(2)}, u32[]{:S(2)}) collective-permute-start(f32[2,128,128]{2,1,0:T(8,128)S(1)} %collective-permute-done.2.refs_5_), channel_id=1, source_target_pairs={{8,10},{10,8},{12,14},{14,12},{9,11},{11,9},{13,15},{15,13},{24,26... | collective-permute-start | bytes 393224 | tf_op jit(solution)/shard_map/ppermute | solution.py:311
  31.5 1.1 %shard_map.67.refs_4_ = f32[256,256]{1,0:T(8,128)S(1)} custom-call(f32[256,1024]{1,0:T(8,128)S(1)} %get-tuple-element.22.q_ref, f32[256,1024]{1,0:T(8,128)S(1)} %get-tuple-element.28.k_ref, f32[256,1024]{1,0:T(8,128)S(1)} %get-tuple-element.29.v_ref, f32[256,128]{1,0:T(8,128)S(1)} %get-tuple-element.23.weight_ref, ...), custom_call_target="tpu_custom_call" | custom-call | flops 805306368 | bytes 1310720 | tf_op jit(solution)/shard_map/pallas_call | solution.py:229
  32.6 1.5 %shard_map.69.refs_3_ = f32[256,1024]{1,0:T(8,128)} custom-call(f32[256,1024]{1,0:T(8,128)S(1)} %get-tuple-element.22.q_ref, f32[256,128]{1,0:T(8,128)S(1)} %get-tuple-element.23.weight_ref, f32[2,128,128]{2,1,0:T(8,128)S(1)} %collective-permute-done.5.refs_0_, f32[2,128,128]{2,1,0:T(8,128)S(1)} %collective-permute-done.refs_1_, ...), custom_call_target="tpu_custom_call" | custom-call | flops 402653184 | bytes 1572864 | tf_op jit(solution)/shard_map/pallas_call | solution.py:290
  34.1 0.0 collective-permute-done.4.refs_0_
  34.1 0.0 collective-permute-done.9.refs_2_
  34.1 0.0 collective-permute-done.7.refs_1_
  34.1 0.6 %shard_map.68 = (f32[256,256]{1,0:T(8,128)S(1)}, f32[256,256]{1,0:T(8,128)S(1)}) custom-call(f32[256,1024]{1,0:T(8,128)S(1)} %get-tuple-element.22.q_ref, f32[256,128]{1,0:T(8,128)S(1)} %get-tuple-element.23.weight_ref, f32[4,128,128]{2,1,0:T(8,128)S(1)} %collective-permute-done.4.refs_0_, f32[4,128,128]{2,1,0:T(8,128)S(1)} %collective-permute-done.7.refs_1_, ...), custom_call_target="tpu_custom_call" | custom-call | flops 335544320 | bytes 1572864 | tf_op jit(solution)/shard_map/pallas_call | solution.py:290
  34.8 1.2 %collective-permute-done.3.refs_0_ = f32[2,128,128]{2,1,0:T(8,128)S(1)} collective-permute-done((f32[2,128,128]{2,1,0:T(8,128)S(1)}, f32[2,128,128]{2,1,0:T(8,128)S(1)}, u32[]{:S(2)}, u32[]{:S(2)}) %collective-permute-start.3) | collective-permute-done | bytes 131104 | tf_op jit(solution)/shard_map/ppermute | solution.py:311
  35.9 1.0 %shard_map.70 = f32[256,1024]{1,0:T(8,128)} custom-call(f32[256,1024]{1,0:T(8,128)S(1)} %get-tuple-element.22.q_ref, f32[256,128]{1,0:T(8,128)S(1)} %get-tuple-element.23.weight_ref, f32[2,128,128]{2,1,0:T(8,128)S(1)} %collective-permute-done.3.refs_0_, f32[256,256]{1,0:T(8,128)S(1)} %get-tuple-element.35.refs_1_, ...), custom_call_target="tpu_custom_call", output_to_operand_aliasing={{}: (5, {})} | custom-call | flops 67108864 | bytes 1572864 | tf_op jit(solution)/shard_map/pallas_call | solution.py:290
  (5 shorter events, 0.1 us)
Async XLA Ops:
  1.3 5.3 %collective-permute-start.5 = (f32[2,128,128]{2,1,0:T(8,128)S(1)}, f32[2,128,128]{2,1,0:T(8,128)S(1)}, u32[]{:S(2)}, u32[]{:S(2)}) collective-permute-start(f32[2,128,128]{2,1,0:T(8,128)S(1)} %states_given.1), channel_id=1, source_target_pairs={{0,2},{2,0},{4,6},{6,4},{8,10},{10,8},{12,14},{14,12},{1,3},{3,1},... | collective-permute-start | bytes 393224 | tf_op jit(solution)/shard_map/ppermute | solution.py:311
  6.0 5.0 %collective-permute-start = (f32[2,128,128]{2,1,0:T(8,128)S(1)}, f32[2,128,128]{2,1,0:T(8,128)S(1)}, u32[]{:S(2)}, u32[]{:S(2)}) collective-permute-start(f32[2,128,128]{2,1,0:T(8,128)S(1)} %get-tuple-element.25), channel_id=1, source_target_pairs={{0,2},{2,0},{4,6},{6,4},{8,10},{10,8},{12,14},{14,12},{1,3},{3,1},... | collective-permute-start | bytes 393224 | tf_op jit(solution)/shard_map/ppermute | solution.py:311
  6.7 7.7 %collective-permute-start.6 = (f32[2,128,128]{2,1,0:T(8,128)S(1)}, f32[2,128,128]{2,1,0:T(8,128)S(1)}, u32[]{:S(2)}, u32[]{:S(2)}) collective-permute-start(f32[2,128,128]{2,1,0:T(8,128)S(1)} %add.14), channel_id=1, source_target_pairs={{0,4},{2,6},{4,0},{6,2},{8,12},{10,14},{12,8},{14,10},{1,5},{3,7},... | collective-permute-start | bytes 393224 | tf_op jit(solution)/shard_map/ppermute | solution.py:311
  11.1 6.1 %collective-permute-start.1 = (f32[2,128,128]{2,1,0:T(8,128)S(1)}, f32[2,128,128]{2,1,0:T(8,128)S(1)}, u32[]{:S(2)}, u32[]{:S(2)}) collective-permute-start(f32[2,128,128]{2,1,0:T(8,128)S(1)} %add.12), channel_id=1, source_target_pairs={{0,4},{2,6},{4,0},{6,2},{8,12},{10,14},{12,8},{14,10},{1,5},{3,7},... | collective-permute-start | bytes 393224 | tf_op jit(solution)/shard_map/ppermute | solution.py:311
  11.6 22.5 %collective-permute-start.4 = (f32[4,128,128]{2,1,0:T(8,128)S(1)}, f32[4,128,128]{2,1,0:T(8,128)S(1)}, u32[]{:S(2)}, u32[]{:S(2)}) collective-permute-start(f32[4,128,128]{2,1,0:T(8,128)S(1)} %get-tuple-element.26), channel_id=1, source_target_pairs={{0,2},{2,0},{4,6},{6,4},{8,10},{10,8},{12,14},{14,12},{1,3},{3,1},... | collective-permute-start | bytes 786440 | tf_op jit(solution)/shard_map/ppermute | solution.py:311
  14.4 10.9 %collective-permute-start.8 = (f32[2,128,128]{2,1,0:T(8,128)S(1)}, f32[2,128,128]{2,1,0:T(8,128)S(1)}, u32[]{:S(2)}, u32[]{:S(2)}) collective-permute-start(f32[2,128,128]{2,1,0:T(8,128)S(1)} %add.15), channel_id=1, source_target_pairs={{0,8},{2,10},{4,12},{6,14},{8,0},{10,2},{12,4},{14,6},{1,9},{3,11}... | collective-permute-start | bytes 393224 | tf_op jit(solution)/shard_map/ppermute | solution.py:311
  17.2 11.8 %collective-permute-start.2 = (f32[2,128,128]{2,1,0:T(8,128)S(1)}, f32[2,128,128]{2,1,0:T(8,128)S(1)}, u32[]{:S(2)}, u32[]{:S(2)}) collective-permute-start(f32[2,128,128]{2,1,0:T(8,128)S(1)} %add.13), channel_id=1, source_target_pairs={{0,8},{2,10},{4,12},{6,14},{8,0},{10,2},{12,4},{14,6},{1,9},{3,11}... | collective-permute-start | bytes 393224 | tf_op jit(solution)/shard_map/ppermute | solution.py:311
  17.5 16.6 %collective-permute-start.7 = (f32[4,128,128]{2,1,0:T(8,128)S(1)}, f32[4,128,128]{2,1,0:T(8,128)S(1)}, u32[]{:S(2)}, u32[]{:S(2)}) collective-permute-start(f32[4,128,128]{2,1,0:T(8,128)S(1)} %pad_maximum_fusion), channel_id=1, source_target_pairs={{0,2},{2,0},{4,6},{6,4},{8,10},{10,8},{12,14},{14,12},{1,3},{3,1},... | collective-permute-start | bytes 786440 | tf_op jit(solution)/shard_map/ppermute | solution.py:311
  25.3 8.8 %collective-permute-start.9 = (f32[2,128,128]{2,1,0:T(8,128)S(1)}, f32[2,128,128]{2,1,0:T(8,128)S(1)}, u32[]{:S(2)}, u32[]{:S(2)}) collective-permute-start(f32[2,128,128]{2,1,0:T(8,128)S(1)} %collective-permute-done.8.refs_4_), channel_id=1, source_target_pairs={{0,4},{2,6},{4,0},{6,2},{8,10},{10,8},{12,14},{14,12},{1,5},{3,7},... | collective-permute-start | bytes 393224 | tf_op jit(solution)/shard_map/ppermute | solution.py:311
  29.1 6.9 %collective-permute-start.3 = (f32[2,128,128]{2,1,0:T(8,128)S(1)}, f32[2,128,128]{2,1,0:T(8,128)S(1)}, u32[]{:S(2)}, u32[]{:S(2)}) collective-permute-start(f32[2,128,128]{2,1,0:T(8,128)S(1)} %collective-permute-done.2.refs_5_), channel_id=1, source_target_pairs={{8,10},{10,8},{12,14},{14,12},{9,11},{11,9},{13,15},{15,13},{24,26... | collective-permute-start | bytes 393224 | tf_op jit(solution)/shard_map/ppermute | solution.py:311

commit v6 on v5

--- a/solution.py
+++ b/solution.py
@@ -305,10 +305,17 @@
     )(*operands)
 
 
-def swapped(array, bit, keep=lambda i: True, alt=None):
-    size = lax.axis_size("seq")
-    pairs = [(i, i ^ (1 << bit if alt is None or i >> alt & 1 else 2)) for i in range(size) if keep(i)]
-    return lax.ppermute(array, "seq", pairs)
+def swapped(array, bit, needs=None):
+    size, cores = lax.axis_size("seq"), lax.axis_size("head")
+    pairs = []
+    for i in range(size):
+        for core in range(cores):
+            if needs is None or needs(i) or cores % 2:
+                to = (i ^ 1 << bit) * cores + core
+            else:
+                to = i * cores + (core ^ 1)
+            pairs.append((i * cores + core, to))
+    return lax.ppermute(array, ("seq", "head"), pairs)
 
 
 def attend(queries, keys, values, level_weight, prefix_weight, prefix_state):
@@ -344,7 +351,7 @@
         other_states.append([swapped(both, 0)])
     top = levels - 1
     needs = lambda i: i >> top & 1
-    last = [swapped(own_states[top][c], 0, needs if c == PARTS - 1 else lambda i: True, top) for c in places]
+    last = [swapped(own_states[top][c], 0, needs if c in (0, 1) else None) for c in places]
 
     flat = [x for level in own_states for x in level]
     terms = [[(1 + i, i * PARTS + c, 0) for i in range(levels)] for c in places]

time: 37.3 us -> 35.6 us (0.954)
  the two profiles are of different devices: /device:TPU:26 before, /device:TPU:0 now
where the time goes in v6:
time: 35.6 us; the launch traced here: 35.3 us
  Pallas kernels  14.5 us (41%)
  starting transfers between devices  12.4 us (35%)
  waiting for transfers between devices  7.36 us (21%)
  other arithmetic  0.93 us (3%)
    ppermute x10, starting transfers between devices, swapped(): return lax.ppermute(array, ('seq', 'head'), pairs)  12.4 us
    pallas_call x4, Pallas kernels, base_part(): pl.pallas_call(functools.partial(base_kernel, place, levels, buckets), ou...  7.76 us
    ppermute x10, waiting for transfers between devices, swapped(): return lax.ppermute(array, ('seq', 'head'), pairs)  7.36 us
    pallas_call x3, Pallas kernels, add_levels(): pl.pallas_call(functools.partial(levels_kernel, places, terms, len(states...  3.12 us
    pallas_call x1, Pallas kernels, own_block_states(): pl.pallas_call(functools.partial(own_kernel, level_weight.shape[1], prefi...  2.27 us
    pallas_call x1, Pallas kernels, given_states(): pl.pallas_call(functools.partial(given_kernel, PARTS), out_shape=jax.Shap...  1.32 us
    concatenate x1, other arithmetic, own_block_states(): jnp.concatenate([jnp.transpose(level_weight, (1, 0, 2)).reshape(-1, rows)...  0.85 us
  transfers between devices with their start and end apart: 10, of which 3 were waited for; matrix products, arithmetic and copies ran while one was open for 3% of the time, Pallas kernels for 34%

profile of v6, /device:TPU:0, one launch (start us, length us, event | category | flops | bytes accessed | tf_op | source)
XLA Modules:
  0.0 35.3 jit_solution(2021749141310283465)
XLA Ops:
  0.0 1.3 %states_given.1 = f32[2,128,128]{2,1,0:T(8,128)S(1)} custom-call(f32[256,1024]{1,0:T(8,128)} %k_hbm.3, f32[256,1024]{1,0:T(8,128)} %v_hbm.3), custom_call_target="tpu_custom_call" | custom-call | flops 67108864 | bytes 524288 | tf_op jit(solution)/shard_map/states_given/pallas_call | solution.py:78
  1.3 3.1 %collective-permute-start.5 = (f32[2,128,128]{2,1,0:T(8,128)S(1)}, f32[2,128,128]{2,1,0:T(8,128)S(1)}, u32[]{:S(2)}, u32[]{:S(2)}) collective-permute-start(f32[2,128,128]{2,1,0:T(8,128)S(1)} %states_given.1), channel_id=1, source_target_pairs={{0,2},{1,3},{2,0},{3,1},{4,6},{5,7},{6,4},{7,5},{8,10},{9,11},{10,... | collective-permute-start | bytes 393224 | tf_op jit(solution)/shard_map/ppermute | solution.py:318
  4.4 0.8 %pad_maximum_fusion.1.line_ref = f32[112,256]{1,0:T(8,128)S(1)} fusion(f32[64,256]{1,0:T(8,128)} %bitcast.4, f32[48,256]{1,0:T(8,128)} %bitcast.5), kind=kLoop, calls=%fused_computation.1 | loop fusion | flops 28672 | bytes 229376 | tf_op jit(solution)/shard_map/concatenate | solution.py:159
  5.2 2.3 %states_own.1 = (f32[256,1024]{1,0:T(8,128)S(1)}, f32[256,1024]{1,0:T(8,128)S(1)}, f32[256,1024]{1,0:T(8,128)S(1)}, f32[2,1024,128]{2,1,0:T(8,128)S(1)}, f32[256...) custom-call(f32[112,256]{1,0:T(8,128)S(1)} %pad_maximum_fusion.1.lin, ...), custom_call_target="tpu_custom_call" | custom-call | flops 134217728 | bytes 6291456 | tf_op jit(solution)/shard_map/states_own/pallas_call | solution.py:169
  7.5 0.1 collective-permute-start
  7.6 0.3 collective-permute-done.5.refs_0_
  7.9 1.9 %collective-permute-start.6 = (f32[2,128,128]{2,1,0:T(8,128)S(1)}, f32[2,128,128]{2,1,0:T(8,128)S(1)}, u32[]{:S(2)}, u32[]{:S(2)}) collective-permute-start(f32[2,128,128]{2,1,0:T(8,128)S(1)} %add.14), channel_id=1, source_target_pairs={{0,4},{1,5},{2,6},{3,7},{4,0},{5,1},{6,2},{7,3},{8,12},{9,13},{10,... | collective-permute-start | bytes 393224 | tf_op jit(solution)/shard_map/ppermute | solution.py:318
  9.8 2.8 %collective-permute-done.refs_1_ = f32[2,128,128]{2,1,0:T(8,128)S(1)} collective-permute-done((f32[2,128,128]{2,1,0:T(8,128)S(1)}, f32[2,128,128]{2,1,0:T(8,128)S(1)}, u32[]{:S(2)}, u32[]{:S(2)}) %collective-permute-start) | collective-permute-done | bytes 131104 | tf_op jit(solution)/shard_map/ppermute | solution.py:318
  12.6 1.6 %collective-permute-start.1 = (f32[2,128,128]{2,1,0:T(8,128)S(1)}, f32[2,128,128]{2,1,0:T(8,128)S(1)}, u32[]{:S(2)}, u32[]{:S(2)}) collective-permute-start(f32[2,128,128]{2,1,0:T(8,128)S(1)} %add.12), channel_id=1, source_target_pairs={{0,4},{1,5},{2,6},{3,7},{4,0},{5,1},{6,2},{7,3},{8,12},{9,13},{10,... | collective-permute-start | bytes 393224 | tf_op jit(solution)/shard_map/ppermute | solution.py:318
  14.2 0.5 %collective-permute-start.4 = (f32[4,128,128]{2,1,0:T(8,128)S(1)}, f32[4,128,128]{2,1,0:T(8,128)S(1)}, u32[]{:S(2)}, u32[]{:S(2)}) collective-permute-start(f32[4,128,128]{2,1,0:T(8,128)S(1)} %get-tuple-element.26), channel_id=1, source_target_pairs={{0,2},{1,3},{2,0},{3,1},{4,6},{5,7},{6,4},{7,5},{8,10},{9,11},{10,... | collective-permute-start | bytes 786440 | tf_op jit(solution)/shard_map/ppermute | solution.py:318
  14.7 2.2 %shard_map.64 = (f32[256,256]{1,0:T(8,128)S(1)}, f32[2,1024,128]{2,1,0:T(8,128)S(1)}) custom-call(f32[256,1024]{1,0:T(8,128)S(1)} %get-tuple-element.22.q_ref, f32[256,1024]{1,0:T(8,128)S(1)} %get-tuple-element.28.k_ref, f32[256,1024]{1,0:T(8,128)S(1)} %get-tuple-element.29.v_ref, f32[256,128]{1,0:T(8,128)S(1)} %get-tuple-element.23.weight_ref, ...), custom_call_target="tpu_custom_call" | custom-call | flops 805306368 | bytes 1310720 | tf_op jit(solution)/shard_map/pallas_call | solution.py:229
  16.9 0.0 collective-permute-done.6.refs_2_
  17.0 2.7 %collective-permute-start.8 = (f32[2,128,128]{2,1,0:T(8,128)S(1)}, f32[2,128,128]{2,1,0:T(8,128)S(1)}, u32[]{:S(2)}, u32[]{:S(2)}) collective-permute-start(f32[2,128,128]{2,1,0:T(8,128)S(1)} %add.15), channel_id=1, source_target_pairs={{0,8},{1,9},{2,10},{3,11},{4,12},{5,13},{6,14},{7,15},{8,0},{9,1},... | collective-permute-start | bytes 393224 | tf_op jit(solution)/shard_map/ppermute | solution.py:318
  19.6 0.0 collective-permute-done.1.refs_3_
  19.7 1.6 %collective-permute-start.2 = (f32[2,128,128]{2,1,0:T(8,128)S(1)}, f32[2,128,128]{2,1,0:T(8,128)S(1)}, u32[]{:S(2)}, u32[]{:S(2)}) collective-permute-start(f32[2,128,128]{2,1,0:T(8,128)S(1)} %add.13), channel_id=1, source_target_pairs={{0,8},{1,9},{2,10},{3,11},{4,12},{5,13},{6,14},{7,15},{8,0},{9,1},... | collective-permute-start | bytes 393224 | tf_op jit(solution)/shard_map/ppermute | solution.py:318
  21.3 0.4 %collective-permute-start.7 = (f32[4,128,128]{2,1,0:T(8,128)S(1)}, f32[4,128,128]{2,1,0:T(8,128)S(1)}, u32[]{:S(2)}, u32[]{:S(2)}) collective-permute-start(f32[4,128,128]{2,1,0:T(8,128)S(1)} %pad_maximum_fusion), channel_id=1, source_target_pairs={{0,2},{1,3},{2,0},{3,1},{4,6},{5,7},{6,4},{7,5},{8,10},{9,11},{10,... | collective-permute-start | bytes 786440 | tf_op jit(solution)/shard_map/ppermute | solution.py:318
  21.7 2.2 %shard_map.65 = (f32[256,256]{1,0:T(8,128)S(1)}, f32[2,1024,128]{2,1,0:T(8,128)S(1)}) custom-call(f32[256,1024]{1,0:T(8,128)S(1)} %get-tuple-element.22.q_ref, f32[256,1024]{1,0:T(8,128)S(1)} %get-tuple-element.28.k_ref, f32[256,1024]{1,0:T(8,128)S(1)} %get-tuple-element.29.v_ref, f32[256,128]{1,0:T(8,128)S(1)} %get-tuple-element.23.weight_ref, ...), custom_call_target="tpu_custom_call" | custom-call | flops 805306368 | bytes 1310720 | tf_op jit(solution)/shard_map/pallas_call | solution.py:229
  23.9 4.3 %collective-permute-done.8.refs_4_ = f32[2,128,128]{2,1,0:T(8,128)S(1)} collective-permute-done((f32[2,128,128]{2,1,0:T(8,128)S(1)}, f32[2,128,128]{2,1,0:T(8,128)S(1)}, u32[]{:S(2)}, u32[]{:S(2)}) %collective-permute-start.8) | collective-permute-done | bytes 131104 | tf_op jit(solution)/shard_map/ppermute | solution.py:318
  28.2 0.0 collective-permute-start.9
  28.2 2.2 %shard_map.66 = (f32[256,256]{1,0:T(8,128)S(1)}, f32[2,1024,128]{2,1,0:T(8,128)S(1)}) custom-call(f32[256,1024]{1,0:T(8,128)S(1)} %get-tuple-element.22.q_ref, f32[256,1024]{1,0:T(8,128)S(1)} %get-tuple-element.28.k_ref, f32[256,1024]{1,0:T(8,128)S(1)} %get-tuple-element.29.v_ref, f32[256,128]{1,0:T(8,128)S(1)} %get-tuple-element.23.weight_ref, ...), custom_call_target="tpu_custom_call" | custom-call | flops 805306368 | bytes 1310720 | tf_op jit(solution)/shard_map/pallas_call | solution.py:229
  30.4 0.0 collective-permute-done.2.refs_5_
  30.4 0.6 %collective-permute-start.3 = (f32[2,128,128]{2,1,0:T(8,128)S(1)}, f32[2,128,128]{2,1,0:T(8,128)S(1)}, u32[]{:S(2)}, u32[]{:S(2)}) collective-permute-start(f32[2,128,128]{2,1,0:T(8,128)S(1)} %collective-permute-done.2.refs_5_), channel_id=1, source_target_pairs={{0,1},{1,0},{2,3},{3,2},{4,5},{5,4},{6,7},{7,6},{8,10},{9,11},{10,... | collective-permute-start | bytes 393224 | tf_op jit(solution)/shard_map/ppermute | solution.py:318
  31.0 1.1 %shard_map.67.refs_4_ = f32[256,256]{1,0:T(8,128)S(1)} custom-call(f32[256,1024]{1,0:T(8,128)S(1)} %get-tuple-element.22.q_ref, f32[256,1024]{1,0:T(8,128)S(1)} %get-tuple-element.28.k_ref, f32[256,1024]{1,0:T(8,128)S(1)} %get-tuple-element.29.v_ref, f32[256,128]{1,0:T(8,128)S(1)} %get-tuple-element.23.weight_ref, ...), custom_call_target="tpu_custom_call" | custom-call | flops 805306368 | bytes 1310720 | tf_op jit(solution)/shard_map/pallas_call | solution.py:229
  32.1 1.5 %shard_map.69.refs_3_ = f32[256,1024]{1,0:T(8,128)} custom-call(f32[256,1024]{1,0:T(8,128)S(1)} %get-tuple-element.22.q_ref, f32[256,128]{1,0:T(8,128)S(1)} %get-tuple-element.23.weight_ref, f32[2,128,128]{2,1,0:T(8,128)S(1)} %collective-permute-done.5.refs_0_, f32[2,128,128]{2,1,0:T(8,128)S(1)} %collective-permute-done.refs_1_, ...), custom_call_target="tpu_custom_call" | custom-call | flops 402653184 | bytes 1572864 | tf_op jit(solution)/shard_map/pallas_call | solution.py:290
  33.6 0.0 collective-permute-done.4.refs_0_
  33.6 0.0 collective-permute-done.9.refs_2_
  33.6 0.0 collective-permute-done.7.refs_1_
  33.6 0.6 %shard_map.68 = (f32[256,256]{1,0:T(8,128)S(1)}, f32[256,256]{1,0:T(8,128)S(1)}) custom-call(f32[256,1024]{1,0:T(8,128)S(1)} %get-tuple-element.22.q_ref, f32[256,128]{1,0:T(8,128)S(1)} %get-tuple-element.23.weight_ref, f32[4,128,128]{2,1,0:T(8,128)S(1)} %collective-permute-done.4.refs_0_, f32[4,128,128]{2,1,0:T(8,128)S(1)} %collective-permute-done.7.refs_1_, ...), custom_call_target="tpu_custom_call" | custom-call | flops 335544320 | bytes 1572864 | tf_op jit(solution)/shard_map/pallas_call | solution.py:290
  34.2 0.0 collective-permute-done.3.refs_0_
  34.2 1.0 %shard_map.70 = f32[256,1024]{1,0:T(8,128)} custom-call(f32[256,1024]{1,0:T(8,128)S(1)} %get-tuple-element.22.q_ref, f32[256,128]{1,0:T(8,128)S(1)} %get-tuple-element.23.weight_ref, f32[2,128,128]{2,1,0:T(8,128)S(1)} %collective-permute-done.3.refs_0_, f32[256,256]{1,0:T(8,128)S(1)} %get-tuple-element.35.refs_1_, ...), custom_call_target="tpu_custom_call", output_to_operand_aliasing={{}: (5, {})} | custom-call | flops 67108864 | bytes 1572864 | tf_op jit(solution)/shard_map/pallas_call | solution.py:290
  (5 shorter events, 0.1 us)
Async XLA Ops:
  1.3 6.6 %collective-permute-start.5 = (f32[2,128,128]{2,1,0:T(8,128)S(1)}, f32[2,128,128]{2,1,0:T(8,128)S(1)}, u32[]{:S(2)}, u32[]{:S(2)}) collective-permute-start(f32[2,128,128]{2,1,0:T(8,128)S(1)} %states_given.1), channel_id=1, source_target_pairs={{0,2},{1,3},{2,0},{3,1},{4,6},{5,7},{6,4},{7,5},{8,10},{9,11},{10,... | collective-permute-start | bytes 393224 | tf_op jit(solution)/shard_map/ppermute | solution.py:318
  7.5 5.0 %collective-permute-start = (f32[2,128,128]{2,1,0:T(8,128)S(1)}, f32[2,128,128]{2,1,0:T(8,128)S(1)}, u32[]{:S(2)}, u32[]{:S(2)}) collective-permute-start(f32[2,128,128]{2,1,0:T(8,128)S(1)} %get-tuple-element.25), channel_id=1, source_target_pairs={{0,2},{1,3},{2,0},{3,1},{4,6},{5,7},{6,4},{7,5},{8,10},{9,11},{10,... | collective-permute-start | bytes 393224 | tf_op jit(solution)/shard_map/ppermute | solution.py:318
  7.9 9.0 %collective-permute-start.6 = (f32[2,128,128]{2,1,0:T(8,128)S(1)}, f32[2,128,128]{2,1,0:T(8,128)S(1)}, u32[]{:S(2)}, u32[]{:S(2)}) collective-permute-start(f32[2,128,128]{2,1,0:T(8,128)S(1)} %add.14), channel_id=1, source_target_pairs={{0,4},{1,5},{2,6},{3,7},{4,0},{5,1},{6,2},{7,3},{8,12},{9,13},{10,... | collective-permute-start | bytes 393224 | tf_op jit(solution)/shard_map/ppermute | solution.py:318
  12.6 7.1 %collective-permute-start.1 = (f32[2,128,128]{2,1,0:T(8,128)S(1)}, f32[2,128,128]{2,1,0:T(8,128)S(1)}, u32[]{:S(2)}, u32[]{:S(2)}) collective-permute-start(f32[2,128,128]{2,1,0:T(8,128)S(1)} %add.12), channel_id=1, source_target_pairs={{0,4},{1,5},{2,6},{3,7},{4,0},{5,1},{6,2},{7,3},{8,12},{9,13},{10,... | collective-permute-start | bytes 393224 | tf_op jit(solution)/shard_map/ppermute | solution.py:318
  14.2 19.3 %collective-permute-start.4 = (f32[4,128,128]{2,1,0:T(8,128)S(1)}, f32[4,128,128]{2,1,0:T(8,128)S(1)}, u32[]{:S(2)}, u32[]{:S(2)}) collective-permute-start(f32[4,128,128]{2,1,0:T(8,128)S(1)} %get-tuple-element.26), channel_id=1, source_target_pairs={{0,2},{1,3},{2,0},{3,1},{4,6},{5,7},{6,4},{7,5},{8,10},{9,11},{10,... | collective-permute-start | bytes 786440 | tf_op jit(solution)/shard_map/ppermute | solution.py:318
  17.0 11.2 %collective-permute-start.8 = (f32[2,128,128]{2,1,0:T(8,128)S(1)}, f32[2,128,128]{2,1,0:T(8,128)S(1)}, u32[]{:S(2)}, u32[]{:S(2)}) collective-permute-start(f32[2,128,128]{2,1,0:T(8,128)S(1)} %add.15), channel_id=1, source_target_pairs={{0,8},{1,9},{2,10},{3,11},{4,12},{5,13},{6,14},{7,15},{8,0},{9,1},... | collective-permute-start | bytes 393224 | tf_op jit(solution)/shard_map/ppermute | solution.py:318
  19.7 10.7 %collective-permute-start.2 = (f32[2,128,128]{2,1,0:T(8,128)S(1)}, f32[2,128,128]{2,1,0:T(8,128)S(1)}, u32[]{:S(2)}, u32[]{:S(2)}) collective-permute-start(f32[2,128,128]{2,1,0:T(8,128)S(1)} %add.13), channel_id=1, source_target_pairs={{0,8},{1,9},{2,10},{3,11},{4,12},{5,13},{6,14},{7,15},{8,0},{9,1},... | collective-permute-start | bytes 393224 | tf_op jit(solution)/shard_map/ppermute | solution.py:318
  21.3 12.3 %collective-permute-start.7 = (f32[4,128,128]{2,1,0:T(8,128)S(1)}, f32[4,128,128]{2,1,0:T(8,128)S(1)}, u32[]{:S(2)}, u32[]{:S(2)}) collective-permute-start(f32[4,128,128]{2,1,0:T(8,128)S(1)} %pad_maximum_fusion), channel_id=1, source_target_pairs={{0,2},{1,3},{2,0},{3,1},{4,6},{5,7},{6,4},{7,5},{8,10},{9,11},{10,... | collective-permute-start | bytes 786440 | tf_op jit(solution)/shard_map/ppermute | solution.py:318
  28.2 5.4 %collective-permute-start.9 = (f32[2,128,128]{2,1,0:T(8,128)S(1)}, f32[2,128,128]{2,1,0:T(8,128)S(1)}, u32[]{:S(2)}, u32[]{:S(2)}) collective-permute-start(f32[2,128,128]{2,1,0:T(8,128)S(1)} %collective-permute-done.8.refs_4_), channel_id=1, source_target_pairs={{0,1},{1,0},{2,3},{3,2},{4,5},{5,4},{6,7},{7,6},{8,10},{9,11},{10,... | collective-permute-start | bytes 393224 | tf_op jit(solution)/shard_map/ppermute | solution.py:318
  30.4 3.8 %collective-permute-start.3 = (f32[2,128,128]{2,1,0:T(8,128)S(1)}, f32[2,128,128]{2,1,0:T(8,128)S(1)}, u32[]{:S(2)}, u32[]{:S(2)}) collective-permute-start(f32[2,128,128]{2,1,0:T(8,128)S(1)} %collective-permute-done.2.refs_5_), channel_id=1, source_target_pairs={{0,1},{1,0},{2,3},{3,2},{4,5},{5,4},{6,7},{7,6},{8,10},{9,11},{10,... | collective-permute-start | bytes 393224 | tf_op jit(solution)/shard_map/ppermute | solution.py:318

commit v7 on v6

--- a/solution.py
+++ b/solution.py
@@ -94,8 +94,8 @@
 
 
 def own_kernel(
-    levels, buckets, line_ref, q_hbm, k_hbm, v_hbm, prefix_hbm,
-    q_out, k_out, v_out, prefix_out, weight_ref, whole_ref, *refs,
+    q_hbm, k_hbm, v_hbm, prefix_hbm,
+    q_out, k_out, v_out, prefix_out, whole_ref, *refs,
 ):
     (*part_refs, given_ref), sems = refs[:-1], refs[-1]
     per = given_ref.shape[0]
@@ -114,25 +114,6 @@
         pltpu.make_async_copy(prefix_hbm.at[pl.ds(first_head(0, per), per)], prefix_out, sems.at[3, 0])
     )
     copies[-1].start()
-    position = lax.axis_index("seq")
-    own_second = lax.rem(position, 2) == 0
-    rows = line_ref.shape[1]
-    heads = q_hbm.shape[1] // DH
-    lines = []
-    for i in range(levels):
-        line = line_ref[i * heads : (i + 1) * heads]
-        if i:
-            line = line * lax.rem(lax.shift_right_logical(position, i - 1), 2).astype(F32)
-        lines.append(jnp.where(own_second, jnp.concatenate([line[half:], line[:half]], axis=0), line))
-    first = line_ref[heads * levels : heads * levels + half * buckets]
-    second = line_ref[heads * levels + half * buckets :]
-    lines.append(jnp.where(own_second, second, first))
-    lines.append(jnp.where(own_second, first, second))
-    spare = weight_ref.shape[1] - heads * (levels + buckets)
-    if spare:
-        lines.append(jnp.zeros((spare, rows), F32))
-    weight_ref[...] = jnp.transpose(jnp.concatenate(lines, axis=0))
-
     copies[1].wait()
     copies[3].wait()
     for j in range(per):
@@ -151,10 +132,49 @@
         copies[i].wait()
 
 
-def own_block_states(queries, keys, values, level_weight, prefix_weight, prefix_state):
+def own_block_states(queries, keys, values, prefix_state):
     rows, columns = keys.shape
     heads = columns // DH
     per = heads // (2 * PARTS)
+    shapes = [queries.shape, keys.shape, values.shape, (per, *prefix_state.shape[1:])]
+    shapes += [(PARTS * per, DH, DH)] + [(per, DH, DH)] * (PARTS + 1)
+    return pl.pallas_call(
+        own_kernel,
+        out_shape=[jax.ShapeDtypeStruct(s, F32) for s in shapes],
+        in_specs=[IN_HBM] * 4,
+        out_specs=[IN_VMEM] * len(shapes),
+        scratch_shapes=[pltpu.SemaphoreType.DMA((4, 2))],
+        compiler_params=pltpu.CompilerParams(vmem_limit_bytes=GRANT - 153 * rows * columns * 4 // 10),
+        cost_estimate=pl.CostEstimate(
+            flops=4 * rows * columns * DH, bytes_accessed=24 * rows * columns, transcendentals=0
+        ),
+        name="states_own",
+    )(queries, keys, values, prefix_state)
+
+
+def columns_kernel(heads, levels, buckets, line_ref, weight_ref):
+    half = heads // 2
+    position = lax.axis_index("seq")
+    own_second = lax.rem(position, 2) == 0
+    rows = line_ref.shape[1]
+    lines = []
+    for i in range(levels):
+        line = line_ref[i * heads : (i + 1) * heads]
+        if i:
+            line = line * lax.rem(lax.shift_right_logical(position, i - 1), 2).astype(F32)
+        lines.append(jnp.where(own_second, jnp.concatenate([line[half:], line[:half]], axis=0), line))
+    first = line_ref[heads * levels : heads * levels + half * buckets]
+    second = line_ref[heads * levels + half * buckets :]
+    lines.append(jnp.where(own_second, second, first))
+    lines.append(jnp.where(own_second, first, second))
+    spare = weight_ref.shape[1] - heads * (levels + buckets)
+    if spare:
+        lines.append(jnp.zeros((spare, rows), F32))
+    weight_ref[...] = jnp.transpose(jnp.concatenate(lines, axis=0))
+
+
+def weight_columns(level_weight, prefix_weight):
+    heads, _, rows = level_weight.shape
     weights = heads * (level_weight.shape[1] + prefix_weight.shape[1])
     lines = jnp.concatenate(
         [
@@ -163,31 +183,26 @@
         ],
         axis=0,
     )
-    shapes = [queries.shape, keys.shape, values.shape, (per, *prefix_state.shape[1:])]
-    shapes += [(rows, pl.cdiv(weights, DH) * DH)]
-    shapes += [(PARTS * per, DH, DH)] + [(per, DH, DH)] * (PARTS + 1)
+    shape = (rows, pl.cdiv(weights, DH) * DH)
     return pl.pallas_call(
-        functools.partial(own_kernel, level_weight.shape[1], prefix_weight.shape[1]),
-        out_shape=[jax.ShapeDtypeStruct(s, F32) for s in shapes],
-        in_specs=[IN_VMEM] + [IN_HBM] * 4,
-        out_specs=[IN_VMEM] * len(shapes),
-        scratch_shapes=[pltpu.SemaphoreType.DMA((4, 2))],
-        compiler_params=pltpu.CompilerParams(vmem_limit_bytes=GRANT - 153 * rows * columns * 4 // 10),
-        cost_estimate=pl.CostEstimate(
-            flops=4 * rows * columns * DH, bytes_accessed=24 * rows * columns, transcendentals=0
-        ),
-        name="states_own",
-    )(lines, queries, keys, values, prefix_state)
-
-
-def base_kernel(place, levels, buckets, q_ref, k_ref, v_ref, weight_ref, prefix_ref, *refs):
+        functools.partial(columns_kernel, heads, level_weight.shape[1], prefix_weight.shape[1]),
+        out_shape=jax.ShapeDtypeStruct(shape, F32),
+        in_specs=[IN_VMEM],
+        out_specs=IN_VMEM,
+        compiler_params=pltpu.CompilerParams(vmem_limit_bytes=GRANT // 4),
+        cost_estimate=pl.CostEstimate(flops=0, bytes_accessed=8 * rows * DH, transcendentals=0),
+        name="columns",
+    )(lines)
+
+
+def base_kernel(place, levels, buckets, offset, q_ref, k_ref, v_ref, weight_ref, prefix_ref, *refs):
     rows = q_ref.shape[0]
     heads = q_ref.shape[1] // DH
-    per = prefix_ref.shape[0]
+    per = heads // (2 * PARTS)
     copy = None
     if len(refs) > 1:
         prefix_hbm, out_ref, next_ref, sem = refs
-        following = pl.ds(first_head(place + 1, per), per)
+        following = pl.ds(first_head(place + 1, per), next_ref.shape[0])
         copy = pltpu.make_async_copy(prefix_hbm.at[following], next_ref, sem)
         copy.start()
     else:
@@ -214,7 +229,7 @@
         for b in range(buckets):
             line = heads * levels + head * buckets + b
             total += through_state(
-                q * weight_ref[:, line : line + 1], prefix_ref[j, b * DH : (b + 1) * DH, :]
+                q * weight_ref[:, line : line + 1], prefix_ref[offset + j, b * DH : (b + 1) * DH, :]
             )
         out_ref[:, j * DH : (j + 1) * DH] = fold_columns(total)
     if copy is not None:
@@ -223,16 +238,18 @@
 
 def base_part(place, levels, buckets, loaded, prefix, prefix_state):
     rows, columns = loaded[0].shape
-    per = prefix.shape[0]
-    more = place + 1 < 2 * PARTS
-    shapes = [(rows, per * DH)] + [prefix.shape] * more
+    per = columns // DH // (2 * PARTS)
+    more = place < PARTS
+    offset = max(place - PARTS, 0) * per
+    ahead = PARTS * per if place == PARTS - 1 else per
+    shapes = [(rows, per * DH)] + [(ahead, *prefix.shape[1:])] * more
     return pl.pallas_call(
-        functools.partial(base_kernel, place, levels, buckets),
+        functools.partial(base_kernel, place, levels, buckets, offset),
         out_shape=[jax.ShapeDtypeStruct(s, F32) for s in shapes],
         in_specs=[IN_VMEM] * (len(loaded) + 1) + [IN_HBM] * more,
         out_specs=[IN_VMEM] * len(shapes),
         scratch_shapes=[pltpu.SemaphoreType.DMA] * more,
-        compiler_params=pltpu.CompilerParams(vmem_limit_bytes=GRANT - 17 * rows * columns * 4),
+        compiler_params=pltpu.CompilerParams(vmem_limit_bytes=GRANT - 185 * rows * columns * 4 // 10),
         cost_estimate=pl.CostEstimate(
             flops=2 * per * DH * rows * rows * 24,
             bytes_accessed=20 * rows * per * DH,
@@ -324,9 +341,8 @@
     places = range(PARTS)
 
     given = [given_states(keys, values)]
-    *loaded, prefix, weights, own, part0, part1, rest = own_block_states(
-        queries, keys, values, level_weight, prefix_weight, prefix_state
-    )
+    *loaded, prefix, own, part0, part1, rest = own_block_states(queries, keys, values, prefix_state)
+    weights = weight_columns(level_weight, prefix_weight)
     given.append(rest)
     received = [swapped(given[c], 0) for c in places]
     parts = (part0, part1)

time: 35.6 us -> 35.8 us (level)
  starting transfers between devices: 12.4 us -> 15.5 us
  waiting for transfers between devices: 7.36 us -> 5.52 us
  other arithmetic: 0.93 us -> 0.09 us
  Pallas kernels: 14.5 us -> 13.9 us
    ppermute x10, starting transfers between devices: 12.4 us -> 15.5 us  [swapped(): return lax.ppermute(array, ('seq', 'head'), pairs)]
    ppermute x10, waiting for transfers between devices: 7.36 us -> 5.52 us  [swapped(): return lax.ppermute(array, ('seq', 'head'), pairs)]
    concatenate x1, other arithmetic: 0.85 us -> 0.01 us  [weight_columns(): jnp.concatenate([jnp.transpose(level_weight, (1, 0, 2)).reshape(-1, rows)...]
    pallas_call x5 -> x6, Pallas kernels: 10 us -> 9.41 us  [the longest x4 7.04 us: base_part(): pl.pallas_call(functools.partial(base_kernel, place, levels, buckets, off...]
  transfers between devices with their start and end apart: 10 -> 10, of which waited for: 3 -> 3; matrix products, arithmetic and copies ran while one was open for 3% -> 0% of each run, Pallas kernels for 34% -> 30%
where the time goes in v7:
time: 35.8 us; the launch traced here: 35.2 us
  starting transfers between devices  15.5 us (43%)
  Pallas kernels  13.9 us (39%)
  waiting for transfers between devices  5.52 us (15%)
    ppermute x10, starting transfers between devices, swapped(): return lax.ppermute(array, ('seq', 'head'), pairs)  15.5 us
    pallas_call x4, Pallas kernels, base_part(): pl.pallas_call(functools.partial(base_kernel, place, levels, buckets, off...  7.04 us
    ppermute x10, waiting for transfers between devices, swapped(): return lax.ppermute(array, ('seq', 'head'), pairs)  5.52 us
    pallas_call x3, Pallas kernels, add_levels(): pl.pallas_call(functools.partial(levels_kernel, places, terms, len(states...  3.12 us
    pallas_call x1, Pallas kernels, own_block_states(): pl.pallas_call(own_kernel, out_shape=[jax.ShapeDtypeStruct(s, F32) for s...  2.27 us
    pallas_call x1, Pallas kernels, given_states(): pl.pallas_call(functools.partial(given_kernel, PARTS), out_shape=jax.Shap...  1.32 us
  transfers between devices with their start and end apart: 10, of which 3 were waited for; matrix products, arithmetic and copies ran while one was open for 0% of the time, Pallas kernels for 30%

profile of v7, /device:TPU:0, one launch (start us, length us, event | category | flops | bytes accessed | tf_op | source)
XLA Modules:
  0.0 35.2 jit_solution(15871055449093576732)
XLA Ops:
  0.0 2.3 %states_own.1 = (f32[256,1024]{1,0:T(8,128)S(1)}, f32[256,1024]{1,0:T(8,128)S(1)}, f32[256,1024]{1,0:T(8,128)S(1)}, f32[2,1024,128]{2,1,0:T(8,128)S(1)}, f32[4,1...) custom-call(f32[256,1024]{1,0:T(8,128)} %q_hbm.1, ...), custom_call_target="tpu_custom_call" | custom-call | flops 134217728 | bytes 6291456 | tf_op jit(solution)/shard_map/states_own/pallas_call | solution.py:141
  2.3 3.1 %collective-permute-start = (f32[2,128,128]{2,1,0:T(8,128)S(1)}, f32[2,128,128]{2,1,0:T(8,128)S(1)}, u32[]{:S(2)}, u32[]{:S(2)}) collective-permute-start(f32[2,128,128]{2,1,0:T(8,128)S(1)} %get-tuple-element.21), channel_id=1, source_target_pairs={{0,2},{1,3},{2,0},{3,1},{4,6},{5,7},{6,4},{7,5},{8,10},{9,11},{10,... | collective-permute-start | bytes 393224 | tf_op jit(solution)/shard_map/ppermute | solution.py:335
  5.3 1.3 %states_given.1 = f32[2,128,128]{2,1,0:T(8,128)S(1)} custom-call(f32[256,1024]{1,0:T(8,128)} %k_hbm.3, f32[256,1024]{1,0:T(8,128)} %v_hbm.3), custom_call_target="tpu_custom_call" | custom-call | flops 67108864 | bytes 524288 | tf_op jit(solution)/shard_map/states_given/pallas_call | solution.py:78
  6.7 0.1 collective-permute-start.5
  6.8 2.0 %collective-permute-start.4 = (f32[4,128,128]{2,1,0:T(8,128)S(1)}, f32[4,128,128]{2,1,0:T(8,128)S(1)}, u32[]{:S(2)}, u32[]{:S(2)}) collective-permute-start(f32[4,128,128]{2,1,0:T(8,128)S(1)} %get-tuple-element.22), channel_id=1, source_target_pairs={{0,2},{1,3},{2,0},{3,1},{4,6},{5,7},{6,4},{7,5},{8,10},{9,11},{10,... | collective-permute-start | bytes 786440 | tf_op jit(solution)/shard_map/ppermute | solution.py:335
  8.8 0.5 %collective-permute-done.refs_1_ = f32[2,128,128]{2,1,0:T(8,128)S(1)} collective-permute-done((f32[2,128,128]{2,1,0:T(8,128)S(1)}, f32[2,128,128]{2,1,0:T(8,128)S(1)}, u32[]{:S(2)}, u32[]{:S(2)}) %collective-permute-start) | collective-permute-done | bytes 131104 | tf_op jit(solution)/shard_map/ppermute | solution.py:335
  9.2 1.6 %collective-permute-start.1 = (f32[2,128,128]{2,1,0:T(8,128)S(1)}, f32[2,128,128]{2,1,0:T(8,128)S(1)}, u32[]{:S(2)}, u32[]{:S(2)}) collective-permute-start(f32[2,128,128]{2,1,0:T(8,128)S(1)} %add.12), channel_id=1, source_target_pairs={{0,4},{1,5},{2,6},{3,7},{4,0},{5,1},{6,2},{7,3},{8,12},{9,13},{10,... | collective-permute-start | bytes 393224 | tf_op jit(solution)/shard_map/ppermute | solution.py:335
  10.9 2.2 %collective-permute-done.5.refs_0_ = f32[2,128,128]{2,1,0:T(8,128)S(1)} collective-permute-done((f32[2,128,128]{2,1,0:T(8,128)S(1)}, f32[2,128,128]{2,1,0:T(8,128)S(1)}, u32[]{:S(2)}, u32[]{:S(2)}) %collective-permute-start.5) | collective-permute-done | bytes 131104 | tf_op jit(solution)/shard_map/ppermute | solution.py:335
  13.1 1.6 %collective-permute-start.6 = (f32[2,128,128]{2,1,0:T(8,128)S(1)}, f32[2,128,128]{2,1,0:T(8,128)S(1)}, u32[]{:S(2)}, u32[]{:S(2)}) collective-permute-start(f32[2,128,128]{2,1,0:T(8,128)S(1)} %add.14), channel_id=1, source_target_pairs={{0,4},{1,5},{2,6},{3,7},{4,0},{5,1},{6,2},{7,3},{8,12},{9,13},{10,... | collective-permute-start | bytes 393224 | tf_op jit(solution)/shard_map/ppermute | solution.py:335
  14.8 0.0 copy-done.1
  14.8 0.0 copy-done
  14.8 0.1 columns.1.weight_ref
  14.9 2.2 %shard_map.64 = (f32[256,256]{1,0:T(8,128)S(1)}, f32[2,1024,128]{2,1,0:T(8,128)S(1)}) custom-call(f32[256,1024]{1,0:T(8,128)S(1)} %get-tuple-element.19.q_ref, f32[256,1024]{1,0:T(8,128)S(1)} %get-tuple-element.24.k_ref, f32[256,1024]{1,0:T(8,128)S(1)} %get-tuple-element.25.v_ref, f32[256,128]{1,0:T(8,128)S(1)} %columns.1.weight_ref, ...), custom_call_target="tpu_custom_call" | custom-call | flops 805306368 | bytes 1310720 | tf_op jit(solution)/shard_map/pallas_call | solution.py:246
  17.1 0.0 collective-permute-done.1.refs_3_
  17.2 2.7 %collective-permute-start.2 = (f32[2,128,128]{2,1,0:T(8,128)S(1)}, f32[2,128,128]{2,1,0:T(8,128)S(1)}, u32[]{:S(2)}, u32[]{:S(2)}) collective-permute-start(f32[2,128,128]{2,1,0:T(8,128)S(1)} %add.13), channel_id=1, source_target_pairs={{0,8},{1,9},{2,10},{3,11},{4,12},{5,13},{6,14},{7,15},{8,0},{9,1},... | collective-permute-start | bytes 393224 | tf_op jit(solution)/shard_map/ppermute | solution.py:335
  19.8 0.0 collective-permute-done.6.refs_2_
  19.8 1.8 %collective-permute-start.8 = (f32[2,128,128]{2,1,0:T(8,128)S(1)}, f32[2,128,128]{2,1,0:T(8,128)S(1)}, u32[]{:S(2)}, u32[]{:S(2)}) collective-permute-start(f32[2,128,128]{2,1,0:T(8,128)S(1)} %add.15), channel_id=1, source_target_pairs={{0,8},{1,9},{2,10},{3,11},{4,12},{5,13},{6,14},{7,15},{8,0},{9,1},... | collective-permute-start | bytes 393224 | tf_op jit(solution)/shard_map/ppermute | solution.py:335
  21.7 2.0 %collective-permute-start.7 = (f32[4,128,128]{2,1,0:T(8,128)S(1)}, f32[4,128,128]{2,1,0:T(8,128)S(1)}, u32[]{:S(2)}, u32[]{:S(2)}) collective-permute-start(f32[4,128,128]{2,1,0:T(8,128)S(1)} %pad_maximum_fusion), channel_id=1, source_target_pairs={{0,2},{1,3},{2,0},{3,1},{4,6},{5,7},{6,4},{7,5},{8,10},{9,11},{10,... | collective-permute-start | bytes 786440 | tf_op jit(solution)/shard_map/ppermute | solution.py:335
  23.7 2.6 %shard_map.65 = (f32[256,256]{1,0:T(8,128)S(1)}, f32[4,1024,128]{2,1,0:T(8,128)S(1)}) custom-call(f32[256,1024]{1,0:T(8,128)S(1)} %get-tuple-element.19.q_ref, f32[256,1024]{1,0:T(8,128)S(1)} %get-tuple-element.24.k_ref, f32[256,1024]{1,0:T(8,128)S(1)} %get-tuple-element.25.v_ref, f32[256,128]{1,0:T(8,128)S(1)} %columns.1.weight_ref, ...), custom_call_target="tpu_custom_call" | custom-call | flops 805306368 | bytes 1310720 | tf_op jit(solution)/shard_map/pallas_call | solution.py:246
  26.3 2.8 %collective-permute-done.8.refs_4_ = f32[2,128,128]{2,1,0:T(8,128)S(1)} collective-permute-done((f32[2,128,128]{2,1,0:T(8,128)S(1)}, f32[2,128,128]{2,1,0:T(8,128)S(1)}, u32[]{:S(2)}, u32[]{:S(2)}) %collective-permute-start.8) | collective-permute-done | bytes 131104 | tf_op jit(solution)/shard_map/ppermute | solution.py:335
  29.1 0.0 collective-permute-start.9
  29.1 1.1 %shard_map.67.refs_4_ = f32[256,256]{1,0:T(8,128)S(1)} custom-call(f32[256,1024]{1,0:T(8,128)S(1)} %get-tuple-element.19.q_ref, f32[256,1024]{1,0:T(8,128)S(1)} %get-tuple-element.24.k_ref, f32[256,1024]{1,0:T(8,128)S(1)} %get-tuple-element.25.v_ref, f32[256,128]{1,0:T(8,128)S(1)} %columns.1.weight_ref, f32[4,1024,128]{2,1,0:T(8,128)S(1)} %get-tuple-element.28.prefix_ref), custom_call_target="tpu_custom_call" | custom-call | flops 805306368 | bytes 1310720 | tf_op jit(solution)/shard_map/pallas_call | solution.py:246
  30.3 0.0 collective-permute-done.2.refs_5_
  30.3 0.6 %collective-permute-start.3 = (f32[2,128,128]{2,1,0:T(8,128)S(1)}, f32[2,128,128]{2,1,0:T(8,128)S(1)}, u32[]{:S(2)}, u32[]{:S(2)}) collective-permute-start(f32[2,128,128]{2,1,0:T(8,128)S(1)} %collective-permute-done.2.refs_5_), channel_id=1, source_target_pairs={{0,1},{1,0},{2,3},{3,2},{4,5},{5,4},{6,7},{7,6},{8,10},{9,11},{10,... | collective-permute-start | bytes 393224 | tf_op jit(solution)/shard_map/ppermute | solution.py:335
  30.9 1.1 %shard_map.66.refs_3_ = f32[256,256]{1,0:T(8,128)S(1)} custom-call(f32[256,1024]{1,0:T(8,128)S(1)} %get-tuple-element.19.q_ref, f32[256,1024]{1,0:T(8,128)S(1)} %get-tuple-element.24.k_ref, f32[256,1024]{1,0:T(8,128)S(1)} %get-tuple-element.25.v_ref, f32[256,128]{1,0:T(8,128)S(1)} %columns.1.weight_ref, f32[4,1024,128]{2,1,0:T(8,128)S(1)} %get-tuple-element.28.prefix_ref), custom_call_target="tpu_custom_call" | custom-call | flops 805306368 | bytes 1310720 | tf_op jit(solution)/shard_map/pallas_call | solution.py:246
  32.0 1.5 %shard_map.69.refs_3_ = f32[256,1024]{1,0:T(8,128)} custom-call(f32[256,1024]{1,0:T(8,128)S(1)} %get-tuple-element.19.q_ref, f32[256,128]{1,0:T(8,128)S(1)} %columns.1.weight_ref, f32[2,128,128]{2,1,0:T(8,128)S(1)} %collective-permute-done.5.refs_0_, f32[2,128,128]{2,1,0:T(8,128)S(1)} %collective-permute-done.refs_1_, ...), custom_call_target="tpu_custom_call" | custom-call | flops 402653184 | bytes 1572864 | tf_op jit(solution)/shard_map/pallas_call | solution.py:307
  33.4 0.0 collective-permute-done.4.refs_0_
  33.5 0.0 collective-permute-done.7.refs_1_
  33.5 0.0 collective-permute-done.9.refs_2_
  33.5 0.6 %shard_map.68 = (f32[256,256]{1,0:T(8,128)S(1)}, f32[256,256]{1,0:T(8,128)S(1)}) custom-call(f32[256,1024]{1,0:T(8,128)S(1)} %get-tuple-element.19.q_ref, f32[256,128]{1,0:T(8,128)S(1)} %columns.1.weight_ref, f32[4,128,128]{2,1,0:T(8,128)S(1)} %collective-permute-done.4.refs_0_, f32[4,128,128]{2,1,0:T(8,128)S(1)} %collective-permute-done.7.refs_1_, ...), custom_call_target="tpu_custom_call" | custom-call | flops 335544320 | bytes 1572864 | tf_op jit(solution)/shard_map/pallas_call | solution.py:307
  34.1 0.0 collective-permute-done.3.refs_0_
  34.1 1.0 %shard_map.70 = f32[256,1024]{1,0:T(8,128)} custom-call(f32[256,1024]{1,0:T(8,128)S(1)} %get-tuple-element.19.q_ref, f32[256,128]{1,0:T(8,128)S(1)} %columns.1.weight_ref, f32[2,128,128]{2,1,0:T(8,128)S(1)} %collective-permute-done.3.refs_0_, f32[256,256]{1,0:T(8,128)S(1)} %get-tuple-element.29.refs_1_, ...), custom_call_target="tpu_custom_call", output_to_operand_aliasing={{}: (5, {})} | custom-call | flops 67108864 | bytes 1572864 | tf_op jit(solution)/shard_map/pallas_call | solution.py:307
  (8 shorter events, 0.1 us)
Async XLA Ops:
  0.0 14.8 %copy-start.1 = (f32[8,6,256]{2,0,1:T(8,128)S(1)}, f32[8,6,256]{2,0,1:T(8,128)}, u32[]{:S(2)}) copy-start(f32[8,6,256]{2,0,1:T(8,128)} %param.9) | copy-start | bytes 147460
  0.0 14.8 %copy-start = (f32[8,8,256]{2,1,0:T(8,128)S(1)}, f32[8,8,256]{2,1,0:T(8,128)}, u32[]{:S(2)}) copy-start(f32[8,8,256]{2,1,0:T(8,128)} %param.10) | copy-start | bytes 196612
  2.3 6.9 %collective-permute-start = (f32[2,128,128]{2,1,0:T(8,128)S(1)}, f32[2,128,128]{2,1,0:T(8,128)S(1)}, u32[]{:S(2)}, u32[]{:S(2)}) collective-permute-start(f32[2,128,128]{2,1,0:T(8,128)S(1)} %get-tuple-element.21), channel_id=1, source_target_pairs={{0,2},{1,3},{2,0},{3,1},{4,6},{5,7},{6,4},{7,5},{8,10},{9,11},{10,... | collective-permute-start | bytes 393224 | tf_op jit(solution)/shard_map/ppermute | solution.py:335
  6.7 6.4 %collective-permute-start.5 = (f32[2,128,128]{2,1,0:T(8,128)S(1)}, f32[2,128,128]{2,1,0:T(8,128)S(1)}, u32[]{:S(2)}, u32[]{:S(2)}) collective-permute-start(f32[2,128,128]{2,1,0:T(8,128)S(1)} %states_given.1), channel_id=1, source_target_pairs={{0,2},{1,3},{2,0},{3,1},{4,6},{5,7},{6,4},{7,5},{8,10},{9,11},{10,... | collective-permute-start | bytes 393224 | tf_op jit(solution)/shard_map/ppermute | solution.py:335
  6.8 26.7 %collective-permute-start.4 = (f32[4,128,128]{2,1,0:T(8,128)S(1)}, f32[4,128,128]{2,1,0:T(8,128)S(1)}, u32[]{:S(2)}, u32[]{:S(2)}) collective-permute-start(f32[4,128,128]{2,1,0:T(8,128)S(1)} %get-tuple-element.22), channel_id=1, source_target_pairs={{0,2},{1,3},{2,0},{3,1},{4,6},{5,7},{6,4},{7,5},{8,10},{9,11},{10,... | collective-permute-start | bytes 786440 | tf_op jit(solution)/shard_map/ppermute | solution.py:335
  9.2 7.9 %collective-permute-start.1 = (f32[2,128,128]{2,1,0:T(8,128)S(1)}, f32[2,128,128]{2,1,0:T(8,128)S(1)}, u32[]{:S(2)}, u32[]{:S(2)}) collective-permute-start(f32[2,128,128]{2,1,0:T(8,128)S(1)} %add.12), channel_id=1, source_target_pairs={{0,4},{1,5},{2,6},{3,7},{4,0},{5,1},{6,2},{7,3},{8,12},{9,13},{10,... | collective-permute-start | bytes 393224 | tf_op jit(solution)/shard_map/ppermute | solution.py:335
  13.1 6.7 %collective-permute-start.6 = (f32[2,128,128]{2,1,0:T(8,128)S(1)}, f32[2,128,128]{2,1,0:T(8,128)S(1)}, u32[]{:S(2)}, u32[]{:S(2)}) collective-permute-start(f32[2,128,128]{2,1,0:T(8,128)S(1)} %add.14), channel_id=1, source_target_pairs={{0,4},{1,5},{2,6},{3,7},{4,0},{5,1},{6,2},{7,3},{8,12},{9,13},{10,... | collective-permute-start | bytes 393224 | tf_op jit(solution)/shard_map/ppermute | solution.py:335
  17.2 13.1 %collective-permute-start.2 = (f32[2,128,128]{2,1,0:T(8,128)S(1)}, f32[2,128,128]{2,1,0:T(8,128)S(1)}, u32[]{:S(2)}, u32[]{:S(2)}) collective-permute-start(f32[2,128,128]{2,1,0:T(8,128)S(1)} %add.13), channel_id=1, source_target_pairs={{0,8},{1,9},{2,10},{3,11},{4,12},{5,13},{6,14},{7,15},{8,0},{9,1},... | collective-permute-start | bytes 393224 | tf_op jit(solution)/shard_map/ppermute | solution.py:335
  19.8 9.3 %collective-permute-start.8 = (f32[2,128,128]{2,1,0:T(8,128)S(1)}, f32[2,128,128]{2,1,0:T(8,128)S(1)}, u32[]{:S(2)}, u32[]{:S(2)}) collective-permute-start(f32[2,128,128]{2,1,0:T(8,128)S(1)} %add.15), channel_id=1, source_target_pairs={{0,8},{1,9},{2,10},{3,11},{4,12},{5,13},{6,14},{7,15},{8,0},{9,1},... | collective-permute-start | bytes 393224 | tf_op jit(solution)/shard_map/ppermute | solution.py:335
  21.7 11.8 %collective-permute-start.7 = (f32[4,128,128]{2,1,0:T(8,128)S(1)}, f32[4,128,128]{2,1,0:T(8,128)S(1)}, u32[]{:S(2)}, u32[]{:S(2)}) collective-permute-start(f32[4,128,128]{2,1,0:T(8,128)S(1)} %pad_maximum_fusion), channel_id=1, source_target_pairs={{0,2},{1,3},{2,0},{3,1},{4,6},{5,7},{6,4},{7,5},{8,10},{9,11},{10,... | collective-permute-start | bytes 786440 | tf_op jit(solution)/shard_map/ppermute | solution.py:335
  29.1 4.3 %collective-permute-start.9 = (f32[2,128,128]{2,1,0:T(8,128)S(1)}, f32[2,128,128]{2,1,0:T(8,128)S(1)}, u32[]{:S(2)}, u32[]{:S(2)}) collective-permute-start(f32[2,128,128]{2,1,0:T(8,128)S(1)} %collective-permute-done.8.refs_4_), channel_id=1, source_target_pairs={{0,1},{1,0},{2,3},{3,2},{4,5},{5,4},{6,7},{7,6},{8,10},{9,11},{10,... | collective-permute-start | bytes 393224 | tf_op jit(solution)/shard_map/ppermute | solution.py:335
  30.3 3.8 %collective-permute-start.3 = (f32[2,128,128]{2,1,0:T(8,128)S(1)}, f32[2,128,128]{2,1,0:T(8,128)S(1)}, u32[]{:S(2)}, u32[]{:S(2)}) collective-permute-start(f32[2,128,128]{2,1,0:T(8,128)S(1)} %collective-permute-done.2.refs_5_), channel_id=1, source_target_pairs={{0,1},{1,0},{2,3},{3,2},{4,5},{5,4},{6,7},{7,6},{8,10},{9,11},{10,... | collective-permute-start | bytes 393224 | tf_op jit(solution)/shard_map/ppermute | solution.py:335

commit v8 on v7

--- a/solution.py
+++ b/solution.py
@@ -281,13 +281,12 @@
                 done += fold_columns(total)
             if store:
                 buf[c, :, at] = done
+                columns = head_columns(first_head(place, per) + j)
+                copy = pltpu.make_async_copy(buf.at[c, :, at], out_hbm.at[:, columns], sems.at[c, j])
+                copy.start()
+                copies.append(copy)
             else:
                 refs[c][:, at] = done
-        if store:
-            columns = head_columns(first_head(place, per), per)
-            copy = pltpu.make_async_copy(buf.at[c], out_hbm.at[:, columns], sems.at[c])
-            copy.start()
-            copies.append(copy)
     for copy in copies:
         copy.wait()
 
@@ -309,7 +308,7 @@
         out_shape=[jax.ShapeDtypeStruct(shape, F32)] * (1 if store else count),
         in_specs=in_specs,
         out_specs=[IN_HBM if store else IN_VMEM] * (1 if store else count),
-        scratch_shapes=[pltpu.VMEM((count, rows, width), F32), pltpu.SemaphoreType.DMA((count,))]
+        scratch_shapes=[pltpu.VMEM((count, rows, width), F32), pltpu.SemaphoreType.DMA((count, width // DH))]
         if store
         else [],
         input_output_aliases=aliases,

time: 35.8 us -> 35.8 us (level)
  no operation moved by 1% of the time
where the time goes in v8:
time: 35.8 us; the launch traced here: 35.1 us
  starting transfers between devices  15.5 us (43%)
  Pallas kernels  13.8 us (39%)
  waiting for transfers between devices  5.52 us (15%)
    ppermute x10, starting transfers between devices, swapped(): return lax.ppermute(array, ('seq', 'head'), pairs)  15.5 us
    pallas_call x4, Pallas kernels, base_part(): pl.pallas_call(functools.partial(base_kernel, place, levels, buckets, off...  7.04 us
    ppermute x10, waiting for transfers between devices, swapped(): return lax.ppermute(array, ('seq', 'head'), pairs)  5.52 us
    pallas_call x3, Pallas kernels, add_levels(): pl.pallas_call(functools.partial(levels_kernel, places, terms, len(states...  3.1 us
    pallas_call x1, Pallas kernels, own_block_states(): pl.pallas_call(own_kernel, out_shape=[jax.ShapeDtypeStruct(s, F32) for s...  2.27 us
    pallas_call x1, Pallas kernels, given_states(): pl.pallas_call(functools.partial(given_kernel, PARTS), out_shape=jax.Shap...  1.32 us
  transfers between devices with their start and end apart: 10, of which 3 were waited for; matrix products, arithmetic and copies ran while one was open for 0% of the time, Pallas kernels for 30%

profile of v8, /device:TPU:0, one launch (start us, length us, event | category | flops | bytes accessed | tf_op | source)
XLA Modules:
  0.0 35.1 jit_solution(10923457708718641761)
XLA Ops:
  0.0 2.3 %states_own.1 = (f32[256,1024]{1,0:T(8,128)S(1)}, f32[256,1024]{1,0:T(8,128)S(1)}, f32[256,1024]{1,0:T(8,128)S(1)}, f32[2,1024,128]{2,1,0:T(8,128)S(1)}, f32[4,1...) custom-call(f32[256,1024]{1,0:T(8,128)} %q_hbm.1, ...), custom_call_target="tpu_custom_call" | custom-call | flops 134217728 | bytes 6291456 | tf_op jit(solution)/shard_map/states_own/pallas_call | solution.py:141
  2.3 3.1 %collective-permute-start = (f32[2,128,128]{2,1,0:T(8,128)S(1)}, f32[2,128,128]{2,1,0:T(8,128)S(1)}, u32[]{:S(2)}, u32[]{:S(2)}) collective-permute-start(f32[2,128,128]{2,1,0:T(8,128)S(1)} %get-tuple-element.21), channel_id=1, source_target_pairs={{0,2},{1,3},{2,0},{3,1},{4,6},{5,7},{6,4},{7,5},{8,10},{9,11},{10,... | collective-permute-start | bytes 393224 | tf_op jit(solution)/shard_map/ppermute | solution.py:334
  5.3 1.3 %states_given.1 = f32[2,128,128]{2,1,0:T(8,128)S(1)} custom-call(f32[256,1024]{1,0:T(8,128)} %k_hbm.3, f32[256,1024]{1,0:T(8,128)} %v_hbm.3), custom_call_target="tpu_custom_call" | custom-call | flops 67108864 | bytes 524288 | tf_op jit(solution)/shard_map/states_given/pallas_call | solution.py:78
  6.7 0.1 collective-permute-start.5
  6.8 2.0 %collective-permute-start.4 = (f32[4,128,128]{2,1,0:T(8,128)S(1)}, f32[4,128,128]{2,1,0:T(8,128)S(1)}, u32[]{:S(2)}, u32[]{:S(2)}) collective-permute-start(f32[4,128,128]{2,1,0:T(8,128)S(1)} %get-tuple-element.22), channel_id=1, source_target_pairs={{0,2},{1,3},{2,0},{3,1},{4,6},{5,7},{6,4},{7,5},{8,10},{9,11},{10,... | collective-permute-start | bytes 786440 | tf_op jit(solution)/shard_map/ppermute | solution.py:334
  8.8 0.5 %collective-permute-done.refs_1_ = f32[2,128,128]{2,1,0:T(8,128)S(1)} collective-permute-done((f32[2,128,128]{2,1,0:T(8,128)S(1)}, f32[2,128,128]{2,1,0:T(8,128)S(1)}, u32[]{:S(2)}, u32[]{:S(2)}) %collective-permute-start) | collective-permute-done | bytes 131104 | tf_op jit(solution)/shard_map/ppermute | solution.py:334
  9.2 1.6 %collective-permute-start.1 = (f32[2,128,128]{2,1,0:T(8,128)S(1)}, f32[2,128,128]{2,1,0:T(8,128)S(1)}, u32[]{:S(2)}, u32[]{:S(2)}) collective-permute-start(f32[2,128,128]{2,1,0:T(8,128)S(1)} %add.12), channel_id=1, source_target_pairs={{0,4},{1,5},{2,6},{3,7},{4,0},{5,1},{6,2},{7,3},{8,12},{9,13},{10,... | collective-permute-start | bytes 393224 | tf_op jit(solution)/shard_map/ppermute | solution.py:334
  10.9 2.2 %collective-permute-done.5.refs_0_ = f32[2,128,128]{2,1,0:T(8,128)S(1)} collective-permute-done((f32[2,128,128]{2,1,0:T(8,128)S(1)}, f32[2,128,128]{2,1,0:T(8,128)S(1)}, u32[]{:S(2)}, u32[]{:S(2)}) %collective-permute-start.5) | collective-permute-done | bytes 131104 | tf_op jit(solution)/shard_map/ppermute | solution.py:334
  13.1 1.6 %collective-permute-start.6 = (f32[2,128,128]{2,1,0:T(8,128)S(1)}, f32[2,128,128]{2,1,0:T(8,128)S(1)}, u32[]{:S(2)}, u32[]{:S(2)}) collective-permute-start(f32[2,128,128]{2,1,0:T(8,128)S(1)} %add.14), channel_id=1, source_target_pairs={{0,4},{1,5},{2,6},{3,7},{4,0},{5,1},{6,2},{7,3},{8,12},{9,13},{10,... | collective-permute-start | bytes 393224 | tf_op jit(solution)/shard_map/ppermute | solution.py:334
  14.8 0.0 copy-done.1
  14.8 0.0 copy-done
  14.8 0.1 columns.1.weight_ref
  14.9 2.2 %shard_map.64 = (f32[256,256]{1,0:T(8,128)S(1)}, f32[2,1024,128]{2,1,0:T(8,128)S(1)}) custom-call(f32[256,1024]{1,0:T(8,128)S(1)} %get-tuple-element.19.q_ref, f32[256,1024]{1,0:T(8,128)S(1)} %get-tuple-element.24.k_ref, f32[256,1024]{1,0:T(8,128)S(1)} %get-tuple-element.25.v_ref, f32[256,128]{1,0:T(8,128)S(1)} %columns.1.weight_ref, ...), custom_call_target="tpu_custom_call" | custom-call | flops 805306368 | bytes 1310720 | tf_op jit(solution)/shard_map/pallas_call | solution.py:246
  17.1 0.0 collective-permute-done.1.refs_3_
  17.2 2.7 %collective-permute-start.2 = (f32[2,128,128]{2,1,0:T(8,128)S(1)}, f32[2,128,128]{2,1,0:T(8,128)S(1)}, u32[]{:S(2)}, u32[]{:S(2)}) collective-permute-start(f32[2,128,128]{2,1,0:T(8,128)S(1)} %add.13), channel_id=1, source_target_pairs={{0,8},{1,9},{2,10},{3,11},{4,12},{5,13},{6,14},{7,15},{8,0},{9,1},... | collective-permute-start | bytes 393224 | tf_op jit(solution)/shard_map/ppermute | solution.py:334
  19.8 0.0 collective-permute-done.6.refs_2_
  19.8 1.8 %collective-permute-start.8 = (f32[2,128,128]{2,1,0:T(8,128)S(1)}, f32[2,128,128]{2,1,0:T(8,128)S(1)}, u32[]{:S(2)}, u32[]{:S(2)}) collective-permute-start(f32[2,128,128]{2,1,0:T(8,128)S(1)} %add.15), channel_id=1, source_target_pairs={{0,8},{1,9},{2,10},{3,11},{4,12},{5,13},{6,14},{7,15},{8,0},{9,1},... | collective-permute-start | bytes 393224 | tf_op jit(solution)/shard_map/ppermute | solution.py:334
  21.7 2.0 %collective-permute-start.7 = (f32[4,128,128]{2,1,0:T(8,128)S(1)}, f32[4,128,128]{2,1,0:T(8,128)S(1)}, u32[]{:S(2)}, u32[]{:S(2)}) collective-permute-start(f32[4,128,128]{2,1,0:T(8,128)S(1)} %pad_maximum_fusion), channel_id=1, source_target_pairs={{0,2},{1,3},{2,0},{3,1},{4,6},{5,7},{6,4},{7,5},{8,10},{9,11},{10,... | collective-permute-start | bytes 786440 | tf_op jit(solution)/shard_map/ppermute | solution.py:334
  23.7 2.6 %shard_map.65 = (f32[256,256]{1,0:T(8,128)S(1)}, f32[4,1024,128]{2,1,0:T(8,128)S(1)}) custom-call(f32[256,1024]{1,0:T(8,128)S(1)} %get-tuple-element.19.q_ref, f32[256,1024]{1,0:T(8,128)S(1)} %get-tuple-element.24.k_ref, f32[256,1024]{1,0:T(8,128)S(1)} %get-tuple-element.25.v_ref, f32[256,128]{1,0:T(8,128)S(1)} %columns.1.weight_ref, ...), custom_call_target="tpu_custom_call" | custom-call | flops 805306368 | bytes 1310720 | tf_op jit(solution)/shard_map/pallas_call | solution.py:246
  26.3 2.8 %collective-permute-done.8.refs_4_ = f32[2,128,128]{2,1,0:T(8,128)S(1)} collective-permute-done((f32[2,128,128]{2,1,0:T(8,128)S(1)}, f32[2,128,128]{2,1,0:T(8,128)S(1)}, u32[]{:S(2)}, u32[]{:S(2)}) %collective-permute-start.8) | collective-permute-done | bytes 131104 | tf_op jit(solution)/shard_map/ppermute | solution.py:334
  29.1 0.0 collective-permute-start.9
  29.1 1.1 %shard_map.67.refs_4_ = f32[256,256]{1,0:T(8,128)S(1)} custom-call(f32[256,1024]{1,0:T(8,128)S(1)} %get-tuple-element.19.q_ref, f32[256,1024]{1,0:T(8,128)S(1)} %get-tuple-element.24.k_ref, f32[256,1024]{1,0:T(8,128)S(1)} %get-tuple-element.25.v_ref, f32[256,128]{1,0:T(8,128)S(1)} %columns.1.weight_ref, f32[4,1024,128]{2,1,0:T(8,128)S(1)} %get-tuple-element.28.prefix_ref), custom_call_target="tpu_custom_call" | custom-call | flops 805306368 | bytes 1310720 | tf_op jit(solution)/shard_map/pallas_call | solution.py:246
  30.3 0.0 collective-permute-done.2.refs_5_
  30.3 0.6 %collective-permute-start.3 = (f32[2,128,128]{2,1,0:T(8,128)S(1)}, f32[2,128,128]{2,1,0:T(8,128)S(1)}, u32[]{:S(2)}, u32[]{:S(2)}) collective-permute-start(f32[2,128,128]{2,1,0:T(8,128)S(1)} %collective-permute-done.2.refs_5_), channel_id=1, source_target_pairs={{0,1},{1,0},{2,3},{3,2},{4,5},{5,4},{6,7},{7,6},{8,10},{9,11},{10,... | collective-permute-start | bytes 393224 | tf_op jit(solution)/shard_map/ppermute | solution.py:334
  30.9 1.1 %shard_map.66.refs_3_ = f32[256,256]{1,0:T(8,128)S(1)} custom-call(f32[256,1024]{1,0:T(8,128)S(1)} %get-tuple-element.19.q_ref, f32[256,1024]{1,0:T(8,128)S(1)} %get-tuple-element.24.k_ref, f32[256,1024]{1,0:T(8,128)S(1)} %get-tuple-element.25.v_ref, f32[256,128]{1,0:T(8,128)S(1)} %columns.1.weight_ref, f32[4,1024,128]{2,1,0:T(8,128)S(1)} %get-tuple-element.28.prefix_ref), custom_call_target="tpu_custom_call" | custom-call | flops 805306368 | bytes 1310720 | tf_op jit(solution)/shard_map/pallas_call | solution.py:246
  32.0 1.4 %shard_map.69.refs_3_ = f32[256,1024]{1,0:T(8,128)} custom-call(f32[256,1024]{1,0:T(8,128)S(1)} %get-tuple-element.19.q_ref, f32[256,128]{1,0:T(8,128)S(1)} %columns.1.weight_ref, f32[2,128,128]{2,1,0:T(8,128)S(1)} %collective-permute-done.5.refs_0_, f32[2,128,128]{2,1,0:T(8,128)S(1)} %collective-permute-done.refs_1_, ...), custom_call_target="tpu_custom_call" | custom-call | flops 402653184 | bytes 1572864 | tf_op jit(solution)/shard_map/pallas_call | solution.py:306
  33.4 0.0 collective-permute-done.4.refs_0_
  33.4 0.0 collective-permute-done.7.refs_1_
  33.4 0.0 collective-permute-done.9.refs_2_
  33.5 0.6 %shard_map.68 = (f32[256,256]{1,0:T(8,128)S(1)}, f32[256,256]{1,0:T(8,128)S(1)}) custom-call(f32[256,1024]{1,0:T(8,128)S(1)} %get-tuple-element.19.q_ref, f32[256,128]{1,0:T(8,128)S(1)} %columns.1.weight_ref, f32[4,128,128]{2,1,0:T(8,128)S(1)} %collective-permute-done.4.refs_0_, f32[4,128,128]{2,1,0:T(8,128)S(1)} %collective-permute-done.7.refs_1_, ...), custom_call_target="tpu_custom_call" | custom-call | flops 335544320 | bytes 1572864 | tf_op jit(solution)/shard_map/pallas_call | solution.py:306
  34.1 0.0 collective-permute-done.3.refs_0_
  34.1 1.0 %shard_map.70 = f32[256,1024]{1,0:T(8,128)} custom-call(f32[256,1024]{1,0:T(8,128)S(1)} %get-tuple-element.19.q_ref, f32[256,128]{1,0:T(8,128)S(1)} %columns.1.weight_ref, f32[2,128,128]{2,1,0:T(8,128)S(1)} %collective-permute-done.3.refs_0_, f32[256,256]{1,0:T(8,128)S(1)} %get-tuple-element.29.refs_1_, ...), custom_call_target="tpu_custom_call", output_to_operand_aliasing={{}: (5, {})} | custom-call | flops 67108864 | bytes 1572864 | tf_op jit(solution)/shard_map/pallas_call | solution.py:306
  (8 shorter events, 0.1 us)
Async XLA Ops:
  0.0 14.8 %copy-start.1 = (f32[8,6,256]{2,0,1:T(8,128)S(1)}, f32[8,6,256]{2,0,1:T(8,128)}, u32[]{:S(2)}) copy-start(f32[8,6,256]{2,0,1:T(8,128)} %param.9) | copy-start | bytes 147460
  0.0 14.8 %copy-start = (f32[8,8,256]{2,1,0:T(8,128)S(1)}, f32[8,8,256]{2,1,0:T(8,128)}, u32[]{:S(2)}) copy-start(f32[8,8,256]{2,1,0:T(8,128)} %param.10) | copy-start | bytes 196612
  2.3 6.9 %collective-permute-start = (f32[2,128,128]{2,1,0:T(8,128)S(1)}, f32[2,128,128]{2,1,0:T(8,128)S(1)}, u32[]{:S(2)}, u32[]{:S(2)}) collective-permute-start(f32[2,128,128]{2,1,0:T(8,128)S(1)} %get-tuple-element.21), channel_id=1, source_target_pairs={{0,2},{1,3},{2,0},{3,1},{4,6},{5,7},{6,4},{7,5},{8,10},{9,11},{10,... | collective-permute-start | bytes 393224 | tf_op jit(solution)/shard_map/ppermute | solution.py:334
  6.7 6.4 %collective-permute-start.5 = (f32[2,128,128]{2,1,0:T(8,128)S(1)}, f32[2,128,128]{2,1,0:T(8,128)S(1)}, u32[]{:S(2)}, u32[]{:S(2)}) collective-permute-start(f32[2,128,128]{2,1,0:T(8,128)S(1)} %states_given.1), channel_id=1, source_target_pairs={{0,2},{1,3},{2,0},{3,1},{4,6},{5,7},{6,4},{7,5},{8,10},{9,11},{10,... | collective-permute-start | bytes 393224 | tf_op jit(solution)/shard_map/ppermute | solution.py:334
  6.8 26.7 %collective-permute-start.4 = (f32[4,128,128]{2,1,0:T(8,128)S(1)}, f32[4,128,128]{2,1,0:T(8,128)S(1)}, u32[]{:S(2)}, u32[]{:S(2)}) collective-permute-start(f32[4,128,128]{2,1,0:T(8,128)S(1)} %get-tuple-element.22), channel_id=1, source_target_pairs={{0,2},{1,3},{2,0},{3,1},{4,6},{5,7},{6,4},{7,5},{8,10},{9,11},{10,... | collective-permute-start | bytes 786440 | tf_op jit(solution)/shard_map/ppermute | solution.py:334
  9.2 7.9 %collective-permute-start.1 = (f32[2,128,128]{2,1,0:T(8,128)S(1)}, f32[2,128,128]{2,1,0:T(8,128)S(1)}, u32[]{:S(2)}, u32[]{:S(2)}) collective-permute-start(f32[2,128,128]{2,1,0:T(8,128)S(1)} %add.12), channel_id=1, source_target_pairs={{0,4},{1,5},{2,6},{3,7},{4,0},{5,1},{6,2},{7,3},{8,12},{9,13},{10,... | collective-permute-start | bytes 393224 | tf_op jit(solution)/shard_map/ppermute | solution.py:334
  13.1 6.7 %collective-permute-start.6 = (f32[2,128,128]{2,1,0:T(8,128)S(1)}, f32[2,128,128]{2,1,0:T(8,128)S(1)}, u32[]{:S(2)}, u32[]{:S(2)}) collective-permute-start(f32[2,128,128]{2,1,0:T(8,128)S(1)} %add.14), channel_id=1, source_target_pairs={{0,4},{1,5},{2,6},{3,7},{4,0},{5,1},{6,2},{7,3},{8,12},{9,13},{10,... | collective-permute-start | bytes 393224 | tf_op jit(solution)/shard_map/ppermute | solution.py:334
  17.2 13.1 %collective-permute-start.2 = (f32[2,128,128]{2,1,0:T(8,128)S(1)}, f32[2,128,128]{2,1,0:T(8,128)S(1)}, u32[]{:S(2)}, u32[]{:S(2)}) collective-permute-start(f32[2,128,128]{2,1,0:T(8,128)S(1)} %add.13), channel_id=1, source_target_pairs={{0,8},{1,9},{2,10},{3,11},{4,12},{5,13},{6,14},{7,15},{8,0},{9,1},... | collective-permute-start | bytes 393224 | tf_op jit(solution)/shard_map/ppermute | solution.py:334
  19.8 9.3 %collective-permute-start.8 = (f32[2,128,128]{2,1,0:T(8,128)S(1)}, f32[2,128,128]{2,1,0:T(8,128)S(1)}, u32[]{:S(2)}, u32[]{:S(2)}) collective-permute-start(f32[2,128,128]{2,1,0:T(8,128)S(1)} %add.15), channel_id=1, source_target_pairs={{0,8},{1,9},{2,10},{3,11},{4,12},{5,13},{6,14},{7,15},{8,0},{9,1},... | collective-permute-start | bytes 393224 | tf_op jit(solution)/shard_map/ppermute | solution.py:334
  21.7 11.7 %collective-permute-start.7 = (f32[4,128,128]{2,1,0:T(8,128)S(1)}, f32[4,128,128]{2,1,0:T(8,128)S(1)}, u32[]{:S(2)}, u32[]{:S(2)}) collective-permute-start(f32[4,128,128]{2,1,0:T(8,128)S(1)} %pad_maximum_fusion), channel_id=1, source_target_pairs={{0,2},{1,3},{2,0},{3,1},{4,6},{5,7},{6,4},{7,5},{8,10},{9,11},{10,... | collective-permute-start | bytes 786440 | tf_op jit(solution)/shard_map/ppermute | solution.py:334
  29.1 4.3 %collective-permute-start.9 = (f32[2,128,128]{2,1,0:T(8,128)S(1)}, f32[2,128,128]{2,1,0:T(8,128)S(1)}, u32[]{:S(2)}, u32[]{:S(2)}) collective-permute-start(f32[2,128,128]{2,1,0:T(8,128)S(1)} %collective-permute-done.8.refs_4_), channel_id=1, source_target_pairs={{0,1},{1,0},{2,3},{3,2},{4,5},{5,4},{6,7},{7,6},{8,10},{9,11},{10,... | collective-permute-start | bytes 393224 | tf_op jit(solution)/shard_map/ppermute | solution.py:334
  30.3 3.8 %collective-permute-start.3 = (f32[2,128,128]{2,1,0:T(8,128)S(1)}, f32[2,128,128]{2,1,0:T(8,128)S(1)}, u32[]{:S(2)}, u32[]{:S(2)}) collective-permute-start(f32[2,128,128]{2,1,0:T(8,128)S(1)} %collective-permute-done.2.refs_5_), channel_id=1, source_target_pairs={{0,1},{1,0},{2,3},{3,2},{4,5},{5,4},{6,7},{7,6},{8,10},{9,11},{10,... | collective-permute-start | bytes 393224 | tf_op jit(solution)/shard_map/ppermute | solution.py:334

commit v9 on v7

--- a/solution.py
+++ b/solution.py
@@ -322,13 +322,13 @@
     )(*operands)
 
 
-def swapped(array, bit, needs=None):
+def swapped(array, bit, needs=None, cross=False):
     size, cores = lax.axis_size("seq"), lax.axis_size("head")
     pairs = []
     for i in range(size):
         for core in range(cores):
             if needs is None or needs(i) or cores % 2:
-                to = (i ^ 1 << bit) * cores + core
+                to = (i ^ (3 << bit - 1 if cross and core % 2 == 0 else 1 << bit)) * cores + core
             else:
                 to = i * cores + (core ^ 1)
             pairs.append((i * cores + core, to))
@@ -358,13 +358,13 @@
     own_states = [list(received)]
     running = [parts[c] + received[c] for c in places]
     for bit in range(1, levels):
-        arrived = [swapped(running[c], bit) for c in places]
+        arrived = [swapped(running[c], bit, cross=bit > 1 and c == PARTS - 1) for c in places]
         own_states.append(arrived)
         running = [a + b for a, b in zip(running, arrived)]
     other_states = [[swapped(own, 0)]]
     for bit in range(1, levels - 1):
         both = jnp.concatenate(own_states[bit], axis=0)
-        other_states.append([swapped(both, 0)])
+        other_states.append([swapped(both, 0, lambda i, bit=bit: i >> bit & 1)])
     top = levels - 1
     needs = lambda i: i >> top & 1
     last = [swapped(own_states[top][c], 0, needs if c in (0, 1) else None) for c in places]

time: 35.8 us -> 35.8 us (level)
  waiting for transfers between devices: 5.52 us -> 7.47 us
  starting transfers between devices: 15.5 us -> 13.6 us
    ppermute x10, starting transfers between devices: 15.5 us -> 13.6 us  [swapped(): return lax.ppermute(array, ('seq', 'head'), pairs)]
    ppermute x10, waiting for transfers between devices: 5.52 us -> 7.47 us  [swapped(): return lax.ppermute(array, ('seq', 'head'), pairs)]
where the time goes in v9:
time: 35.8 us; the launch traced here: 35.2 us
  Pallas kernels  13.9 us (39%)
  starting transfers between devices  13.6 us (38%)
  waiting for transfers between devices  7.47 us (21%)
    ppermute x10, starting transfers between devices, swapped(): return lax.ppermute(array, ('seq', 'head'), pairs)  13.6 us
    ppermute x10, waiting for transfers between devices, swapped(): return lax.ppermute(array, ('seq', 'head'), pairs)  7.47 us
    pallas_call x4, Pallas kernels, base_part(): pl.pallas_call(functools.partial(base_kernel, place, levels, buckets, off...  7.04 us
    pallas_call x3, Pallas kernels, add_levels(): pl.pallas_call(functools.partial(levels_kernel, places, terms, len(states...  3.12 us
    pallas_call x1, Pallas kernels, own_block_states(): pl.pallas_call(own_kernel, out_shape=[jax.ShapeDtypeStruct(s, F32) for s...  2.27 us
    pallas_call x1, Pallas kernels, given_states(): pl.pallas_call(functools.partial(given_kernel, PARTS), out_shape=jax.Shap...  1.32 us
  transfers between devices with their start and end apart: 10, of which 3 were waited for; matrix products, arithmetic and copies ran while one was open for 0% of the time, Pallas kernels for 30%

profile of v9, /device:TPU:0, one launch (start us, length us, event | category | flops | bytes accessed | tf_op | source)
XLA Modules:
  0.0 35.2 jit_solution(8673852675895179124)
XLA Ops:
  0.0 2.3 %states_own.1 = (f32[256,1024]{1,0:T(8,128)S(1)}, f32[256,1024]{1,0:T(8,128)S(1)}, f32[256,1024]{1,0:T(8,128)S(1)}, f32[2,1024,128]{2,1,0:T(8,128)S(1)}, f32[4,1...) custom-call(f32[256,1024]{1,0:T(8,128)} %q_hbm.1, ...), custom_call_target="tpu_custom_call" | custom-call | flops 134217728 | bytes 6291456 | tf_op jit(solution)/shard_map/states_own/pallas_call | solution.py:141
  2.3 3.1 %collective-permute-start = (f32[2,128,128]{2,1,0:T(8,128)S(1)}, f32[2,128,128]{2,1,0:T(8,128)S(1)}, u32[]{:S(2)}, u32[]{:S(2)}) collective-permute-start(f32[2,128,128]{2,1,0:T(8,128)S(1)} %get-tuple-element.21), channel_id=1, source_target_pairs={{0,2},{1,3},{2,0},{3,1},{4,6},{5,7},{6,4},{7,5},{8,10},{9,11},{10,... | collective-permute-start | bytes 393224 | tf_op jit(solution)/shard_map/ppermute | solution.py:335
  5.3 1.3 %states_given.1 = f32[2,128,128]{2,1,0:T(8,128)S(1)} custom-call(f32[256,1024]{1,0:T(8,128)} %k_hbm.3, f32[256,1024]{1,0:T(8,128)} %v_hbm.3), custom_call_target="tpu_custom_call" | custom-call | flops 67108864 | bytes 524288 | tf_op jit(solution)/shard_map/states_given/pallas_call | solution.py:78
  6.7 0.1 collective-permute-start.5
  6.8 2.0 %collective-permute-start.4 = (f32[4,128,128]{2,1,0:T(8,128)S(1)}, f32[4,128,128]{2,1,0:T(8,128)S(1)}, u32[]{:S(2)}, u32[]{:S(2)}) collective-permute-start(f32[4,128,128]{2,1,0:T(8,128)S(1)} %get-tuple-element.22), channel_id=1, source_target_pairs={{0,2},{1,3},{2,0},{3,1},{4,6},{5,7},{6,4},{7,5},{8,10},{9,11},{10,... | collective-permute-start | bytes 786440 | tf_op jit(solution)/shard_map/ppermute | solution.py:335
  8.8 0.5 %collective-permute-done.refs_1_ = f32[2,128,128]{2,1,0:T(8,128)S(1)} collective-permute-done((f32[2,128,128]{2,1,0:T(8,128)S(1)}, f32[2,128,128]{2,1,0:T(8,128)S(1)}, u32[]{:S(2)}, u32[]{:S(2)}) %collective-permute-start) | collective-permute-done | bytes 131104 | tf_op jit(solution)/shard_map/ppermute | solution.py:335
  9.2 1.6 %collective-permute-start.1 = (f32[2,128,128]{2,1,0:T(8,128)S(1)}, f32[2,128,128]{2,1,0:T(8,128)S(1)}, u32[]{:S(2)}, u32[]{:S(2)}) collective-permute-start(f32[2,128,128]{2,1,0:T(8,128)S(1)} %add.12), channel_id=1, source_target_pairs={{0,4},{1,5},{2,6},{3,7},{4,0},{5,1},{6,2},{7,3},{8,12},{9,13},{10,... | collective-permute-start | bytes 393224 | tf_op jit(solution)/shard_map/ppermute | solution.py:335
  10.9 2.2 %collective-permute-done.5.refs_0_ = f32[2,128,128]{2,1,0:T(8,128)S(1)} collective-permute-done((f32[2,128,128]{2,1,0:T(8,128)S(1)}, f32[2,128,128]{2,1,0:T(8,128)S(1)}, u32[]{:S(2)}, u32[]{:S(2)}) %collective-permute-start.5) | collective-permute-done | bytes 131104 | tf_op jit(solution)/shard_map/ppermute | solution.py:335
  13.1 1.6 %collective-permute-start.6 = (f32[2,128,128]{2,1,0:T(8,128)S(1)}, f32[2,128,128]{2,1,0:T(8,128)S(1)}, u32[]{:S(2)}, u32[]{:S(2)}) collective-permute-start(f32[2,128,128]{2,1,0:T(8,128)S(1)} %add.14), channel_id=1, source_target_pairs={{0,4},{1,5},{2,6},{3,7},{4,0},{5,1},{6,2},{7,3},{8,12},{9,13},{10,... | collective-permute-start | bytes 393224 | tf_op jit(solution)/shard_map/ppermute | solution.py:335
  14.8 0.0 copy-done.1
  14.8 0.0 copy-done
  14.8 0.1 columns.1.weight_ref
  14.9 2.2 %shard_map.64 = (f32[256,256]{1,0:T(8,128)S(1)}, f32[2,1024,128]{2,1,0:T(8,128)S(1)}) custom-call(f32[256,1024]{1,0:T(8,128)S(1)} %get-tuple-element.19.q_ref, f32[256,1024]{1,0:T(8,128)S(1)} %get-tuple-element.24.k_ref, f32[256,1024]{1,0:T(8,128)S(1)} %get-tuple-element.25.v_ref, f32[256,128]{1,0:T(8,128)S(1)} %columns.1.weight_ref, ...), custom_call_target="tpu_custom_call" | custom-call | flops 805306368 | bytes 1310720 | tf_op jit(solution)/shard_map/pallas_call | solution.py:246
  17.1 0.0 collective-permute-done.1.refs_3_
  17.2 2.5 %collective-permute-start.2 = (f32[2,128,128]{2,1,0:T(8,128)S(1)}, f32[2,128,128]{2,1,0:T(8,128)S(1)}, u32[]{:S(2)}, u32[]{:S(2)}) collective-permute-start(f32[2,128,128]{2,1,0:T(8,128)S(1)} %add.13), channel_id=1, source_target_pairs={{0,12},{1,9},{2,14},{3,11},{4,8},{5,13},{6,10},{7,15},{8,4},{9,1},... | collective-permute-start | bytes 393224 | tf_op jit(solution)/shard_map/ppermute | solution.py:335
  19.7 0.0 collective-permute-done.6.refs_2_
  19.7 2.0 %collective-permute-start.8 = (f32[2,128,128]{2,1,0:T(8,128)S(1)}, f32[2,128,128]{2,1,0:T(8,128)S(1)}, u32[]{:S(2)}, u32[]{:S(2)}) collective-permute-start(f32[2,128,128]{2,1,0:T(8,128)S(1)} %add.15), channel_id=1, source_target_pairs={{0,8},{1,9},{2,10},{3,11},{4,12},{5,13},{6,14},{7,15},{8,0},{9,1},... | collective-permute-start | bytes 393224 | tf_op jit(solution)/shard_map/ppermute | solution.py:335
  21.7 0.1 collective-permute-start.7
  21.8 2.6 %shard_map.65 = (f32[256,256]{1,0:T(8,128)S(1)}, f32[4,1024,128]{2,1,0:T(8,128)S(1)}) custom-call(f32[256,1024]{1,0:T(8,128)S(1)} %get-tuple-element.19.q_ref, f32[256,1024]{1,0:T(8,128)S(1)} %get-tuple-element.24.k_ref, f32[256,1024]{1,0:T(8,128)S(1)} %get-tuple-element.25.v_ref, f32[256,128]{1,0:T(8,128)S(1)} %columns.1.weight_ref, ...), custom_call_target="tpu_custom_call" | custom-call | flops 805306368 | bytes 1310720 | tf_op jit(solution)/shard_map/pallas_call | solution.py:246
  24.4 4.8 %collective-permute-done.8.refs_4_ = f32[2,128,128]{2,1,0:T(8,128)S(1)} collective-permute-done((f32[2,128,128]{2,1,0:T(8,128)S(1)}, f32[2,128,128]{2,1,0:T(8,128)S(1)}, u32[]{:S(2)}, u32[]{:S(2)}) %collective-permute-start.8) | collective-permute-done | bytes 131104 | tf_op jit(solution)/shard_map/ppermute | solution.py:335
  29.1 0.0 collective-permute-start.9
  29.1 1.1 %shard_map.67.refs_4_ = f32[256,256]{1,0:T(8,128)S(1)} custom-call(f32[256,1024]{1,0:T(8,128)S(1)} %get-tuple-element.19.q_ref, f32[256,1024]{1,0:T(8,128)S(1)} %get-tuple-element.24.k_ref, f32[256,1024]{1,0:T(8,128)S(1)} %get-tuple-element.25.v_ref, f32[256,128]{1,0:T(8,128)S(1)} %columns.1.weight_ref, f32[4,1024,128]{2,1,0:T(8,128)S(1)} %get-tuple-element.28.prefix_ref), custom_call_target="tpu_custom_call" | custom-call | flops 805306368 | bytes 1310720 | tf_op jit(solution)/shard_map/pallas_call | solution.py:246
  30.3 0.0 collective-permute-done.2.refs_5_
  30.3 0.6 %collective-permute-start.3 = (f32[2,128,128]{2,1,0:T(8,128)S(1)}, f32[2,128,128]{2,1,0:T(8,128)S(1)}, u32[]{:S(2)}, u32[]{:S(2)}) collective-permute-start(f32[2,128,128]{2,1,0:T(8,128)S(1)} %collective-permute-done.2.refs_5_), channel_id=1, source_target_pairs={{0,1},{1,0},{2,3},{3,2},{4,5},{5,4},{6,7},{7,6},{8,10},{9,11},{10,... | collective-permute-start | bytes 393224 | tf_op jit(solution)/shard_map/ppermute | solution.py:335
  30.9 1.1 %shard_map.66.refs_3_ = f32[256,256]{1,0:T(8,128)S(1)} custom-call(f32[256,1024]{1,0:T(8,128)S(1)} %get-tuple-element.19.q_ref, f32[256,1024]{1,0:T(8,128)S(1)} %get-tuple-element.24.k_ref, f32[256,1024]{1,0:T(8,128)S(1)} %get-tuple-element.25.v_ref, f32[256,128]{1,0:T(8,128)S(1)} %columns.1.weight_ref, f32[4,1024,128]{2,1,0:T(8,128)S(1)} %get-tuple-element.28.prefix_ref), custom_call_target="tpu_custom_call" | custom-call | flops 805306368 | bytes 1310720 | tf_op jit(solution)/shard_map/pallas_call | solution.py:246
  32.0 1.5 %shard_map.69.refs_3_ = f32[256,1024]{1,0:T(8,128)} custom-call(f32[256,1024]{1,0:T(8,128)S(1)} %get-tuple-element.19.q_ref, f32[256,128]{1,0:T(8,128)S(1)} %columns.1.weight_ref, f32[2,128,128]{2,1,0:T(8,128)S(1)} %collective-permute-done.5.refs_0_, f32[2,128,128]{2,1,0:T(8,128)S(1)} %collective-permute-done.refs_1_, ...), custom_call_target="tpu_custom_call" | custom-call | flops 402653184 | bytes 1572864 | tf_op jit(solution)/shard_map/pallas_call | solution.py:307
  33.4 0.0 collective-permute-done.4.refs_0_
  33.5 0.0 collective-permute-done.7.refs_1_
  33.5 0.0 collective-permute-done.9.refs_2_
  33.5 0.6 %shard_map.68 = (f32[256,256]{1,0:T(8,128)S(1)}, f32[256,256]{1,0:T(8,128)S(1)}) custom-call(f32[256,1024]{1,0:T(8,128)S(1)} %get-tuple-element.19.q_ref, f32[256,128]{1,0:T(8,128)S(1)} %columns.1.weight_ref, f32[4,128,128]{2,1,0:T(8,128)S(1)} %collective-permute-done.4.refs_0_, f32[4,128,128]{2,1,0:T(8,128)S(1)} %collective-permute-done.7.refs_1_, ...), custom_call_target="tpu_custom_call" | custom-call | flops 335544320 | bytes 1572864 | tf_op jit(solution)/shard_map/pallas_call | solution.py:307
  34.1 0.0 collective-permute-done.3.refs_0_
  34.1 1.0 %shard_map.70 = f32[256,1024]{1,0:T(8,128)} custom-call(f32[256,1024]{1,0:T(8,128)S(1)} %get-tuple-element.19.q_ref, f32[256,128]{1,0:T(8,128)S(1)} %columns.1.weight_ref, f32[2,128,128]{2,1,0:T(8,128)S(1)} %collective-permute-done.3.refs_0_, f32[256,256]{1,0:T(8,128)S(1)} %get-tuple-element.29.refs_1_, ...), custom_call_target="tpu_custom_call", output_to_operand_aliasing={{}: (5, {})} | custom-call | flops 67108864 | bytes 1572864 | tf_op jit(solution)/shard_map/pallas_call | solution.py:307
  (8 shorter events, 0.1 us)
Async XLA Ops:
  0.0 14.8 %copy-start.1 = (f32[8,6,256]{2,0,1:T(8,128)S(1)}, f32[8,6,256]{2,0,1:T(8,128)}, u32[]{:S(2)}) copy-start(f32[8,6,256]{2,0,1:T(8,128)} %param.9) | copy-start | bytes 147460
  0.0 14.8 %copy-start = (f32[8,8,256]{2,1,0:T(8,128)S(1)}, f32[8,8,256]{2,1,0:T(8,128)}, u32[]{:S(2)}) copy-start(f32[8,8,256]{2,1,0:T(8,128)} %param.10) | copy-start | bytes 196612
  2.3 6.9 %collective-permute-start = (f32[2,128,128]{2,1,0:T(8,128)S(1)}, f32[2,128,128]{2,1,0:T(8,128)S(1)}, u32[]{:S(2)}, u32[]{:S(2)}) collective-permute-start(f32[2,128,128]{2,1,0:T(8,128)S(1)} %get-tuple-element.21), channel_id=1, source_target_pairs={{0,2},{1,3},{2,0},{3,1},{4,6},{5,7},{6,4},{7,5},{8,10},{9,11},{10,... | collective-permute-start | bytes 393224 | tf_op jit(solution)/shard_map/ppermute | solution.py:335
  6.7 6.4 %collective-permute-start.5 = (f32[2,128,128]{2,1,0:T(8,128)S(1)}, f32[2,128,128]{2,1,0:T(8,128)S(1)}, u32[]{:S(2)}, u32[]{:S(2)}) collective-permute-start(f32[2,128,128]{2,1,0:T(8,128)S(1)} %states_given.1), channel_id=1, source_target_pairs={{0,2},{1,3},{2,0},{3,1},{4,6},{5,7},{6,4},{7,5},{8,10},{9,11},{10,... | collective-permute-start | bytes 393224 | tf_op jit(solution)/shard_map/ppermute | solution.py:335
  6.8 26.7 %collective-permute-start.4 = (f32[4,128,128]{2,1,0:T(8,128)S(1)}, f32[4,128,128]{2,1,0:T(8,128)S(1)}, u32[]{:S(2)}, u32[]{:S(2)}) collective-permute-start(f32[4,128,128]{2,1,0:T(8,128)S(1)} %get-tuple-element.22), channel_id=1, source_target_pairs={{0,2},{1,3},{2,0},{3,1},{4,6},{5,7},{6,4},{7,5},{8,10},{9,11},{10,... | collective-permute-start | bytes 786440 | tf_op jit(solution)/shard_map/ppermute | solution.py:335
  9.2 7.9 %collective-permute-start.1 = (f32[2,128,128]{2,1,0:T(8,128)S(1)}, f32[2,128,128]{2,1,0:T(8,128)S(1)}, u32[]{:S(2)}, u32[]{:S(2)}) collective-permute-start(f32[2,128,128]{2,1,0:T(8,128)S(1)} %add.12), channel_id=1, source_target_pairs={{0,4},{1,5},{2,6},{3,7},{4,0},{5,1},{6,2},{7,3},{8,12},{9,13},{10,... | collective-permute-start | bytes 393224 | tf_op jit(solution)/shard_map/ppermute | solution.py:335
  13.1 6.6 %collective-permute-start.6 = (f32[2,128,128]{2,1,0:T(8,128)S(1)}, f32[2,128,128]{2,1,0:T(8,128)S(1)}, u32[]{:S(2)}, u32[]{:S(2)}) collective-permute-start(f32[2,128,128]{2,1,0:T(8,128)S(1)} %add.14), channel_id=1, source_target_pairs={{0,4},{1,5},{2,6},{3,7},{4,0},{5,1},{6,2},{7,3},{8,12},{9,13},{10,... | collective-permute-start | bytes 393224 | tf_op jit(solution)/shard_map/ppermute | solution.py:335
  17.2 13.1 %collective-permute-start.2 = (f32[2,128,128]{2,1,0:T(8,128)S(1)}, f32[2,128,128]{2,1,0:T(8,128)S(1)}, u32[]{:S(2)}, u32[]{:S(2)}) collective-permute-start(f32[2,128,128]{2,1,0:T(8,128)S(1)} %add.13), channel_id=1, source_target_pairs={{0,12},{1,9},{2,14},{3,11},{4,8},{5,13},{6,10},{7,15},{8,4},{9,1},... | collective-permute-start | bytes 393224 | tf_op jit(solution)/shard_map/ppermute | solution.py:335
  19.7 9.4 %collective-permute-start.8 = (f32[2,128,128]{2,1,0:T(8,128)S(1)}, f32[2,128,128]{2,1,0:T(8,128)S(1)}, u32[]{:S(2)}, u32[]{:S(2)}) collective-permute-start(f32[2,128,128]{2,1,0:T(8,128)S(1)} %add.15), channel_id=1, source_target_pairs={{0,8},{1,9},{2,10},{3,11},{4,12},{5,13},{6,14},{7,15},{8,0},{9,1},... | collective-permute-start | bytes 393224 | tf_op jit(solution)/shard_map/ppermute | solution.py:335
  21.7 11.8 %collective-permute-start.7 = (f32[4,128,128]{2,1,0:T(8,128)S(1)}, f32[4,128,128]{2,1,0:T(8,128)S(1)}, u32[]{:S(2)}, u32[]{:S(2)}) collective-permute-start(f32[4,128,128]{2,1,0:T(8,128)S(1)} %pad_maximum_fusion), channel_id=1, source_target_pairs={{0,1},{1,0},{2,3},{3,2},{4,6},{5,7},{6,4},{7,5},{8,9},{9,8},{10,11... | collective-permute-start | bytes 786440 | tf_op jit(solution)/shard_map/ppermute | solution.py:335
  29.1 4.3 %collective-permute-start.9 = (f32[2,128,128]{2,1,0:T(8,128)S(1)}, f32[2,128,128]{2,1,0:T(8,128)S(1)}, u32[]{:S(2)}, u32[]{:S(2)}) collective-permute-start(f32[2,128,128]{2,1,0:T(8,128)S(1)} %collective-permute-done.8.refs_4_), channel_id=1, source_target_pairs={{0,1},{1,0},{2,3},{3,2},{4,5},{5,4},{6,7},{7,6},{8,10},{9,11},{10,... | collective-permute-start | bytes 393224 | tf_op jit(solution)/shard_map/ppermute | solution.py:335
  30.3 3.8 %collective-permute-start.3 = (f32[2,128,128]{2,1,0:T(8,128)S(1)}, f32[2,128,128]{2,1,0:T(8,128)S(1)}, u32[]{:S(2)}, u32[]{:S(2)}) collective-permute-start(f32[2,128,128]{2,1,0:T(8,128)S(1)} %collective-permute-done.2.refs_5_), channel_id=1, source_target_pairs={{0,1},{1,0},{2,3},{3,2},{4,5},{5,4},{6,7},{7,6},{8,10},{9,11},{10,... | collective-permute-start | bytes 393224 | tf_op jit(solution)/shard_map/ppermute | solution.py:335
